TPU v7x, 32 devices: a whole 2x2x4 slice. The times are simulated.
32 devices in a mesh: dp: 4 (over y, core), expert: 8 (over z, x).
Axes of the slice: x: 2, y: 2, z: 4, core: 2. Of those that a mesh axis runs over, the one named last changes fastest.
Arguments:
- tokens: bfloat16 [2048, 7168], P('expert', 'dp'), may hold values from -6 to 6
- cotangent: bfloat16 [2048, 7168], P('expert', 'dp'), may hold values from -1.796875 to 1.796875
- expert_ids: int32 [2048, 8], P('expert'), may hold values from 0 to 255, as said below
- route_probs: bfloat16 [2048, 8], P('expert'), may hold values from 0.099609375 to 1
- w_up: bfloat16 [8, 7168, 1024], P('expert', 'dp'), may hold values from -0.0625 to 0.0625
- w_down: bfloat16 [8, 1024, 7168], P('expert', None, 'dp'), may hold values from -0.1875 to 0.1875
Outputs:
- grad_tokens: bfloat16 [2048, 7168], P('expert', 'dp')
- grad_probs: bfloat16 [2048, 8], P('expert')
- grad_up: bfloat16 [8, 7168, 1024], P('expert', 'dp')
- grad_down: bfloat16 [8, 1024, 7168], P('expert', None, 'dp')
Inputs may be any that keep to these rules, and one draw needn't show every extreme that they name: `expert_ids`: A token names each id at most once. Within one block of 256 tokens each id below 8 is named by at most 8 tokens; one such id is named by exactly 8 tokens in every block, and in most blocks another one too; loads of the ids below 8 are strongly uneven.
All inputs are finite; a program needn't handle non-finite values.
Results may differ from a plain program's by a relative error of at most 0.008.
Values may be sent and summed in bfloat16 or wider, within the bound.
No kernel may reach another device: no remote copies, remote signals or barrier semaphores. Data moves between devices by JAX's collectives and lax.ppermute only.
A program may use at most 64 MiB of HBM per device.

v0:
```python
import jax
import jax.numpy as jnp
from jax import lax
from jax.sharding import PartitionSpec as P

CAP = 8


def activate(hidden, query, gate_rows):
    sigma_h = jax.nn.sigmoid(hidden)
    act_rows = (hidden * sigma_h).astype(jnp.bfloat16)
    score_rows = jnp.sum(act_rows.astype(jnp.float32) * query, axis=1).astype(jnp.bfloat16)
    hidden_grad = (gate_rows[:, None] * query * sigma_h * (1.0 + hidden * (1.0 - sigma_h))).astype(
        jnp.bfloat16
    )
    return (act_rows, hidden_grad, score_rows)


def contract(left, right, left_dim, right_dim):
    return lax.dot_general(
        left, right, (((left_dim,), (right_dim,)), ((), ())), preferred_element_type=jnp.float32
    )


def on_device(tokens, cotangent, expert_ids, route_probs, w_up, w_down):
    experts = lax.axis_size("expert")
    block_rows = tokens.shape[0]
    feat_width = tokens.shape[1]
    top_count = expert_ids.shape[1]
    slot_count = experts * CAP
    numbers = jnp.arange(experts, dtype=jnp.int32)
    chosen = (expert_ids[:, :, None] == numbers[None, None, :]).astype(jnp.int32)
    per_token = jnp.sum(chosen, axis=1)
    before = jnp.cumsum(per_token, axis=0) - per_token
    order_rank = jnp.sum(chosen * before[:, None, :], axis=2)
    target = jnp.where(expert_ids < experts, expert_ids * CAP + order_rank, slot_count)
    placed = (target[:, :, None] == jnp.arange(slot_count, dtype=jnp.int32)[None, None, :]).astype(
        jnp.bfloat16
    )
    holder = jnp.sum(placed, axis=1)
    flat_placed = placed.reshape(block_rows * top_count, slot_count)
    stacked = jnp.concatenate([tokens, cotangent], axis=1)
    outgoing = contract(holder, stacked, 0, 0).astype(jnp.bfloat16)
    weights_out = contract(flat_placed, route_probs.reshape(-1), 0, 0).astype(jnp.bfloat16)
    send_x = outgoing[:, :feat_width].reshape(experts, CAP, feat_width)
    send_dy = outgoing[:, feat_width:].reshape(experts, CAP, feat_width)
    send_gate = weights_out.reshape(experts, CAP)
    rows_x, rows_dy, rows_gate = (
        lax.all_to_all(send_x, "expert", split_axis=0, concat_axis=0, tiled=True),
        lax.all_to_all(send_dy, "expert", split_axis=0, concat_axis=0, tiled=True),
        lax.all_to_all(send_gate, "expert", split_axis=0, concat_axis=0, tiled=True),
    )
    rows_x = rows_x.reshape(slot_count, feat_width)
    rows_dy = rows_dy.reshape(slot_count, feat_width)
    gate_rows = rows_gate.reshape(slot_count).astype(jnp.float32)
    up_weight = w_up[0]
    down_weight = w_down[0]
    part_hidden = jnp.dot(rows_x, up_weight, preferred_element_type=jnp.float32)
    part_query = contract(rows_dy, down_weight, 1, 1)
    full_hidden, full_query = lax.psum((part_hidden, part_query), "dp")
    act_rows, hidden_grad, score_rows = activate(full_hidden, full_query, gate_rows)
    scaled = (gate_rows[:, None] * rows_dy.astype(jnp.float32)).astype(jnp.bfloat16)
    row_grad = contract(hidden_grad, up_weight, 1, 1).astype(jnp.bfloat16)
    grad_up = contract(rows_x, hidden_grad, 0, 0).astype(jnp.bfloat16)[None]
    grad_down = contract(act_rows, scaled, 0, 0).astype(jnp.bfloat16)[None]
    back_rows, back_score = (
        lax.all_to_all(
            row_grad.reshape(experts, CAP, feat_width),
            "expert",
            split_axis=0,
            concat_axis=0,
            tiled=True,
        ),
        lax.all_to_all(
            score_rows.reshape(experts, CAP), "expert", split_axis=0, concat_axis=0, tiled=True
        ),
    )
    grad_tokens = contract(holder, back_rows.reshape(slot_count, feat_width), 1, 0).astype(
        jnp.bfloat16
    )
    grad_probs = (
        jnp.dot(flat_placed, back_score.reshape(slot_count), preferred_element_type=jnp.float32)
        .reshape(block_rows, top_count)
        .astype(jnp.bfloat16)
    )
    return (grad_tokens, grad_probs, grad_up, grad_down)


def solution(mesh):
    in_specs = (
        P("expert", "dp"),
        P("expert", "dp"),
        P("expert", None),
        P("expert", None),
        P("expert", "dp", None),
        P("expert", None, "dp"),
    )
    out_specs = (
        P("expert", "dp"),
        P("expert", None),
        P("expert", "dp", None),
        P("expert", None, "dp"),
    )
    return jax.shard_map(
        on_device, mesh=mesh, in_specs=in_specs, out_specs=out_specs, check_vma=False
    )
```

profile of v0, /device:TPU:0, one launch (start us, length us, event | category | flops | bytes accessed | tf_op | source)
XLA Modules:
  0.0 113.1 jit_solution(1898974032367609925)
XLA Ops:
  7.2 0.0 copy-start
  7.2 0.7 convert_reduce_fusion
  7.9 0.6 reduce-window.6
  8.5 0.2 slice_reduce_fusion
  8.7 0.1 bitcast_subtract_fusion
  8.8 0.7 select_reduce_fusion
  9.6 0.7 add_select_fusion
  10.3 0.1 fusion.23
  10.3 1.9 %convolution_convert_fusion = bf16[64,3584]{1,0:T(8,128)(2,1)S(1)} fusion(bf16[256,64]{0,1:T(8,128)(2,1)S(1)} %fusion.23, bf16[256,1792]{1,0:T(8,128)(2,1)} %param.7, bf16[256,1792]{1,0:T(8,128)(2,1)} %param.6), kind=kOutput, calls=%fused_computation | convolution fusion | flops 121339904 | bytes 2326528 | tf_op jit(solution)/shard_map/dot_general | solution.py:20
  12.2 0.7 slice_bitcast_fusion.1
  12.9 15.5 %all_to_all.31 = bf16[8,8,1792]{2,1,0:T(8,128)(2,1)S(1)} all-to-all(bf16[8,8,1792]{2,1,0:T(8,128)(2,1)S(1)} %get-tuple-element.9), channel_id=1, replica_groups=mesh['dp'=4,'expert'=8] {'expert'}, dimensions={0} | all-to-all | bytes 458752 | tf_op jit(solution)/shard_map/all_to_all | solution.py:49
  28.4 3.4 %all-to-all-start.1 = ((bf16[8,8,1792]{2,1,0:T(8,128)(2,1)}), bf16[8,8,1792]{2,1,0:T(8,128)(2,1)S(1)}, u32[]{:S(2)}, u32[]{:S(2)}) async-start(bf16[8,8,1792]{2,1,0:T(8,128)(2,1)} %get-tuple-element.8), calls=%async_computation.1 | async-start | bytes 458752 | tf_op jit(solution)/shard_map/all_to_all | solution.py:50
  31.9 0.0 all-reduce.3.cloned.1.call-start
  31.9 3.5 %fusion.2 = f32[64,1024]{1,0:T(8,128)} fusion(bf16[1,1792,1024]{2,1,0:T(8,128)(2,1)} %param.10, bf16[8,8,1792]{2,1,0:T(8,128)(2,1)S(1)} %all_to_all.31), kind=kOutput, calls=%fused_computation.5 | convolution fusion | flops 234881024 | bytes 4161536 | tf_op jit(solution)/shard_map/dot_general | solution.py:58
  35.4 4.5 %all-to-all-done.1 = bf16[8,8,1792]{2,1,0:T(8,128)(2,1)S(1)} async-done(((bf16[8,8,1792]{2,1,0:T(8,128)(2,1)}), bf16[8,8,1792]{2,1,0:T(8,128)(2,1)S(1)}, u32[]{:S(2)}, u32[]{:S(2)}) %all-to-all-start.1) | async-done | bytes 229408 | tf_op jit(solution)/shard_map/all_to_all | solution.py:50
  39.9 4.0 %fusion.4 = f32[64,1024]{1,0:T(8,128)} fusion(bf16[1,1024,1792]{2,1,0:T(8,128)(2,1)} %param.11, bf16[8,8,1792]{2,1,0:T(8,128)(2,1)S(1)} %all-to-all-done.1), kind=kOutput, calls=%fused_computation.7 | convolution fusion | flops 234881024 | bytes 4161536 | tf_op jit(solution)/shard_map/dot_general | solution.py:20
  43.9 0.0 all-reduce.3.cloned.1.call-update
  43.9 0.0 copy-done
  43.9 0.2 fusion.17
  44.1 0.1 all_to_all.25
  44.2 9.7 %all_to_all.32 = bf16[8,1,8]{2,1,0:T(2,128)(2,1)S(1)} all-to-all(bf16[8,1,8]{2,1,0:T(2,128)(2,1)S(1)} %all_to_all.25), channel_id=1, replica_groups=mesh['dp'=4,'expert'=8] {'expert'}, dimensions={0} | all-to-all | bytes 256 | tf_op jit(solution)/shard_map/all_to_all | solution.py:51
  53.9 0.1 reshape.105
  54.0 22.4 %all-reduce.3.cloned.1.call-done = (f32[64,1024]{1,0:T(8,128)}, f32[64,1024]{1,0:T(8,128)}) async-done(((f32[64,1024]{1,0:T(8,128)}, f32[64,1024]{1,0:T(8,128)}), (f32[64,1024]{1,0:T(8,128)}, f32[64,1024]{1,0:T(8,128)})) %all-reduce.3.cloned.1.call-update) | async-done | bytes 524304 | tf_op jit(solution)/shard_map/psum | solution.py:60
  76.4 0.0 copy-start.1
  76.4 1.3 %multiply_reduce_fusion = (bf16[64]{0:T(256)(128)(2,1)S(1)}, bf16[64,1024]{1,0:T(8,128)(2,1)S(1)}) fusion(f32[64,1024]{1,0:T(8,128)} %get-tuple-element.5, f32[64,1024]{1,0:T(8,128)} %get-tuple-element.4, f32[64]{0:T(128)S(1)} %reshape.105), kind=kLoop, calls=%fused_computation.27 | loop fusion | flops 982976 | bytes 655744 | tf_op jit(solution)/shard_map/reduce_sum | solution.py:12
  77.7 0.7 convert_element_type.87
  78.4 5.5 %all-to-all-start.4 = ((bf16[8,1,8]{2,1,0:T(2,128)(2,1)}), bf16[8,1,8]{2,1,0:T(2,128)(2,1)S(1)}, u32[]{:S(2)}, u32[]{:S(2)}) async-start(bf16[8,1,8]{2,1,0:T(2,128)(2,1)} %convert_element_type.87), calls=%async_computation.4 | async-start | bytes 8192 | tf_op jit(solution)/shard_map/all_to_all | solution.py:74
  83.9 4.0 %fusion.11 = bf16[8,8,1792]{2,1,0:T(8,128)(2,1)} fusion(bf16[64,1024]{1,0:T(8,128)(2,1)S(1)} %get-tuple-element.7, bf16[1,1792,1024]{2,1,0:T(8,128)(2,1)} %param.10), kind=kOutput, calls=%fused_computation.13 | convolution fusion | flops 234995712 | bytes 4030464 | tf_op jit(solution)/shard_map/dot_general | solution.py:20
  87.9 0.0 copy-done.1
  87.9 3.0 %fusion.7 = bf16[1,1024,1792]{2,1,0:T(8,128)(2,1)} fusion(bf16[8,8,1792]{2,1,0:T(8,128)(2,1)S(1)} %all-to-all-done.1, f32[64]{0:T(128)S(1)} %reshape.105, f32[64,1024]{1,0:T(8,128)S(1)} %copy-done.1), kind=kOutput, calls=%fused_computation.10 | convolution fusion | flops 237387776 | bytes 4161792 | tf_op jit(solution)/shard_map/dot_general | solution.py:20
  90.9 0.0 all-to-all-done.4
  90.9 6.0 %all-to-all-start.3 = ((bf16[8,8,1792]{2,1,0:T(8,128)(2,1)}), bf16[8,8,1792]{2,1,0:T(8,128)(2,1)S(1)}, u32[]{:S(2)}, u32[]{:S(2)}) async-start(bf16[8,8,1792]{2,1,0:T(8,128)(2,1)} %fusion.11), calls=%async_computation.3 | async-start | bytes 458752 | tf_op jit(solution)/shard_map/all_to_all | solution.py:67
  96.9 3.0 %fusion.6 = bf16[1,1792,1024]{2,1,0:T(8,128)(2,1)} fusion(bf16[64,1024]{1,0:T(8,128)(2,1)S(1)} %get-tuple-element.7, bf16[8,8,1792]{2,1,0:T(8,128)(2,1)S(1)} %all_to_all.31), kind=kOutput, calls=%fused_computation.9 | convolution fusion | flops 236716032 | bytes 4030464 | tf_op jit(solution)/shard_map/dot_general | solution.py:20
  99.9 0.1 reshape.108
  100.0 0.3 fusion.21
  100.4 0.8 copy.29
  101.2 3.7 %all-to-all-done.3 = bf16[8,8,1792]{2,1,0:T(8,128)(2,1)S(1)} async-done(((bf16[8,8,1792]{2,1,0:T(8,128)(2,1)}), bf16[8,8,1792]{2,1,0:T(8,128)(2,1)S(1)}, u32[]{:S(2)}, u32[]{:S(2)}) %all-to-all-start.3) | async-done | bytes 229408 | tf_op jit(solution)/shard_map/all_to_all | solution.py:67
  104.9 1.3 %convolution_convert_fusion.3 = bf16[256,1792]{1,0:T(8,128)(2,1)} fusion(bf16[256,64]{0,1:T(8,128)(2,1)S(1)} %fusion.23, bf16[8,8,1792]{2,1,0:T(8,128)(2,1)S(1)} %all-to-all-done.3), kind=kOutput, calls=%fused_computation.11 | convolution fusion | flops 59179008 | bytes 1179648 | tf_op jit(solution)/shard_map/dot_general | solution.py:20
  (4 shorter events, 0.1 us)
Async XLA Ops:
  7.2 36.8 %copy-start = (bf16[256,8]{0,1:T(8,128)(2,1)S(1)}, bf16[256,8]{0,1:T(8,128)(2,1)}, u32[]{:S(2)}) copy-start(bf16[256,8]{0,1:T(8,128)(2,1)} %param.9) | copy-start | bytes 12292
  28.4 11.5 %all-to-all-start.1 = ((bf16[8,8,1792]{2,1,0:T(8,128)(2,1)}), bf16[8,8,1792]{2,1,0:T(8,128)(2,1)S(1)}, u32[]{:S(2)}, u32[]{:S(2)}) async-start(bf16[8,8,1792]{2,1,0:T(8,128)(2,1)} %get-tuple-element.8), calls=%async_computation.1 | async-start | bytes 458752 | tf_op jit(solution)/shard_map/all_to_all | solution.py:50
  31.9 44.5 %all-reduce.3.cloned.1.call-start = ((), (), s32[]{:S(2)}) async-start(), calls=%async_computation.5 | async-start | bytes 1048576 | tf_op jit(solution)/shard_map/psum | solution.py:60
  76.4 11.5 %copy-start.1 = (f32[64,1024]{1,0:T(8,128)S(1)}, f32[64,1024]{1,0:T(8,128)}, u32[]{:S(2)}) copy-start(f32[64,1024]{1,0:T(8,128)} %get-tuple-element.4) | copy-start | bytes 786436
  78.4 12.5 %all-to-all-start.4 = ((bf16[8,1,8]{2,1,0:T(2,128)(2,1)}), bf16[8,1,8]{2,1,0:T(2,128)(2,1)S(1)}, u32[]{:S(2)}, u32[]{:S(2)}) async-start(bf16[8,1,8]{2,1,0:T(2,128)(2,1)} %convert_element_type.87), calls=%async_computation.4 | async-start | bytes 8192 | tf_op jit(solution)/shard_map/all_to_all | solution.py:74
  90.9 14.0 %all-to-all-start.3 = ((bf16[8,8,1792]{2,1,0:T(8,128)(2,1)}), bf16[8,8,1792]{2,1,0:T(8,128)(2,1)S(1)}, u32[]{:S(2)}, u32[]{:S(2)}) async-start(bf16[8,8,1792]{2,1,0:T(8,128)(2,1)} %fusion.11), calls=%async_computation.3 | async-start | bytes 458752 | tf_op jit(solution)/shard_map/all_to_all | solution.py:67
Sparse Core Ops, SparseCore 0:
  44.1 32.3 all-reduce.2
where the time goes:
time: 114 us; the launch traced here: 113 us
  waiting for transfers between devices  30.7 us (27%)
  blocking collectives  25.2 us (22%)
  matrix products  21.2 us (19%)
  starting transfers between devices  14.9 us (13%)
  between operations  14.1 us (12%)
  other arithmetic  4.27 us (4%)
  local copies, waits for them, and re-layouts  2.74 us (2%)
    psum x1, waiting for transfers between devices, on_device(): full_hidden, full_query = lax.psum((part_hidden, part_query), 'dp')  22.4 us
    dot_general x7, matrix products, contract(): lax.dot_general(left, right, (((left_dim,), (right_dim,)), ((), ())), pre...  17.4 us
    all_to_all x1, blocking collectives, on_device(): lax.all_to_all(send_x, 'expert', split_axis=0, concat_axis=0, tiled=True)  15.5 us
    all_to_all x1, blocking collectives, on_device(): lax.all_to_all(send_gate, 'expert', split_axis=0, concat_axis=0, tiled=True)  9.66 us
    all_to_all x1, starting transfers between devices, on_device(): lax.all_to_all(row_grad.reshape(experts, CAP, feat_width), 'expert', spli...  5.99 us
    all_to_all x1, starting transfers between devices, on_device(): lax.all_to_all(score_rows.reshape(experts, CAP), 'expert', split_axis=0,...  5.51 us
    all_to_all x1, waiting for transfers between devices, on_device(): lax.all_to_all(send_dy, 'expert', split_axis=0, concat_axis=0, tiled=True)  4.52 us
    all_to_all x1, waiting for transfers between devices, on_device(): lax.all_to_all(row_grad.reshape(experts, CAP, feat_width), 'expert', spli...  3.73 us
  transfers between devices with their start and end apart: 4, of which 3 were waited for; matrix products, arithmetic and copies ran while one was open for 13% of the time, Pallas kernels for 0%

commit v1 on v0

v1 whole, which is shorter than its diff:
```python
import jax
import jax.numpy as jnp
from jax import lax
from jax.sharding import PartitionSpec as P

CAP = 8
LANES = 128


def contract(left, right, left_dim, right_dim):
    return lax.dot_general(
        left, right, (((left_dim,), (right_dim,)), ((), ())), preferred_element_type=jnp.float32
    )


def swap(value, bit):
    count = lax.axis_size("dp")
    return lax.ppermute(value, "dp", [(i, i ^ bit) for i in range(count)])


def on_device(tokens, cotangent, expert_ids, route_probs, w_up, w_down):
    experts = lax.axis_size("expert")
    dp_count = lax.axis_size("dp")
    block_rows, feat_width = tokens.shape
    hidden_units = w_up.shape[2]
    slot_count = experts * CAP
    paired = dp_count > 1 and dp_count & (dp_count - 1) == 0
    slots = jnp.arange(slot_count, dtype=jnp.int32)
    hit = expert_ids[:, :, None] == (slots // CAP)[None, None, :]
    member = jnp.any(hit, axis=1).astype(jnp.bfloat16)
    gate_of = jnp.sum(jnp.where(hit, route_probs[:, :, None], 0), axis=1).astype(jnp.float32)
    times = jnp.arange(block_rows, dtype=jnp.int32)
    earlier = (times[:, None] > times[None, :]).astype(jnp.bfloat16)
    rank = contract(earlier, member, 1, 0)
    holder = jnp.where(rank == (slots % CAP).astype(jnp.float32)[None, :], member, 0)
    gates = jnp.sum(holder.astype(jnp.float32) * gate_of, axis=0)
    stacked = jnp.concatenate([tokens, cotangent], axis=1)
    outgoing = contract(holder, stacked, 0, 0).astype(jnp.bfloat16)
    gate_cols = jnp.broadcast_to(gates.astype(jnp.bfloat16)[:, None], (slot_count, LANES))
    send = jnp.concatenate([outgoing, gate_cols], axis=1).reshape(experts, CAP, -1)
    rows = lax.all_to_all(send, "expert", split_axis=0, concat_axis=0, tiled=True)
    rows = rows.reshape(slot_count, -1)
    rows_x = rows[:, :feat_width]
    rows_dy = rows[:, feat_width : 2 * feat_width]
    gate_rows = rows[:, 2 * feat_width : 2 * feat_width + 1].astype(jnp.float32)
    up_weight = w_up[0]
    down_weight = w_down[0]
    part = jnp.concatenate(
        [jnp.dot(rows_x, up_weight, preferred_element_type=jnp.float32), contract(rows_dy, down_weight, 1, 1)],
        axis=1,
    )
    if paired:
        half = slot_count // 2
        core = lax.axis_index("dp") & 1
        gives = lax.dynamic_slice_in_dim(part, (1 - core) * half, half, 0).astype(jnp.bfloat16)
        total = lax.dynamic_slice_in_dim(part, core * half, half, 0) + swap(gives, 1).astype(jnp.float32)
        bit = 2
        while bit < dp_count:
            rounded = lax.reduce_precision(total, 8, 7)
            total = rounded + swap(rounded.astype(jnp.bfloat16), bit).astype(jnp.float32)
            bit *= 2
        gate_part = lax.dynamic_slice_in_dim(gate_rows, core * half, half, 0)
    else:
        total = lax.psum(part, "dp")
        gate_part = gate_rows
    hidden = total[:, :hidden_units]
    query = total[:, hidden_units:]
    sigma_h = jax.nn.sigmoid(hidden)
    act = (hidden * sigma_h).astype(jnp.bfloat16)
    score = jnp.sum(act.astype(jnp.float32) * query, axis=1, keepdims=True).astype(jnp.bfloat16)
    hidden_grad = (gate_part * query * sigma_h * (1.0 + hidden * (1.0 - sigma_h))).astype(jnp.bfloat16)
    packed = jnp.concatenate(
        [act, hidden_grad, jnp.broadcast_to(score, (score.shape[0], LANES))], axis=1
    )
    if paired:
        other = swap(packed, 1)
        low = jnp.where(core == 0, packed, other)
        high = jnp.where(core == 0, other, packed)
        packed = jnp.concatenate([low, high], axis=0)
    act = packed[:, :hidden_units]
    hidden_grad = packed[:, hidden_units : 2 * hidden_units]
    scaled = (gate_rows * rows_dy.astype(jnp.float32)).astype(jnp.bfloat16)
    row_grad = contract(hidden_grad, up_weight, 1, 1).astype(jnp.bfloat16)
    back = jnp.concatenate([row_grad, packed[:, 2 * hidden_units :]], axis=1).reshape(experts, CAP, -1)
    back = lax.all_to_all(back, "expert", split_axis=0, concat_axis=0, tiled=True)
    back = back.reshape(slot_count, -1)
    grad_up = contract(rows_x, hidden_grad, 0, 0).astype(jnp.bfloat16)[None]
    grad_down = contract(act, scaled, 0, 0).astype(jnp.bfloat16)[None]
    grad_tokens = contract(holder, back[:, :feat_width], 1, 0).astype(jnp.bfloat16)
    own = (slots[:, None] // CAP == jnp.arange(experts, dtype=jnp.int32)[None, :])
    by_expert = contract(holder, jnp.where(own, back[:, feat_width : feat_width + 1], 0), 1, 0)
    picks = expert_ids[:, :, None] == jnp.arange(experts, dtype=jnp.int32)[None, None, :]
    grad_probs = jnp.sum(jnp.where(picks, by_expert[:, None, :], 0), axis=2).astype(jnp.bfloat16)
    return (grad_tokens, grad_probs, grad_up, grad_down)


def solution(mesh):
    in_specs = (
        P("expert", "dp"),
        P("expert", "dp"),
        P("expert", None),
        P("expert", None),
        P("expert", "dp", None),
        P("expert", None, "dp"),
    )
    out_specs = (
        P("expert", "dp"),
        P("expert", None),
        P("expert", "dp", None),
        P("expert", None, "dp"),
    )
    return jax.shard_map(
        on_device, mesh=mesh, in_specs=in_specs, out_specs=out_specs, check_vma=False
    )
```

time: 114 us -> 58.6 us (0.51)
  blocking collectives: 25.2 us -> 0 us
  between operations: 14.1 us -> 0.75 us
  waiting for transfers between devices: 30.7 us -> 22.9 us
  matrix products: 21.2 us -> 17.3 us
  local copies, waits for them, and re-layouts: 2.74 us -> 0.37 us
  starting transfers between devices: 14.9 us -> 12.6 us
    all_to_all x2 -> x0, blocking collectives: 25.2 us -> none  [the longest x1 15.5 us: on_device(): lax.all_to_all(send_x, 'expert', split_axis=0, concat_axis=0, tiled=True)]
    psum x1 -> x0, waiting for transfers between devices: 22.4 us -> none  [on_device(): full_hidden, full_query = lax.psum((part_hidden, part_query), 'dp')]
    all_to_all x3 -> x2, waiting for transfers between devices: 8.26 us -> 16.3 us  [the longest x1 13.4 us: on_device(): lax.all_to_all(send, 'expert', split_axis=0, concat_axis=0, tiled=True)]
    ppermute x0 -> x3, waiting for transfers between devices: none -> 6.58 us  [swap(): return lax.ppermute(value, 'dp', [(i, i ^ bit) for i in range(count)])]
    all_to_all x3 -> x2, starting transfers between devices: 14.9 us -> 10.9 us  [the longest x1 7.28 us: on_device(): lax.all_to_all(send, 'expert', split_axis=0, concat_axis=0, tiled=True)]
    dot_general x2 -> x1, matrix products: 3.85 us -> 0.77 us  [on_device(): jnp.dot(rows_x, up_weight, preferred_element_type=jnp.float32)]
    ppermute x0 -> x3, starting transfers between devices: none -> 1.73 us  [swap(): return lax.ppermute(value, 'dp', [(i, i ^ bit) for i in range(count)])]
    reshape x0 -> x2, other arithmetic: none -> 1.53 us  [the longest x1 0.82 us: on_device(): jnp.concatenate([outgoing, gate_cols], axis=1).reshape(experts, CAP, -1)]
  transfers between devices with their start and end apart: 4 -> 5, of which waited for: 3 -> 5; matrix products, arithmetic and copies ran while one was open for 13% -> 11% of each run, Pallas kernels for 0% -> 0%
where the time goes in v1:
time: 58.6 us; the launch traced here: 58.2 us
  waiting for transfers between devices  22.9 us (39%)
  matrix products  17.3 us (30%)
  starting transfers between devices  12.6 us (22%)
  other arithmetic  4.27 us (7%)
  between operations  0.75 us (1%)
    dot_general x8, matrix products, contract(): lax.dot_general(left, right, (((left_dim,), (right_dim,)), ((), ())), pre...  16.5 us
    all_to_all x1, waiting for transfers between devices, on_device(): lax.all_to_all(send, 'expert', split_axis=0, concat_axis=0, tiled=True)  13.4 us
    all_to_all x1, starting transfers between devices, on_device(): lax.all_to_all(send, 'expert', split_axis=0, concat_axis=0, tiled=True)  7.28 us
    ppermute x3, waiting for transfers between devices, swap(): return lax.ppermute(value, 'dp', [(i, i ^ bit) for i in range(count)])  6.58 us
    all_to_all x1, starting transfers between devices, on_device(): lax.all_to_all(back, 'expert', split_axis=0, concat_axis=0, tiled=True)  3.64 us
    all_to_all x1, waiting for transfers between devices, on_device(): lax.all_to_all(back, 'expert', split_axis=0, concat_axis=0, tiled=True)  2.87 us
    ppermute x3, starting transfers between devices, swap(): return lax.ppermute(value, 'dp', [(i, i ^ bit) for i in range(count)])  1.73 us
  transfers between devices with their start and end apart: 5, of which 5 were waited for; matrix products, arithmetic and copies ran while one was open for 11% of the time, Pallas kernels for 0%

profile of v1, /device:TPU:0, one launch (start us, length us, event | category | flops | bytes accessed | tf_op | source)
XLA Modules:
  0.0 58.2 jit_solution(14496348026128370947)
XLA Ops:
  0.6 0.8 %compare_reduce_fusion = pred[256,64]{0,1:T(8,128)(4,1)S(1)} fusion(s32[256,8]{0,1:T(8,128)} %param.8, s32[64]{0:T(128)S(1)} %get-tuple-element.11), kind=kLoop, calls=%fused_computation.19 | loop fusion | flops 245760 | bytes 24832 | tf_op jit(solution)/shard_map/reduce_or | solution.py:30
  1.5 0.8 %fusion.20 = bf16[256,64]{0,1:T(8,128)(2,1)S(1)} fusion(s32[256,8]{0,1:T(8,128)} %param.8, s32[64]{0:T(128)S(1)} %get-tuple-element.11, bf16[256,8]{0,1:T(8,128)(2,1)} %param.9), kind=kLoop, calls=%fused_computation.35 | loop fusion | flops 376832 | bytes 45312 | tf_op jit(solution)/shard_map/reduce_sum | solution.py:31
  2.3 0.3 multiply_reduce_fusion.1
  2.6 1.9 %convolution_convert_fusion = bf16[64,3584]{1,0:T(8,128)(2,1)S(1)} fusion(bf16[256,64]{0,1:T(8,128)(2,1)S(1)} %get-tuple-element.10, bf16[256,1792]{1,0:T(8,128)(2,1)} %param.7, bf16[256,1792]{1,0:T(8,128)(2,1)} %param.6), kind=kOutput, calls=%fused_computation | convolution fusion | flops 121339904 | bytes 2326528 | tf_op jit(solution)/shard_map/dot_general | solution.py:11
  4.5 0.1 broadcast_in_dim.74
  4.6 0.8 %maximum_bitcast_fusion = bf16[8,8,3712]{2,1,0:T(8,128)(2,1)} fusion(bf16[64,128]{1,0:T(8,128)(2,1)S(1)} %broadcast_in_dim.74, bf16[64,3584]{1,0:T(8,128)(2,1)S(1)} %convolution_convert_fusion), kind=kLoop, calls=%fused_computation.24 | loop fusion | flops 950272 | bytes 950272 | tf_op jit(solution)/shard_map/reshape | solution.py:40
  5.4 7.3 %all-to-all-start = ((bf16[8,8,3712]{2,1,0:T(8,128)(2,1)}), bf16[8,8,3712]{2,1,0:T(8,128)(2,1)S(1)}, u32[]{:S(2)}, u32[]{:S(2)}) async-start(bf16[8,8,3712]{2,1,0:T(8,128)(2,1)} %maximum_bitcast_fusion), calls=%async_computation | async-start | bytes 950272 | tf_op jit(solution)/shard_map/all_to_all | solution.py:41
  12.7 13.4 %all-to-all-done = bf16[8,8,3712]{2,1,0:T(8,128)(2,1)S(1)} async-done(((bf16[8,8,3712]{2,1,0:T(8,128)(2,1)}), bf16[8,8,3712]{2,1,0:T(8,128)(2,1)S(1)}, u32[]{:S(2)}, u32[]{:S(2)}) %all-to-all-start) | async-done | bytes 475168 | tf_op jit(solution)/shard_map/all_to_all | solution.py:41
  26.1 0.0 copy-start
  26.1 3.4 %fusion = f32[64,1024]{1,0:T(8,128)S(1)} fusion(bf16[1,1024,1792]{2,1,0:T(8,128)(2,1)} %param.11, bf16[64,3712]{1,0:T(8,128)(2,1)S(1)} %bitcast.24), kind=kOutput, calls=%fused_computation.3 | convolution fusion | flops 234881024 | bytes 4161536 | tf_op jit(solution)/shard_map/dot_general | solution.py:11
  29.5 0.0 copy-done
  29.5 0.8 %fusion.4 = f32[64,1024]{1,0:T(8,128)S(1)} fusion(bf16[1,1792,1024]{2,1,0:T(8,128)(2,1)S(1)} %copy-done, bf16[64,3712]{1,0:T(8,128)(2,1)S(1)} %bitcast.25), kind=kOutput, calls=%fused_computation.7 | convolution fusion | flops 234881024 | bytes 4161536 | tf_op jit(solution)/shard_map/dot_general | solution.py:49
  30.3 0.1 collective-permute-start
  30.4 1.3 %collective-permute-done = bf16[32,2048]{1,0:T(8,128)(2,1)S(1)} collective-permute-done((bf16[32,2048]{1,0:T(8,128)(2,1)S(1)}, bf16[32,2048]{1,0:T(8,128)(2,1)S(1)}, u32[]{:S(2)}, u32[]{:S(2)}) %collective-permute-start) | collective-permute-done | bytes 131104 | tf_op jit(solution)/shard_map/ppermute | solution.py:18
  31.8 1.6 %collective-permute-start.1 = (bf16[32,2048]{1,0:T(8,128)(2,1)S(1)}, bf16[32,2048]{1,0:T(8,128)(2,1)S(1)}, u32[]{:S(2)}, u32[]{:S(2)}) collective-permute-start(bf16[32,2048]{1,0:T(8,128)(2,1)S(1)} %fusion.43), channel_id=1, source_target_pairs={{0,16},{8,24},{16,0},{24,8},{1,17},{9,25},{17,1},{25,9},{2,18},{10... | collective-permute-start | bytes 393224 | tf_op jit(solution)/shard_map/ppermute | solution.py:18
  33.4 0.1 dynamic-slice_reduce_fusion
  33.5 3.9 %collective-permute-done.1 = bf16[32,2048]{1,0:T(8,128)(2,1)S(1)} collective-permute-done((bf16[32,2048]{1,0:T(8,128)(2,1)S(1)}, bf16[32,2048]{1,0:T(8,128)(2,1)S(1)}, u32[]{:S(2)}, u32[]{:S(2)}) %collective-permute-start.1) | collective-permute-done | bytes 131104 | tf_op jit(solution)/shard_map/ppermute | solution.py:18
  37.4 0.1 convert_add_fusion
  37.5 0.2 multiply_reduce_fusion
  37.6 0.1 broadcast_in_dim.75
  37.7 0.1 collective-permute-start.2
  37.8 1.3 %collective-permute-done.2 = bf16[32,2176]{1,0:T(8,128)(2,1)S(1)} collective-permute-done((bf16[32,2176]{1,0:T(8,128)(2,1)S(1)}, bf16[32,2176]{1,0:T(8,128)(2,1)S(1)}, u32[]{:S(2)}, u32[]{:S(2)}) %collective-permute-start.2) | collective-permute-done | bytes 139296 | tf_op jit(solution)/shard_map/ppermute | solution.py:18
  39.2 3.3 %fusion.8 = bf16[64,1792]{1,0:T(8,128)(2,1)S(1)} fusion(bf16[1,1792,1024]{2,1,0:T(8,128)(2,1)} %param.10, bf16[32,2176]{1,0:T(8,128)(2,1)S(1)} %get-tuple-element.7, bf16[32,2176]{1,0:T(8,128)(2,1)S(1)} %get-tuple-element.6), kind=kOutput, calls=%fused_computation.12 | convolution fusion | flops 235257856 | bytes 4177920 | tf_op jit(solution)/shard_map/dot_general | solution.py:11
  42.5 0.7 %maximum_bitcast_fusion.1 = bf16[8,8,1920]{2,1,0:T(8,128)(2,1)} fusion(bf16[64,128]{1,0:T(8,128)(2,1)S(1)} %fusion.30, bf16[64,1792]{1,0:T(8,128)(2,1)S(1)} %fusion.8), kind=kLoop, calls=%fused_computation.38 | loop fusion | flops 491520 | bytes 491520 | tf_op jit(solution)/shard_map/reshape | solution.py:84
  43.2 3.6 %all-to-all-start.1 = ((bf16[8,8,1920]{2,1,0:T(8,128)(2,1)}), bf16[8,8,1920]{2,1,0:T(8,128)(2,1)S(1)}, u32[]{:S(2)}, u32[]{:S(2)}) async-start(bf16[8,8,1920]{2,1,0:T(8,128)(2,1)} %maximum_bitcast_fusion.1), calls=%async_computation.1 | async-start | bytes 491520 | tf_op jit(solution)/shard_map/all_to_all | solution.py:85
  46.8 0.1 fusion.36
  46.9 3.0 %fusion.6 = bf16[1,1792,1024]{2,1,0:T(8,128)(2,1)} fusion(bf16[64,3712]{1,0:T(8,128)(2,1)S(1)} %bitcast.28, bf16[32,2176]{1,0:T(8,128)(2,1)S(1)} %get-tuple-element.7, bf16[32,2176]{1,0:T(8,128)(2,1)S(1)} %get-tuple-element.6), kind=kOutput, calls=%fused_computation.9 | convolution fusion | flops 236978176 | bytes 4177920 | tf_op jit(solution)/shard_map/dot_general | solution.py:11
  49.9 0.0 copy-start.1
  49.9 3.0 %fusion.7 = bf16[1,1024,1792]{2,1,0:T(8,128)(2,1)} fusion(f32[64]{0:T(128)S(1)} %fusion.36, bf16[64,3712]{1,0:T(8,128)(2,1)S(1)} %bitcast.29, bf16[32,2176]{1,0:T(8,128)(2,1)S(1)} %get-tuple-element.6, bf16[32,2176]{1,0:T(8,128)(2,1)S(1)} %get-tuple-element.7), kind=kOutput, calls=%fused_computation.10 | convolution fusion | flops 237322240 | bytes 4178432 | tf_op jit(solution)/shard_map/dot_general | solution.py:11
  53.0 2.9 %all-to-all-done.1 = bf16[8,8,1920]{2,1,0:T(8,128)(2,1)S(1)} async-done(((bf16[8,8,1920]{2,1,0:T(8,128)(2,1)}), bf16[8,8,1920]{2,1,0:T(8,128)(2,1)S(1)}, u32[]{:S(2)}, u32[]{:S(2)}) %all-to-all-start.1) | async-done | bytes 245792 | tf_op jit(solution)/shard_map/all_to_all | solution.py:85
  55.8 1.3 %convolution_convert_fusion.3 = bf16[256,1792]{1,0:T(8,128)(2,1)} fusion(bf16[256,64]{0,1:T(8,128)(2,1)S(1)} %get-tuple-element.10, bf16[64,1920]{1,0:T(8,128)(2,1)S(1)} %bitcast.30), kind=kOutput, calls=%fused_computation.11 | convolution fusion | flops 59179008 | bytes 1179648 | tf_op jit(solution)/shard_map/dot_general | solution.py:11
  57.2 0.1 slice_reduce_fusion
  57.3 0.3 fusion.31
  57.5 0.0 copy-done.1
  57.5 0.6 %select_reduce_fusion = bf16[256,8]{0,1:T(8,128)(2,1)} fusion(f32[256,8]{0,1:T(8,128)S(1)} %fusion.31, s32[256,8]{0,1:T(8,128)S(1)} %copy-done.1), kind=kLoop, calls=%fused_computation.55 | loop fusion | flops 47104 | bytes 20480 | tf_op jit(solution)/shard_map/reduce_sum | solution.py:93
  (7 shorter events, 0.1 us)
Async XLA Ops:
  5.4 20.7 %all-to-all-start = ((bf16[8,8,3712]{2,1,0:T(8,128)(2,1)}), bf16[8,8,3712]{2,1,0:T(8,128)(2,1)S(1)}, u32[]{:S(2)}, u32[]{:S(2)}) async-start(bf16[8,8,3712]{2,1,0:T(8,128)(2,1)} %maximum_bitcast_fusion), calls=%async_computation | async-start | bytes 950272 | tf_op jit(solution)/shard_map/all_to_all | solution.py:41
  26.1 3.4 %copy-start = (bf16[1,1792,1024]{2,1,0:T(8,128)(2,1)S(1)}, bf16[1,1792,1024]{2,1,0:T(8,128)(2,1)}, u32[]{:S(2)}) copy-start(bf16[1,1792,1024]{2,1,0:T(8,128)(2,1)} %param.10) | copy-start | bytes 11010052
  30.3 1.4 %collective-permute-start = (bf16[32,2048]{1,0:T(8,128)(2,1)S(1)}, bf16[32,2048]{1,0:T(8,128)(2,1)S(1)}, u32[]{:S(2)}, u32[]{:S(2)}) collective-permute-start(bf16[32,2048]{1,0:T(8,128)(2,1)S(1)} %fusion.16), channel_id=1, source_target_pairs={{0,8},{8,0},{16,24},{24,16},{1,9},{9,1},{17,25},{25,17},{2,10},{10... | collective-permute-start | bytes 393224 | tf_op jit(solution)/shard_map/ppermute | solution.py:18
  31.8 5.6 %collective-permute-start.1 = (bf16[32,2048]{1,0:T(8,128)(2,1)S(1)}, bf16[32,2048]{1,0:T(8,128)(2,1)S(1)}, u32[]{:S(2)}, u32[]{:S(2)}) collective-permute-start(bf16[32,2048]{1,0:T(8,128)(2,1)S(1)} %fusion.43), channel_id=1, source_target_pairs={{0,16},{8,24},{16,0},{24,8},{1,17},{9,25},{17,1},{25,9},{2,18},{10... | collective-permute-start | bytes 393224 | tf_op jit(solution)/shard_map/ppermute | solution.py:18
  37.7 1.4 %collective-permute-start.2 = (bf16[32,2176]{1,0:T(8,128)(2,1)S(1)}, bf16[32,2176]{1,0:T(8,128)(2,1)S(1)}, u32[]{:S(2)}, u32[]{:S(2)}) collective-permute-start(bf16[32,2176]{1,0:T(8,128)(2,1)S(1)} %pad_maximum_fusion), channel_id=1, source_target_pairs={{0,8},{8,0},{16,24},{24,16},{1,9},{9,1},{17,25},{25,17},{2,10},{10... | collective-permute-start | bytes 417800 | tf_op jit(solution)/shard_map/ppermute | solution.py:18
  43.2 12.6 %all-to-all-start.1 = ((bf16[8,8,1920]{2,1,0:T(8,128)(2,1)}), bf16[8,8,1920]{2,1,0:T(8,128)(2,1)S(1)}, u32[]{:S(2)}, u32[]{:S(2)}) async-start(bf16[8,8,1920]{2,1,0:T(8,128)(2,1)} %maximum_bitcast_fusion.1), calls=%async_computation.1 | async-start | bytes 491520 | tf_op jit(solution)/shard_map/all_to_all | solution.py:85
  49.9 7.6 %copy-start.1 = (s32[256,8]{0,1:T(8,128)S(1)}, s32[256,8]{0,1:T(8,128)}, u32[]{:S(2)}) copy-start(s32[256,8]{0,1:T(8,128)} %param.8) | copy-start | bytes 24580

commit v2 on v1

v2 whole, which is shorter than its diff:
```python
import jax
import jax.numpy as jnp
from jax import lax
from jax.experimental import pallas as pl
from jax.experimental.pallas import tpu as pltpu
from jax.sharding import PartitionSpec as P

CAP = 8
LANES = 128
VMEM = pl.BlockSpec(memory_space=pltpu.VMEM)
ANY = pl.BlockSpec(memory_space=pl.ANY)
HBM = pl.BlockSpec(memory_space=pltpu.HBM)


def contract(left, right, left_dim, right_dim):
    return lax.dot_general(
        left, right, (((left_dim,), (right_dim,)), ((), ())), preferred_element_type=jnp.float32
    )


def swap(value, bit):
    count = lax.axis_size("dp")
    return lax.ppermute(value, "dp", [(i, i ^ bit) for i in range(count)])


def padded(width):
    return -(-width // LANES) * LANES


def chunks(width, wanted):
    return [(at, min(at + wanted, width)) for at in range(0, width, wanted)]


def in_vmem(value):
    return pltpu.with_memory_space_constraint(value, pltpu.VMEM)


def in_hbm(value):
    return pltpu.with_memory_space_constraint(value, pltpu.HBM)


def params(mib):
    return pltpu.CompilerParams(vmem_limit_bytes=mib << 20)


def cost(flops, nbytes):
    return pl.CostEstimate(flops=flops, bytes_accessed=nbytes, transcendentals=0)


def route(ids, probs, tokens, cotangent, up_weight, down_weight, slot_count):
    names, block_rows = ids.shape
    width = tokens.shape[1]
    step = padded(width)
    parts = chunks(width, padded(-(-width // 2)))

    def kernel(
        ids_ref, probs_ref, tok_hbm, cot_hbm, up_hbm, down_hbm,
        send_ref, hold_ref, up_ref, down_ref,
        tok, cot, out, in_sems, out_sems, weight_sems,
    ):
        jobs = []
        for source, target, base in ((tok_hbm, tok, 0), (cot_hbm, cot, step)):
            for low, high in parts:
                n = len(jobs)
                copy = pltpu.make_async_copy(
                    source.at[:, low:high], target.at[:, low:high], in_sems.at[n]
                )
                copy.start()
                jobs.append((copy, target, base, low, high))
        loads = [
            pltpu.make_async_copy(up_hbm, up_ref, weight_sems.at[0]),
            pltpu.make_async_copy(down_hbm, down_ref, weight_sems.at[1]),
        ]
        for load in loads:
            load.start()
        slots = lax.broadcasted_iota(jnp.int32, (slot_count, block_rows), 0)
        shift = CAP.bit_length() - 1
        expert = lax.shift_right_logical(slots, shift)
        place = (slots & (CAP - 1)).astype(jnp.float32)
        member = jnp.zeros((slot_count, block_rows), jnp.float32)
        gate = jnp.zeros((slot_count, block_rows), jnp.float32)
        for k in range(names):
            named = ids_ref[k : k + 1, :] == expert
            member = jnp.where(named, 1.0, member)
            gate = jnp.where(named, probs_ref[k : k + 1, :].astype(jnp.float32), gate)
        before = lax.broadcasted_iota(jnp.int32, (block_rows, block_rows), 0)
        after = lax.broadcasted_iota(jnp.int32, (block_rows, block_rows), 1)
        earlier = jnp.where(before < after, 1.0, 0.0).astype(jnp.bfloat16)
        rank = contract(member.astype(jnp.bfloat16), earlier, 1, 0)
        held = jnp.where(rank == place, member, 0.0)
        gates = jnp.sum(held * gate, axis=1, keepdims=True)
        hold = held.astype(jnp.bfloat16)
        hold_ref[...] = hold
        out[:, 2 * step :] = jnp.broadcast_to(gates, (slot_count, LANES)).astype(jnp.bfloat16)
        outs = [pltpu.make_async_copy(
            out.at[:, 2 * step :], send_ref.at[:, 2 * step :], out_sems.at[len(jobs)]
        )]
        outs[0].start()
        for n, (copy, target, base, low, high) in enumerate(jobs):
            copy.wait()
            out[:, base + low : base + high] = contract(hold, target[:, low:high], 1, 0).astype(
                jnp.bfloat16
            )
            end = base + (step if high == width else high)
            push = pltpu.make_async_copy(
                out.at[:, base + low : end], send_ref.at[:, base + low : end], out_sems.at[n]
            )
            push.start()
            outs.append(push)
        for push in outs + loads:
            push.wait()

    count = 2 * len(parts)
    return pl.pallas_call(
        kernel,
        out_shape=(
            jax.ShapeDtypeStruct((slot_count, 2 * step + LANES), jnp.bfloat16),
            jax.ShapeDtypeStruct((slot_count, block_rows), jnp.bfloat16),
            pltpu.VMEM(up_weight.shape, jnp.bfloat16),
            pltpu.VMEM(down_weight.shape, jnp.bfloat16),
        ),
        in_specs=[VMEM, VMEM, HBM, HBM, HBM, HBM],
        out_specs=(ANY, VMEM, VMEM, VMEM),
        scratch_shapes=[
            pltpu.VMEM(tokens.shape, jnp.bfloat16),
            pltpu.VMEM(tokens.shape, jnp.bfloat16),
            pltpu.VMEM((slot_count, 2 * step + LANES), jnp.bfloat16),
            pltpu.SemaphoreType.DMA((count,)),
            pltpu.SemaphoreType.DMA((count + 1,)),
            pltpu.SemaphoreType.DMA((2,)),
        ],
        compiler_params=params(16),
        cost_estimate=cost(4 * slot_count * block_rows * width, 8 * block_rows * width),
        name="route",
    )(ids, probs, *map(in_hbm, (tokens, cotangent, up_weight, down_weight)))


def core_rows(half):
    core = lax.axis_index("dp") & 1
    return pl.multiple_of(core * half, half), pl.multiple_of((1 - core) * half, half)


def products(rows, up_weight, down_weight):
    slot_count = rows.shape[0]
    half = slot_count // 2
    width, units = up_weight.shape
    step = padded(width)

    def kernel(rows_ref, up_ref, down_ref, give_ref, keep_ref, whole):
        mine, other = core_rows(half)
        for low, high in chunks(units, 256):
            whole[:, low:high] = contract(rows_ref[:, :width], up_ref[:, low:high], 1, 0)
        for low, high in chunks(units, 256):
            whole[:, units + low : units + high] = contract(
                rows_ref[:, step : step + width], down_ref[low:high, :], 1, 1
            )
        give_ref[...] = whole[pl.ds(other, half), :].astype(jnp.bfloat16)
        keep_ref[...] = whole[pl.ds(mine, half), :]

    return pl.pallas_call(
        kernel,
        out_shape=(
            jax.ShapeDtypeStruct((half, 2 * units), jnp.bfloat16),
            jax.ShapeDtypeStruct((half, 2 * units), jnp.float32),
        ),
        in_specs=[VMEM, VMEM, VMEM],
        out_specs=(VMEM, VMEM),
        scratch_shapes=[pltpu.VMEM((slot_count, 2 * units), jnp.float32)],
        compiler_params=params(24),
        cost_estimate=cost(4 * slot_count * width * units, 4 * width * units),
        name="products",
    )(rows, in_vmem(up_weight), in_vmem(down_weight))


def activate(rows, own, other, units, gate_at):
    half = own.shape[0]

    def kernel(rows_ref, own_ref, other_ref, out_ref):
        mine, _ = core_rows(half)
        gate = rows_ref[pl.ds(mine, half), gate_at : gate_at + LANES].astype(jnp.float32)[:, :1]
        total = own_ref[...].astype(jnp.float32) + other_ref[...].astype(jnp.float32)
        hidden = total[:, :units]
        query = total[:, units:]
        sigma_h = jax.nn.sigmoid(hidden)
        act = (hidden * sigma_h).astype(jnp.bfloat16)
        score = jnp.sum(act.astype(jnp.float32) * query, axis=1, keepdims=True)
        grad = gate * query * sigma_h * (1.0 + hidden * (1.0 - sigma_h))
        out_ref[:, :units] = act
        out_ref[:, units : 2 * units] = grad.astype(jnp.bfloat16)
        out_ref[:, 2 * units :] = jnp.broadcast_to(score, (half, LANES)).astype(jnp.bfloat16)

    return pl.pallas_call(
        kernel,
        out_shape=jax.ShapeDtypeStruct((half, 2 * units + LANES), jnp.bfloat16),
        in_specs=[VMEM, VMEM, VMEM],
        out_specs=VMEM,
        compiler_params=params(16),
        cost_estimate=cost(20 * half * units, 12 * half * units),
        name="activate",
    )(rows, own, other)


def returned(own, other, up_weight):
    half = own.shape[0]
    width, units = up_weight.shape
    step = padded(width)

    def kernel(own_ref, other_ref, up_ref, send_ref, act_ref, grad_ref, whole):
        mine, theirs = core_rows(half)
        whole[pl.ds(mine, half), :] = own_ref[...]
        whole[pl.ds(theirs, half), :] = other_ref[...]
        grad = whole[:, units : 2 * units]
        for low, high in chunks(width, 256):
            send_ref[:, low:high] = contract(grad, up_ref[low:high, :], 1, 1).astype(jnp.bfloat16)
        send_ref[:, step:] = whole[:, 2 * units :]
        act_ref[...] = whole[:, :units]
        grad_ref[...] = grad

    return pl.pallas_call(
        kernel,
        out_shape=(
            jax.ShapeDtypeStruct((2 * half, step + LANES), jnp.bfloat16),
            jax.ShapeDtypeStruct((2 * half, units), jnp.bfloat16),
            jax.ShapeDtypeStruct((2 * half, units), jnp.bfloat16),
        ),
        in_specs=[VMEM, VMEM, VMEM],
        out_specs=(VMEM,) * 3,
        scratch_shapes=[pltpu.VMEM((2 * half, own.shape[1]), jnp.bfloat16)],
        compiler_params=params(16),
        cost_estimate=cost(4 * half * width * units, 2 * width * units),
        name="returned",
    )(own, other, in_vmem(up_weight))


def collect(ids, hold, back, width):
    names, block_rows = ids.shape
    slot_count = hold.shape[0]
    experts = slot_count // CAP
    step = padded(width)
    parts = chunks(width, padded(-(-width // 2)))

    def kernel(ids_ref, hold_ref, back_ref, tok_ref, prob_ref, buf, sems):
        pushes = []
        for n, (low, high) in enumerate(parts):
            buf[:, low:high] = contract(hold_ref[...], back_ref[:, low:high], 0, 0).astype(jnp.bfloat16)
            push = pltpu.make_async_copy(buf.at[:, low:high], tok_ref.at[:, low:high], sems.at[n])
            push.start()
            pushes.append(push)
        scores = hold_ref[...].astype(jnp.float32) * back_ref[:, step : step + 1].astype(jnp.float32)
        total = jnp.zeros((names, block_rows), jnp.float32)
        for e in range(experts):
            score = jnp.sum(scores[e * CAP : (e + 1) * CAP, :], axis=0, keepdims=True)
            total = jnp.where(ids_ref[...] == e, score, total)
        prob_ref[...] = total.astype(jnp.bfloat16)
        for push in pushes:
            push.wait()

    return pl.pallas_call(
        kernel,
        out_shape=(
            jax.ShapeDtypeStruct((block_rows, width), jnp.bfloat16),
            jax.ShapeDtypeStruct((names, block_rows), jnp.bfloat16),
        ),
        in_specs=[VMEM, VMEM, VMEM],
        out_specs=(ANY, VMEM),
        scratch_shapes=[
            pltpu.VMEM((block_rows, width), jnp.bfloat16),
            pltpu.SemaphoreType.DMA((len(parts),)),
        ],
        compiler_params=params(16),
        cost_estimate=cost(2 * slot_count * block_rows * width, 4 * block_rows * width),
        name="collect",
    )(ids, hold, back)


def exchange(rows, experts):
    rows = rows.reshape(experts, CAP, -1)
    rows = lax.all_to_all(rows, "expert", split_axis=0, concat_axis=0, tiled=True)
    return rows.reshape(experts * CAP, -1)


def on_device(tokens, cotangent, expert_ids, route_probs, w_up, w_down):
    experts = lax.axis_size("expert")
    dp_count = lax.axis_size("dp")
    width = tokens.shape[1]
    step = padded(width)
    units = w_up.shape[2]
    slot_count = experts * CAP
    ids = expert_ids.T
    send, hold, up_weight, down_weight = route(
        ids, route_probs.T, tokens, cotangent, w_up[0], w_down[0], slot_count
    )
    rows = exchange(send, experts)
    gate_rows = rows[:, 2 * step : 2 * step + 1].astype(jnp.float32)
    if dp_count > 1 and dp_count & (dp_count - 1) == 0:
        gives, keeps = products(rows, up_weight, down_weight)
        own = (keeps + swap(gives, 1).astype(jnp.float32)).astype(jnp.bfloat16)
        other = jnp.zeros_like(own)
        bit = 2
        while bit < dp_count:
            if bit > 2:
                own = (own.astype(jnp.float32) + other.astype(jnp.float32)).astype(jnp.bfloat16)
            other = swap(own, bit)
            bit *= 2
        packed = activate(rows, own, other, units, 2 * step)
        back, act, hidden_grad = returned(packed, swap(packed, 1), up_weight)
    else:
        hidden = contract(rows[:, :width], up_weight, 1, 0)
        query = contract(rows[:, step : step + width], down_weight, 1, 1)
        hidden, query = lax.psum((hidden, query), "dp")
        sigma_h = jax.nn.sigmoid(hidden)
        act = (hidden * sigma_h).astype(jnp.bfloat16)
        score = jnp.sum(act.astype(jnp.float32) * query, axis=1, keepdims=True).astype(jnp.bfloat16)
        hidden_grad = gate_rows * query * sigma_h * (1.0 + hidden * (1.0 - sigma_h))
        hidden_grad = hidden_grad.astype(jnp.bfloat16)
        pad = jnp.zeros((slot_count, step - width), jnp.bfloat16)
        row_grad = contract(hidden_grad, up_weight, 1, 1).astype(jnp.bfloat16)
        back = jnp.concatenate([row_grad, pad, jnp.broadcast_to(score, (slot_count, LANES))], axis=1)
    back = exchange(back, experts)
    scaled = (gate_rows * rows[:, step : step + width].astype(jnp.float32)).astype(jnp.bfloat16)
    grad_up = contract(rows[:, :width], hidden_grad, 0, 0).astype(jnp.bfloat16)[None]
    grad_down = contract(act, scaled, 0, 0).astype(jnp.bfloat16)[None]
    grad_tokens, grad_probs = collect(ids, hold, back, width)
    return (grad_tokens, grad_probs.T, grad_up, grad_down)


def solution(mesh):
    in_specs = (
        P("expert", "dp"),
        P("expert", "dp"),
        P("expert", None),
        P("expert", None),
        P("expert", "dp", None),
        P("expert", None, "dp"),
    )
    out_specs = (
        P("expert", "dp"),
        P("expert", None),
        P("expert", "dp", None),
        P("expert", None, "dp"),
    )
    return jax.shard_map(
        on_device, mesh=mesh, in_specs=in_specs, out_specs=out_specs, check_vma=False
    )
```

time: 58.6 us -> 53.9 us (0.920)
  blocking collectives: 0 us -> 20.6 us
  waiting for transfers between devices: 22.9 us -> 9.61 us
  matrix products: 17.3 us -> 6.01 us
  Pallas kernels: 0 us -> 9.88 us
  starting transfers between devices: 12.6 us -> 5.32 us
  other arithmetic: 4.27 us -> 0.13 us
  local copies, waits for them, and re-layouts: 0.37 us -> 1.38 us
    all_to_all x0 -> x1, blocking collectives: none -> 20.6 us  [exchange(): lax.all_to_all(rows, 'expert', split_axis=0, concat_axis=0, tiled=True)]
    all_to_all x2 -> x1, waiting for transfers between devices: 16.3 us -> 2.9 us  [exchange(): lax.all_to_all(rows, 'expert', split_axis=0, concat_axis=0, tiled=True)]
    dot_general x8 -> x2, matrix products: 16.5 us -> 6.01 us  [contract(): lax.dot_general(left, right, (((left_dim,), (right_dim,)), ((), ())), pre...]
    pallas_call x0 -> x5, Pallas kernels: none -> 9.88 us  [the longest x1 4.05 us: route(): pl.pallas_call(kernel, out_shape=(jax.ShapeDtypeStruct((slot_count, 2 * s...]
    all_to_all x2 -> x1, starting transfers between devices: 10.9 us -> 3.59 us  [exchange(): lax.all_to_all(rows, 'expert', split_axis=0, concat_axis=0, tiled=True)]
    reduce_sum x3 -> x0, other arithmetic: 1.63 us -> none  [the longest x1 0.83 us: on_device(): jnp.sum(jnp.where(hit, route_probs[:, :, None], 0), axis=1)]
    reshape x2 -> x0, other arithmetic: 1.53 us -> none  [the longest x1 0.82 us: on_device(): jnp.concatenate([outgoing, gate_cols], axis=1).reshape(experts, CAP, -1)]
    unnamed x4 -> x6, local copies, waits for them, and re-layouts: 0.01 us -> 1.38 us
  transfers between devices with their start and end apart: 5 -> 4, of which waited for: 5 -> 4; matrix products, arithmetic and copies ran while one was open for 11% -> 11% of each run, Pallas kernels for 0% -> 0%
where the time goes in v2:
time: 53.9 us; the launch traced here: 53.6 us
  blocking collectives  20.6 us (38%)
  Pallas kernels  9.88 us (18%)
  waiting for transfers between devices  9.61 us (18%)
  matrix products  6.01 us (11%)
  starting transfers between devices  5.32 us (10%)
  local copies, waits for them, and re-layouts  1.38 us (3%)
  between operations  0.7 us (1%)
    all_to_all x1, blocking collectives, exchange(): lax.all_to_all(rows, 'expert', split_axis=0, concat_axis=0, tiled=True)  20.6 us
    ppermute x3, waiting for transfers between devices, swap(): return lax.ppermute(value, 'dp', [(i, i ^ bit) for i in range(count)])  6.71 us
    dot_general x2, matrix products, contract(): lax.dot_general(left, right, (((left_dim,), (right_dim,)), ((), ())), pre...  6.01 us
    pallas_call x1, Pallas kernels, route(): pl.pallas_call(kernel, out_shape=(jax.ShapeDtypeStruct((slot_count, 2 * s...  4.05 us
    all_to_all x1, starting transfers between devices, exchange(): lax.all_to_all(rows, 'expert', split_axis=0, concat_axis=0, tiled=True)  3.59 us
    all_to_all x1, waiting for transfers between devices, exchange(): lax.all_to_all(rows, 'expert', split_axis=0, concat_axis=0, tiled=True)  2.9 us
    pallas_call x1, Pallas kernels, returned(): pl.pallas_call(kernel, out_shape=(jax.ShapeDtypeStruct((2 * half, step +...  1.94 us
    pallas_call x1, Pallas kernels, products(): pl.pallas_call(kernel, out_shape=(jax.ShapeDtypeStruct((half, 2 * units),...  1.87 us
  transfers between devices with their start and end apart: 4, of which 4 were waited for; matrix products, arithmetic and copies ran while one was open for 11% of the time, Pallas kernels for 0%

profile of v2, /device:TPU:0, one launch (start us, length us, event | category | flops | bytes accessed | tf_op | source)
XLA Modules:
  0.0 53.6 jit_solution(15880573202243514318)
XLA Ops:
  0.6 0.0 copy-start
  0.6 0.7 %copy-done = s32[256,8]{0,1:T(8,128)S(1)} copy-done((s32[256,8]{0,1:T(8,128)S(1)}, s32[256,8]{0,1:T(8,128)}, u32[]{:S(2)}) %copy-start) | copy-done | bytes 8216
  1.3 0.0 copy-start.2
  1.3 0.7 %copy-done.2 = bf16[256,8]{0,1:T(8,128)(2,1)S(1)} copy-done((bf16[256,8]{0,1:T(8,128)(2,1)S(1)}, bf16[256,8]{0,1:T(8,128)(2,1)}, u32[]{:S(2)}) %copy-start.2) | copy-done | bytes 4120
  2.0 4.0 %route.1 = (bf16[64,3712]{1,0:T(8,128)(2,1)S(1)}, bf16[64,256]{1,0:T(8,128)(2,1)S(1)}, bf16[1792,1024]{1,0:T(8,128)(2,1)S(1)}, bf16[1024,1792]{1,0:T(8,128)(2,1)S(1)}) custom-call(s32[8,256]{1,0:T(8,128)S(1)} %bitcast.22, bf16[8,256]{1,0:T(8,128)(2,1)S(1)} %bitcast.24, bf16[256,1792]{1,0:T(8,128)(2,1)} %tok_hbm.1, bf16[256,1792]{1,0:T(8,128)(2,1)} %cot_hbm.1, ...), custom_call_target="tpu_custom_call" | custom-call | flops 117440512 | bytes 3670016 | tf_op jit(solution)/shard_map/route/pallas_call | solution.py:114
  6.1 20.6 %all_to_all.10 = bf16[8,8,3712]{2,1,0:T(8,128)(2,1)S(1)} all-to-all(bf16[8,8,3712]{2,1,0:T(8,128)(2,1)S(1)} %bitcast.21), channel_id=1, replica_groups=mesh['dp'=4,'expert'=8] {'expert'}, dimensions={0} | all-to-all | bytes 950272 | tf_op jit(solution)/shard_map/all_to_all | solution.py:278
  26.6 1.9 %products.1 = (bf16[32,2048]{1,0:T(8,128)(2,1)S(1)}, f32[32,2048]{1,0:T(8,128)S(1)}) custom-call(bf16[64,3712]{1,0:T(8,128)(2,1)S(1)} %bitcast.15, bf16[1792,1024]{1,0:T(8,128)(2,1)S(1)} %get-tuple-element.17.up_ref, bf16[1024,1792]{1,0:T(8,128)(2,1)S(1)} %get-tuple-element.18.down_ref), custom_call_target="tpu_custom_call" | custom-call | flops 469762048 | bytes 7340032 | tf_op jit(solution)/shard_map/products/pallas_call | solution.py:160
  28.5 0.1 collective-permute-start
  28.6 1.3 %collective-permute-done = bf16[32,2048]{1,0:T(8,128)(2,1)S(1)} collective-permute-done((bf16[32,2048]{1,0:T(8,128)(2,1)S(1)}, bf16[32,2048]{1,0:T(8,128)(2,1)S(1)}, u32[]{:S(2)}, u32[]{:S(2)}) %collective-permute-start) | collective-permute-done | bytes 131104 | tf_op jit(solution)/shard_map/ppermute | solution.py:23
  29.9 1.6 %collective-permute-start.1 = (bf16[32,2048]{1,0:T(8,128)(2,1)S(1)}, bf16[32,2048]{1,0:T(8,128)(2,1)S(1)}, u32[]{:S(2)}, u32[]{:S(2)}) collective-permute-start(bf16[32,2048]{1,0:T(8,128)(2,1)S(1)} %add_convert_fusion.own_ref), channel_id=1, source_target_pairs={{0,16},{8,24},{16,0},{24,8},{1,17},{9,25},{17,1},{25,9},{2,18},{10... | collective-permute-start | bytes 393224 | tf_op jit(solution)/shard_map/ppermute | solution.py:23
  31.5 4.0 %collective-permute-done.1.other_ref = bf16[32,2048]{1,0:T(8,128)(2,1)S(1)} collective-permute-done((bf16[32,2048]{1,0:T(8,128)(2,1)S(1)}, bf16[32,2048]{1,0:T(8,128)(2,1)S(1)}, u32[]{:S(2)}, u32[]{:S(2)}) %collective-permute-start.1) | collective-permute-done | bytes 131104 | tf_op jit(solution)/shard_map/ppermute | solution.py:23
  35.6 0.2 activate.1.own_ref
  35.8 0.1 collective-permute-start.2
  35.8 1.3 %collective-permute-done.2.other_ref = bf16[32,2176]{1,0:T(8,128)(2,1)S(1)} collective-permute-done((bf16[32,2176]{1,0:T(8,128)(2,1)S(1)}, bf16[32,2176]{1,0:T(8,128)(2,1)S(1)}, u32[]{:S(2)}, u32[]{:S(2)}) %collective-permute-start.2) | collective-permute-done | bytes 139296 | tf_op jit(solution)/shard_map/ppermute | solution.py:23
  37.2 1.9 %returned.1 = (bf16[64,1920]{1,0:T(8,128)(2,1)}, bf16[64,1024]{1,0:T(8,128)(2,1)S(1)}, bf16[64,1024]{1,0:T(8,128)(2,1)S(1)}) custom-call(bf16[32,2176]{1,0:T(8,128)(2,1)S(1)} %activate.1.own_ref, bf16[32,2176]{1,0:T(8,128)(2,1)S(1)} %collective-permute-done.2.other_ref, bf16[1792,1024]{1,0:T(8,128)(2,1)S(1)} %get-tuple-element.17.up_ref), custom_call_target="tpu_custom_call" | custom-call | flops 234881024 | bytes 3670016 | tf_op jit(solution)/shard_map/returned/pallas_call | solution.py:219
  39.1 3.6 %all-to-all-start.1 = ((bf16[8,8,1920]{2,1,0:T(8,128)(2,1)}), bf16[8,8,1920]{2,1,0:T(8,128)(2,1)S(1)}, u32[]{:S(2)}, u32[]{:S(2)}) async-start(bf16[8,8,1920]{2,1,0:T(8,128)(2,1)} %bitcast.6), calls=%async_computation.1 | async-start | bytes 491520 | tf_op jit(solution)/shard_map/all_to_all | solution.py:278
  42.7 0.1 convert_reduce_fusion
  42.8 0.0 copy-start.1
  42.8 3.0 %fusion = bf16[1,1792,1024]{2,1,0:T(8,128)(2,1)} fusion(bf16[64,1024]{1,0:T(8,128)(2,1)S(1)} %get-tuple-element.24, bf16[64,3712]{1,0:T(8,128)(2,1)S(1)} %bitcast.18), kind=kOutput, calls=%fused_computation.2 | convolution fusion | flops 236716032 | bytes 4030464 | tf_op jit(solution)/shard_map/dot_general | solution.py:16
  45.8 3.0 %fusion.1 = bf16[1,1024,1792]{2,1,0:T(8,128)(2,1)} fusion(bf16[64,1024]{1,0:T(8,128)(2,1)S(1)} %get-tuple-element.25, bf16[64,3712]{1,0:T(8,128)(2,1)S(1)} %bitcast.19, f32[64]{0:T(128)S(1)} %convert_reduce_fusion), kind=kOutput, calls=%fused_computation.3 | convolution fusion | flops 237060096 | bytes 4030976 | tf_op jit(solution)/shard_map/dot_general | solution.py:16
  48.8 2.9 %all-to-all-done.1 = bf16[8,8,1920]{2,1,0:T(8,128)(2,1)S(1)} async-done(((bf16[8,8,1920]{2,1,0:T(8,128)(2,1)}), bf16[8,8,1920]{2,1,0:T(8,128)(2,1)S(1)}, u32[]{:S(2)}, u32[]{:S(2)}) %all-to-all-start.1) | async-done | bytes 245792 | tf_op jit(solution)/shard_map/all_to_all | solution.py:278
  51.7 0.0 copy-done.1
  51.7 1.8 %collect.1 = (bf16[256,1792]{1,0:T(8,128)(2,1)}, bf16[8,256]{1,0:T(8,128)(2,1)}) custom-call(s32[8,256]{1,0:T(8,128)S(1)} %bitcast.23, bf16[64,256]{1,0:T(8,128)(2,1)S(1)} %get-tuple-element.15.hold_ref, bf16[64,1920]{1,0:T(8,128)(2,1)S(1)} %bitcast.20), custom_call_target="tpu_custom_call" | custom-call | flops 58720256 | bytes 1835008 | tf_op jit(solution)/shard_map/collect/pallas_call | solution.py:258
  (1 shorter events, 0.0 us)
Async XLA Ops:
  0.6 0.7 %copy-start = (s32[256,8]{0,1:T(8,128)S(1)}, s32[256,8]{0,1:T(8,128)}, u32[]{:S(2)}) copy-start(s32[256,8]{0,1:T(8,128)} %param.8) | copy-start | bytes 24580
  1.3 0.7 %copy-start.2 = (bf16[256,8]{0,1:T(8,128)(2,1)S(1)}, bf16[256,8]{0,1:T(8,128)(2,1)}, u32[]{:S(2)}) copy-start(bf16[256,8]{0,1:T(8,128)(2,1)} %param.9) | copy-start | bytes 12292
  28.5 1.4 %collective-permute-start = (bf16[32,2048]{1,0:T(8,128)(2,1)S(1)}, bf16[32,2048]{1,0:T(8,128)(2,1)S(1)}, u32[]{:S(2)}, u32[]{:S(2)}) collective-permute-start(bf16[32,2048]{1,0:T(8,128)(2,1)S(1)} %get-tuple-element.20), channel_id=1, source_target_pairs={{0,8},{8,0},{16,24},{24,16},{1,9},{9,1},{17,25},{25,17},{2,10},{10... | collective-permute-start | bytes 393224 | tf_op jit(solution)/shard_map/ppermute | solution.py:23
  29.9 5.6 %collective-permute-start.1 = (bf16[32,2048]{1,0:T(8,128)(2,1)S(1)}, bf16[32,2048]{1,0:T(8,128)(2,1)S(1)}, u32[]{:S(2)}, u32[]{:S(2)}) collective-permute-start(bf16[32,2048]{1,0:T(8,128)(2,1)S(1)} %add_convert_fusion.own_ref), channel_id=1, source_target_pairs={{0,16},{8,24},{16,0},{24,8},{1,17},{9,25},{17,1},{25,9},{2,18},{10... | collective-permute-start | bytes 393224 | tf_op jit(solution)/shard_map/ppermute | solution.py:23
  35.8 1.4 %collective-permute-start.2 = (bf16[32,2176]{1,0:T(8,128)(2,1)S(1)}, bf16[32,2176]{1,0:T(8,128)(2,1)S(1)}, u32[]{:S(2)}, u32[]{:S(2)}) collective-permute-start(bf16[32,2176]{1,0:T(8,128)(2,1)S(1)} %activate.1.own_ref), channel_id=1, source_target_pairs={{0,8},{8,0},{16,24},{24,16},{1,9},{9,1},{17,25},{25,17},{2,10},{10... | collective-permute-start | bytes 417800 | tf_op jit(solution)/shard_map/ppermute | solution.py:23
  39.1 12.6 %all-to-all-start.1 = ((bf16[8,8,1920]{2,1,0:T(8,128)(2,1)}), bf16[8,8,1920]{2,1,0:T(8,128)(2,1)S(1)}, u32[]{:S(2)}, u32[]{:S(2)}) async-start(bf16[8,8,1920]{2,1,0:T(8,128)(2,1)} %bitcast.6), calls=%async_computation.1 | async-start | bytes 491520 | tf_op jit(solution)/shard_map/all_to_all | solution.py:278
  42.8 8.9 %copy-start.1 = (s32[256,8]{0,1:T(8,128)S(1)}, s32[256,8]{0,1:T(8,128)}, u32[]{:S(2)}) copy-start(s32[256,8]{0,1:T(8,128)} %param.8) | copy-start | bytes 24580

commit v3 on v2

v3 whole, which is shorter than its diff:
```python
import jax
import jax.numpy as jnp
from jax import lax
from jax.experimental import pallas as pl
from jax.experimental.pallas import tpu as pltpu
from jax.sharding import PartitionSpec as P

CAP = 8
LANES = 128
VMEM = pl.BlockSpec(memory_space=pltpu.VMEM)
ANY = pl.BlockSpec(memory_space=pl.ANY)
HBM = pl.BlockSpec(memory_space=pltpu.HBM)


def contract(left, right, left_dim, right_dim):
    return lax.dot_general(
        left, right, (((left_dim,), (right_dim,)), ((), ())), preferred_element_type=jnp.float32
    )


def swap(value, bit):
    count = lax.axis_size("dp")
    return lax.ppermute(value, "dp", [(i, i ^ bit) for i in range(count)])


def padded(width):
    return -(-width // LANES) * LANES


def chunks(width, wanted):
    return [(at, min(at + wanted, width)) for at in range(0, width, wanted)]


def in_vmem(value):
    return pltpu.with_memory_space_constraint(value, pltpu.VMEM)


def in_hbm(value):
    return pltpu.with_memory_space_constraint(value, pltpu.HBM)


def params(mib):
    return pltpu.CompilerParams(vmem_limit_bytes=mib << 20)


def cost(flops, nbytes):
    return pl.CostEstimate(flops=flops, bytes_accessed=nbytes, transcendentals=0)


def route(ids, probs, tokens, cotangent, up_weight, slot_count):
    names, block_rows = ids.shape
    width = tokens.shape[1]
    step = padded(width)
    parts = chunks(width, padded(-(-width // 2)))

    def kernel(
        ids_hbm, probs_hbm, tok_hbm, cot_hbm, up_hbm,
        send_ref, hold_ref, up_ref,
        ids_ref, probs_ref, tok, cot, out, name_sems, in_sems, out_sems, weight_sems,
    ):
        small = [
            pltpu.make_async_copy(ids_hbm, ids_ref, name_sems.at[0]),
            pltpu.make_async_copy(probs_hbm, probs_ref, name_sems.at[1]),
        ]
        for copy in small:
            copy.start()
        jobs = []
        for source, target, base in ((tok_hbm, tok, 0), (cot_hbm, cot, step)):
            for low, high in parts:
                n = len(jobs)
                copy = pltpu.make_async_copy(
                    source.at[:, low:high], target.at[:, low:high], in_sems.at[n]
                )
                copy.start()
                jobs.append((copy, target, base, low, high))
        loads = []
        for n, (low, high) in enumerate(chunks(width, 448)):
            loads.append(
                pltpu.make_async_copy(up_hbm.at[low:high], up_ref.at[low:high], weight_sems.at[n])
            )
            loads[-1].start()
        slots = lax.broadcasted_iota(jnp.int32, (slot_count, block_rows), 0)
        expert = lax.shift_right_logical(slots, CAP.bit_length() - 1)
        place = (slots & (CAP - 1)).astype(jnp.float32)
        before = lax.broadcasted_iota(jnp.int32, (block_rows, block_rows), 0)
        after = lax.broadcasted_iota(jnp.int32, (block_rows, block_rows), 1)
        earlier = jnp.where(before < after, 1.0, 0.0).astype(jnp.bfloat16)
        member = jnp.zeros((slot_count, block_rows), jnp.float32)
        gate = jnp.zeros((slot_count, block_rows), jnp.float32)
        for copy in small:
            copy.wait()
        for k in range(names):
            named = ids_ref[k : k + 1, :] == expert
            member = jnp.where(named, 1.0, member)
            gate = jnp.where(named, probs_ref[k : k + 1, :].astype(jnp.float32), gate)
        rank = contract(member.astype(jnp.bfloat16), earlier, 1, 0)
        held = jnp.where(rank == place, member, 0.0)
        gates = jnp.sum(held * gate, axis=1, keepdims=True)
        hold = held.astype(jnp.bfloat16)
        hold_ref[...] = hold
        outs = []
        for n, (copy, target, base, low, high) in enumerate(jobs):
            copy.wait()
            rows = contract(hold, target[:, low:high], 1, 0)
            if base:
                rows = rows * gates
            out[:, base + low : base + high] = rows.astype(jnp.bfloat16)
            end = base + (step if high == width else high)
            push = pltpu.make_async_copy(
                out.at[:, base + low : end], send_ref.at[:, base + low : end], out_sems.at[n]
            )
            push.start()
            outs.append(push)
        for push in outs + loads:
            push.wait()

    count = 2 * len(parts)
    return pl.pallas_call(
        kernel,
        out_shape=(
            jax.ShapeDtypeStruct((slot_count, 2 * step), jnp.bfloat16),
            jax.ShapeDtypeStruct((slot_count, block_rows), jnp.bfloat16),
            pltpu.VMEM(up_weight.shape, jnp.bfloat16),
        ),
        in_specs=[HBM] * 5,
        out_specs=(ANY, VMEM, VMEM),
        scratch_shapes=[
            pltpu.VMEM(ids.shape, ids.dtype),
            pltpu.VMEM(probs.shape, probs.dtype),
            pltpu.VMEM(tokens.shape, jnp.bfloat16),
            pltpu.VMEM(tokens.shape, jnp.bfloat16),
            pltpu.VMEM((slot_count, 2 * step), jnp.bfloat16),
            pltpu.SemaphoreType.DMA((2,)),
            pltpu.SemaphoreType.DMA((count,)),
            pltpu.SemaphoreType.DMA((count,)),
            pltpu.SemaphoreType.DMA((len(chunks(width, 448)),)),
        ],
        compiler_params=params(16),
        cost_estimate=cost(4 * slot_count * block_rows * width, 8 * block_rows * width),
        name="route",
    )(*map(in_hbm, (ids, probs, tokens, cotangent, up_weight)))


def core_rows(half):
    core = lax.axis_index("dp") & 1
    return pl.multiple_of(core * half, half), pl.multiple_of((1 - core) * half, half)


def products(rows, up_weight, down_weight):
    slot_count = rows.shape[0]
    half = slot_count // 2
    width, units = up_weight.shape
    step = padded(width)

    parts = chunks(units, 256)

    def kernel(rows_ref, up_ref, down_hbm, give_ref, keep_ref, whole, down_ref, sems):
        loads = []
        for n, (low, high) in enumerate(parts):
            loads.append(
                pltpu.make_async_copy(down_hbm.at[low:high], down_ref.at[low:high], sems.at[n])
            )
            loads[-1].start()
        mine, other = core_rows(half)
        for low, high in parts:
            whole[:, low:high] = contract(rows_ref[:, :width], up_ref[:, low:high], 1, 0)
        for (low, high), load in zip(parts, loads):
            load.wait()
            whole[:, units + low : units + high] = contract(
                rows_ref[:, step : step + width], down_ref[low:high, :], 1, 1
            )
        give_ref[...] = whole[pl.ds(other, half), :].astype(jnp.bfloat16)
        keep_ref[...] = whole[pl.ds(mine, half), :]

    return pl.pallas_call(
        kernel,
        out_shape=(
            jax.ShapeDtypeStruct((half, 2 * units), jnp.bfloat16),
            jax.ShapeDtypeStruct((half, 2 * units), jnp.float32),
        ),
        in_specs=[VMEM, VMEM, HBM],
        out_specs=(VMEM, VMEM),
        scratch_shapes=[
            pltpu.VMEM((slot_count, 2 * units), jnp.float32),
            pltpu.VMEM(down_weight.shape, jnp.bfloat16),
            pltpu.SemaphoreType.DMA((len(parts),)),
        ],
        compiler_params=params(24),
        cost_estimate=cost(4 * slot_count * width * units, 4 * width * units),
        name="products",
    )(rows, in_vmem(up_weight), in_hbm(down_weight))


def activate(own, other, units):
    half = own.shape[0]

    def kernel(own_ref, other_ref, out_ref):
        total = own_ref[...].astype(jnp.float32) + other_ref[...].astype(jnp.float32)
        hidden = total[:, :units]
        query = total[:, units:]
        sigma_h = jax.nn.sigmoid(hidden)
        act = (hidden * sigma_h).astype(jnp.bfloat16)
        score = jnp.sum(act.astype(jnp.float32) * query, axis=1, keepdims=True)
        grad = query * sigma_h * (1.0 + hidden * (1.0 - sigma_h))
        out_ref[:, :units] = act
        out_ref[:, units : 2 * units] = grad.astype(jnp.bfloat16)
        out_ref[:, 2 * units :] = jnp.broadcast_to(score, (half, LANES)).astype(jnp.bfloat16)

    return pl.pallas_call(
        kernel,
        out_shape=jax.ShapeDtypeStruct((half, 2 * units + LANES), jnp.bfloat16),
        in_specs=[VMEM, VMEM],
        out_specs=VMEM,
        compiler_params=params(16),
        cost_estimate=cost(20 * half * units, 12 * half * units),
        name="activate",
    )(own, other)


def returned(own, other, up_weight):
    half = own.shape[0]
    width, units = up_weight.shape
    step = padded(width)
    parts = chunks(width, 256)

    def kernel(own_ref, other_ref, up_ref, send_ref, act_ref, grad_ref, out, sems):
        for at, source in zip(core_rows(half), (own_ref, other_ref)):
            act_ref[pl.ds(at, half), :] = source[:, :units]
            grad_ref[pl.ds(at, half), :] = source[:, units : 2 * units]
            out[pl.ds(at, half), step:] = source[:, 2 * units :]
        pushes = []
        for n, (low, high) in enumerate(parts):
            out[:, low:high] = contract(grad_ref[...], up_ref[low:high, :], 1, 1).astype(jnp.bfloat16)
            end = step + LANES if high == width else high
            push = pltpu.make_async_copy(out.at[:, low:end], send_ref.at[:, low:end], sems.at[n])
            push.start()
            pushes.append(push)
        for push in pushes:
            push.wait()

    return pl.pallas_call(
        kernel,
        out_shape=(
            jax.ShapeDtypeStruct((2 * half, step + LANES), jnp.bfloat16),
            jax.ShapeDtypeStruct((2 * half, units), jnp.bfloat16),
            jax.ShapeDtypeStruct((2 * half, units), jnp.bfloat16),
        ),
        in_specs=[VMEM, VMEM, VMEM],
        out_specs=(ANY, VMEM, VMEM),
        scratch_shapes=[
            pltpu.VMEM((2 * half, step + LANES), jnp.bfloat16),
            pltpu.SemaphoreType.DMA((len(parts),)),
        ],
        compiler_params=params(16),
        cost_estimate=cost(4 * half * width * units, 2 * width * units),
        name="returned",
    )(own, other, in_vmem(up_weight))


def collect(ids, probs, hold, back, width):
    names, block_rows = ids.shape
    slot_count = hold.shape[0]
    experts = slot_count // CAP
    step = padded(width)
    parts = chunks(width, 256)

    def kernel(ids_ref, probs_ref, hold_ref, back_ref, tok_ref, prob_ref, buf, sems):
        pushes = []
        for n, (low, high) in enumerate(parts):
            buf[:, low:high] = contract(hold_ref[...], back_ref[:, low:high], 0, 0).astype(jnp.bfloat16)
            push = pltpu.make_async_copy(buf.at[:, low:high], tok_ref.at[:, low:high], sems.at[n])
            push.start()
            pushes.append(push)
        scores = hold_ref[...].astype(jnp.float32) * back_ref[:, step : step + 1].astype(jnp.float32)
        total = jnp.zeros((names, block_rows), jnp.float32)
        for e in range(experts):
            score = jnp.sum(scores[e * CAP : (e + 1) * CAP, :], axis=0, keepdims=True)
            total = jnp.where(ids_ref[...] == e, score, total)
        prob_ref[...] = (total / probs_ref[...].astype(jnp.float32)).astype(jnp.bfloat16)
        for push in pushes:
            push.wait()

    return pl.pallas_call(
        kernel,
        out_shape=(
            jax.ShapeDtypeStruct((block_rows, width), jnp.bfloat16),
            jax.ShapeDtypeStruct((names, block_rows), jnp.bfloat16),
        ),
        in_specs=[VMEM] * 4,
        out_specs=(ANY, VMEM),
        scratch_shapes=[
            pltpu.VMEM((block_rows, width), jnp.bfloat16),
            pltpu.SemaphoreType.DMA((len(parts),)),
        ],
        compiler_params=params(16),
        cost_estimate=cost(2 * slot_count * block_rows * width, 4 * block_rows * width),
        name="collect",
    )(ids, probs, hold, back)


def exchange(rows, experts):
    rows = rows.reshape(experts, CAP, -1)
    rows = lax.all_to_all(rows, "expert", split_axis=0, concat_axis=0, tiled=True)
    return rows.reshape(experts * CAP, -1)


def on_device(tokens, cotangent, expert_ids, route_probs, w_up, w_down):
    experts = lax.axis_size("expert")
    dp_count = lax.axis_size("dp")
    width = tokens.shape[1]
    step = padded(width)
    units = w_up.shape[2]
    slot_count = experts * CAP
    ids = expert_ids.T
    probs = route_probs.T
    down_weight = w_down[0]
    send, hold, up_weight = route(ids, probs, tokens, cotangent, w_up[0], slot_count)
    rows = exchange(send, experts)
    if dp_count > 1 and dp_count & (dp_count - 1) == 0:
        gives, keeps = products(rows, up_weight, down_weight)
        own = (keeps + swap(gives, 1).astype(jnp.float32)).astype(jnp.bfloat16)
        other = jnp.zeros_like(own)
        bit = 2
        while bit < dp_count:
            if bit > 2:
                own = (own.astype(jnp.float32) + other.astype(jnp.float32)).astype(jnp.bfloat16)
            other = swap(own, bit)
            bit *= 2
        packed = activate(own, other, units)
        back, act, hidden_grad = returned(packed, swap(packed, 1), up_weight)
    else:
        hidden = contract(rows[:, :width], up_weight, 1, 0)
        query = contract(rows[:, step : step + width], down_weight, 1, 1)
        hidden, query = lax.psum((hidden, query), "dp")
        sigma_h = jax.nn.sigmoid(hidden)
        act = (hidden * sigma_h).astype(jnp.bfloat16)
        score = jnp.sum(act.astype(jnp.float32) * query, axis=1, keepdims=True).astype(jnp.bfloat16)
        hidden_grad = (query * sigma_h * (1.0 + hidden * (1.0 - sigma_h))).astype(jnp.bfloat16)
        pad = jnp.zeros((slot_count, step - width), jnp.bfloat16)
        row_grad = contract(hidden_grad, up_weight, 1, 1).astype(jnp.bfloat16)
        back = jnp.concatenate([row_grad, pad, jnp.broadcast_to(score, (slot_count, LANES))], axis=1)
    back = exchange(back, experts)
    grad_up = contract(rows[:, :width], hidden_grad, 0, 0).astype(jnp.bfloat16)[None]
    grad_down = contract(act, rows[:, step : step + width], 0, 0).astype(jnp.bfloat16)[None]
    grad_tokens, grad_probs = collect(ids, probs, hold, back, width)
    return (grad_tokens, grad_probs.T, grad_up, grad_down)


def solution(mesh):
    in_specs = (
        P("expert", "dp"),
        P("expert", "dp"),
        P("expert", None),
        P("expert", None),
        P("expert", "dp", None),
        P("expert", None, "dp"),
    )
    out_specs = (
        P("expert", "dp"),
        P("expert", None),
        P("expert", "dp", None),
        P("expert", None, "dp"),
    )
    return jax.shard_map(
        on_device, mesh=mesh, in_specs=in_specs, out_specs=out_specs, check_vma=False
    )
```

time: 53.9 us -> 53.2 us (0.987)
  local copies, waits for them, and re-layouts: 1.38 us -> 0.01 us
  Pallas kernels: 9.88 us -> 10.9 us
    pallas_call x1, Pallas kernels: 1.87 us -> 3.65 us  [products(): pl.pallas_call(kernel, out_shape=(jax.ShapeDtypeStruct((half, 2 * units),...]
    unnamed x6 -> x4, local copies, waits for them, and re-layouts: 1.38 us -> 0.01 us
    pallas_call x1, Pallas kernels: 4.05 us -> 3.37 us  [route(): pl.pallas_call(kernel, out_shape=(jax.ShapeDtypeStruct((slot_count, 2 * s...]
where the time goes in v3:
time: 53.2 us; the launch traced here: 52.9 us
  blocking collectives  20.3 us (38%)
  Pallas kernels  10.9 us (20%)
  waiting for transfers between devices  9.83 us (18%)
  matrix products  5.96 us (11%)
  starting transfers between devices  5.24 us (10%)
  between operations  0.69 us (1%)
    all_to_all x1, blocking collectives, exchange(): lax.all_to_all(rows, 'expert', split_axis=0, concat_axis=0, tiled=True)  20.3 us
    ppermute x3, waiting for transfers between devices, swap(): return lax.ppermute(value, 'dp', [(i, i ^ bit) for i in range(count)])  6.71 us
    dot_general x2, matrix products, contract(): lax.dot_general(left, right, (((left_dim,), (right_dim,)), ((), ())), pre...  5.96 us
    pallas_call x1, Pallas kernels, products(): pl.pallas_call(kernel, out_shape=(jax.ShapeDtypeStruct((half, 2 * units),...  3.65 us
    all_to_all x1, starting transfers between devices, exchange(): lax.all_to_all(rows, 'expert', split_axis=0, concat_axis=0, tiled=True)  3.54 us
    pallas_call x1, Pallas kernels, route(): pl.pallas_call(kernel, out_shape=(jax.ShapeDtypeStruct((slot_count, 2 * s...  3.37 us
    all_to_all x1, waiting for transfers between devices, exchange(): lax.all_to_all(rows, 'expert', split_axis=0, concat_axis=0, tiled=True)  3.12 us
    pallas_call x1, Pallas kernels, returned(): pl.pallas_call(kernel, out_shape=(jax.ShapeDtypeStruct((2 * half, step +...  1.92 us
  transfers between devices with their start and end apart: 4, of which 4 were waited for; matrix products, arithmetic and copies ran while one was open for 11% of the time, Pallas kernels for 0%

profile of v3, /device:TPU:0, one launch (start us, length us, event | category | flops | bytes accessed | tf_op | source)
XLA Modules:
  0.0 52.9 jit_solution(4822309720488409344)
XLA Ops:
  0.6 3.4 %route.1 = (bf16[64,3584]{1,0:T(8,128)(2,1)S(1)}, bf16[64,256]{1,0:T(8,128)(2,1)S(1)}, bf16[1792,1024]{1,0:T(8,128)(2,1)S(1)}) custom-call(s32[8,256]{1,0:T(8,128)} %bitcast.20, bf16[8,256]{1,0:T(8,128)(2,1)} %bitcast.22, bf16[256,1792]{1,0:T(8,128)(2,1)} %tok_hbm.1, bf16[256,1792]{1,0:T(8,128)(2,1)} %cot_hbm.1, bf16[1792,1024]{1,0:T(8,128)(2,1)} %bitcast.24), custom_call_target="tpu_custom_call" | custom-call | flops 117440512 | bytes 3670016 | tf_op jit(solution)/shard_map/route/pallas_call | solution.py:118
  4.0 20.3 %all_to_all.10 = bf16[8,8,3584]{2,1,0:T(8,128)(2,1)S(1)} all-to-all(bf16[8,8,3584]{2,1,0:T(8,128)(2,1)S(1)} %bitcast.19), channel_id=1, replica_groups=mesh['dp'=4,'expert'=8] {'expert'}, dimensions={0} | all-to-all | bytes 917504 | tf_op jit(solution)/shard_map/all_to_all | solution.py:303
  24.3 3.6 %products.1 = (bf16[32,2048]{1,0:T(8,128)(2,1)S(1)}, f32[32,2048]{1,0:T(8,128)S(1)}) custom-call(bf16[64,3584]{1,0:T(8,128)(2,1)S(1)} %bitcast.15, bf16[1792,1024]{1,0:T(8,128)(2,1)S(1)} %get-tuple-element.16.up_ref, bf16[1024,1792]{1,0:T(8,128)(2,1)} %bitcast.25), custom_call_target="tpu_custom_call" | custom-call | flops 469762048 | bytes 7340032 | tf_op jit(solution)/shard_map/products/pallas_call | solution.py:175
  27.9 0.1 collective-permute-start
  28.0 1.3 %collective-permute-done = bf16[32,2048]{1,0:T(8,128)(2,1)S(1)} collective-permute-done((bf16[32,2048]{1,0:T(8,128)(2,1)S(1)}, bf16[32,2048]{1,0:T(8,128)(2,1)S(1)}, u32[]{:S(2)}, u32[]{:S(2)}) %collective-permute-start) | collective-permute-done | bytes 131104 | tf_op jit(solution)/shard_map/ppermute | solution.py:23
  29.4 1.6 %collective-permute-start.1 = (bf16[32,2048]{1,0:T(8,128)(2,1)S(1)}, bf16[32,2048]{1,0:T(8,128)(2,1)S(1)}, u32[]{:S(2)}, u32[]{:S(2)}) collective-permute-start(bf16[32,2048]{1,0:T(8,128)(2,1)S(1)} %add_convert_fusion.own_ref), channel_id=1, source_target_pairs={{0,16},{8,24},{16,0},{24,8},{1,17},{9,25},{17,1},{25,9},{2,18},{10... | collective-permute-start | bytes 393224 | tf_op jit(solution)/shard_map/ppermute | solution.py:23
  31.0 4.0 %collective-permute-done.1.other_ref = bf16[32,2048]{1,0:T(8,128)(2,1)S(1)} collective-permute-done((bf16[32,2048]{1,0:T(8,128)(2,1)S(1)}, bf16[32,2048]{1,0:T(8,128)(2,1)S(1)}, u32[]{:S(2)}, u32[]{:S(2)}) %collective-permute-start.1) | collective-permute-done | bytes 131104 | tf_op jit(solution)/shard_map/ppermute | solution.py:23
  35.0 0.1 activate.1.own_ref
  35.1 0.1 collective-permute-start.2
  35.2 1.3 %collective-permute-done.2.other_ref = bf16[32,2176]{1,0:T(8,128)(2,1)S(1)} collective-permute-done((bf16[32,2176]{1,0:T(8,128)(2,1)S(1)}, bf16[32,2176]{1,0:T(8,128)(2,1)S(1)}, u32[]{:S(2)}, u32[]{:S(2)}) %collective-permute-start.2) | collective-permute-done | bytes 139296 | tf_op jit(solution)/shard_map/ppermute | solution.py:23
  36.5 1.9 %returned.1 = (bf16[64,1920]{1,0:T(8,128)(2,1)}, bf16[64,1024]{1,0:T(8,128)(2,1)S(1)}, bf16[64,1024]{1,0:T(8,128)(2,1)S(1)}) custom-call(bf16[32,2176]{1,0:T(8,128)(2,1)S(1)} %activate.1.own_ref, bf16[32,2176]{1,0:T(8,128)(2,1)S(1)} %collective-permute-done.2.other_ref, bf16[1792,1024]{1,0:T(8,128)(2,1)S(1)} %get-tuple-element.16.up_ref), custom_call_target="tpu_custom_call" | custom-call | flops 234881024 | bytes 3670016 | tf_op jit(solution)/shard_map/returned/pallas_call | solution.py:241
  38.5 3.5 %all-to-all-start.1 = ((bf16[8,8,1920]{2,1,0:T(8,128)(2,1)}), bf16[8,8,1920]{2,1,0:T(8,128)(2,1)S(1)}, u32[]{:S(2)}, u32[]{:S(2)}) async-start(bf16[8,8,1920]{2,1,0:T(8,128)(2,1)} %bitcast.6), calls=%async_computation.1 | async-start | bytes 491520 | tf_op jit(solution)/shard_map/all_to_all | solution.py:303
  42.0 0.0 copy-start
  42.0 0.0 copy-start.1
  42.0 3.0 %fusion.1 = bf16[1,1024,1792]{2,1,0:T(8,128)(2,1)} fusion(bf16[64,1024]{1,0:T(8,128)(2,1)S(1)} %get-tuple-element.23, bf16[64,3584]{1,0:T(8,128)(2,1)S(1)} %bitcast.16), kind=kOutput, calls=%fused_computation.3 | convolution fusion | flops 236716032 | bytes 4030464 | tf_op jit(solution)/shard_map/dot_general | solution.py:16
  45.0 3.0 %fusion = bf16[1,1792,1024]{2,1,0:T(8,128)(2,1)} fusion(bf16[64,1024]{1,0:T(8,128)(2,1)S(1)} %get-tuple-element.22, bf16[64,3584]{1,0:T(8,128)(2,1)S(1)} %bitcast.17), kind=kOutput, calls=%fused_computation.2 | convolution fusion | flops 236716032 | bytes 4030464 | tf_op jit(solution)/shard_map/dot_general | solution.py:16
  48.0 3.1 %all-to-all-done.1 = bf16[8,8,1920]{2,1,0:T(8,128)(2,1)S(1)} async-done(((bf16[8,8,1920]{2,1,0:T(8,128)(2,1)}), bf16[8,8,1920]{2,1,0:T(8,128)(2,1)S(1)}, u32[]{:S(2)}, u32[]{:S(2)}) %all-to-all-start.1) | async-done | bytes 245792 | tf_op jit(solution)/shard_map/all_to_all | solution.py:303
  51.1 0.0 copy-done
  51.1 0.0 copy-done.1
  51.1 1.8 %collect.1 = (bf16[256,1792]{1,0:T(8,128)(2,1)}, bf16[8,256]{1,0:T(8,128)(2,1)}) custom-call(s32[8,256]{1,0:T(8,128)S(1)} %bitcast.21, bf16[8,256]{1,0:T(8,128)(2,1)S(1)} %bitcast.23, bf16[64,256]{1,0:T(8,128)(2,1)S(1)} %get-tuple-element.14.hold_ref, bf16[64,1920]{1,0:T(8,128)(2,1)S(1)} %bitcast.18), custom_call_target="tpu_custom_call" | custom-call | flops 58720256 | bytes 1835008 | tf_op jit(solution)/shard_map/collect/pallas_call | solution.py:283
  (1 shorter events, 0.0 us)
Async XLA Ops:
  27.9 1.4 %collective-permute-start = (bf16[32,2048]{1,0:T(8,128)(2,1)S(1)}, bf16[32,2048]{1,0:T(8,128)(2,1)S(1)}, u32[]{:S(2)}, u32[]{:S(2)}) collective-permute-start(bf16[32,2048]{1,0:T(8,128)(2,1)S(1)} %get-tuple-element.18), channel_id=1, source_target_pairs={{0,8},{8,0},{16,24},{24,16},{1,9},{9,1},{17,25},{25,17},{2,10},{10... | collective-permute-start | bytes 393224 | tf_op jit(solution)/shard_map/ppermute | solution.py:23
  29.4 5.6 %collective-permute-start.1 = (bf16[32,2048]{1,0:T(8,128)(2,1)S(1)}, bf16[32,2048]{1,0:T(8,128)(2,1)S(1)}, u32[]{:S(2)}, u32[]{:S(2)}) collective-permute-start(bf16[32,2048]{1,0:T(8,128)(2,1)S(1)} %add_convert_fusion.own_ref), channel_id=1, source_target_pairs={{0,16},{8,24},{16,0},{24,8},{1,17},{9,25},{17,1},{25,9},{2,18},{10... | collective-permute-start | bytes 393224 | tf_op jit(solution)/shard_map/ppermute | solution.py:23
  35.1 1.4 %collective-permute-start.2 = (bf16[32,2176]{1,0:T(8,128)(2,1)S(1)}, bf16[32,2176]{1,0:T(8,128)(2,1)S(1)}, u32[]{:S(2)}, u32[]{:S(2)}) collective-permute-start(bf16[32,2176]{1,0:T(8,128)(2,1)S(1)} %activate.1.own_ref), channel_id=1, source_target_pairs={{0,8},{8,0},{16,24},{24,16},{1,9},{9,1},{17,25},{25,17},{2,10},{10... | collective-permute-start | bytes 417800 | tf_op jit(solution)/shard_map/ppermute | solution.py:23
  38.5 12.6 %all-to-all-start.1 = ((bf16[8,8,1920]{2,1,0:T(8,128)(2,1)}), bf16[8,8,1920]{2,1,0:T(8,128)(2,1)S(1)}, u32[]{:S(2)}, u32[]{:S(2)}) async-start(bf16[8,8,1920]{2,1,0:T(8,128)(2,1)} %bitcast.6), calls=%async_computation.1 | async-start | bytes 491520 | tf_op jit(solution)/shard_map/all_to_all | solution.py:303
  42.0 9.1 %copy-start = (s32[256,8]{0,1:T(8,128)S(1)}, s32[256,8]{0,1:T(8,128)}, u32[]{:S(2)}) copy-start(s32[256,8]{0,1:T(8,128)} %param.8) | copy-start | bytes 24580
  42.0 9.1 %copy-start.1 = (bf16[256,8]{0,1:T(8,128)(2,1)S(1)}, bf16[256,8]{0,1:T(8,128)(2,1)}, u32[]{:S(2)}) copy-start(bf16[256,8]{0,1:T(8,128)(2,1)} %param.9) | copy-start | bytes 12292

commit v4 on v3

--- a/solution.py
+++ b/solution.py
@@ -47,38 +47,21 @@
     return pl.CostEstimate(flops=flops, bytes_accessed=nbytes, transcendentals=0)
 
 
-def route(ids, probs, tokens, cotangent, up_weight, slot_count):
+def route(ids, probs, tokens, cotangent, weights, slot_count):
     names, block_rows = ids.shape
     width = tokens.shape[1]
     step = padded(width)
-    parts = chunks(width, padded(-(-width // 2)))
-
-    def kernel(
-        ids_hbm, probs_hbm, tok_hbm, cot_hbm, up_hbm,
-        send_ref, hold_ref, up_ref,
-        ids_ref, probs_ref, tok, cot, out, name_sems, in_sems, out_sems, weight_sems,
-    ):
-        small = [
-            pltpu.make_async_copy(ids_hbm, ids_ref, name_sems.at[0]),
-            pltpu.make_async_copy(probs_hbm, probs_ref, name_sems.at[1]),
+
+    def kernel(ids_hbm, probs_hbm, tok_hbm, cot_hbm, *refs):
+        send_ref, hold_ref, ids_ref, probs_ref, tok, cot, sems = refs[len(weights) :]
+        copies = [
+            pltpu.make_async_copy(source, target, sems.at[n])
+            for n, (source, target) in enumerate(
+                ((ids_hbm, ids_ref), (probs_hbm, probs_ref), (tok_hbm, tok), (cot_hbm, cot))
+            )
         ]
-        for copy in small:
+        for copy in copies:
             copy.start()
-        jobs = []
-        for source, target, base in ((tok_hbm, tok, 0), (cot_hbm, cot, step)):
-            for low, high in parts:
-                n = len(jobs)
-                copy = pltpu.make_async_copy(
-                    source.at[:, low:high], target.at[:, low:high], in_sems.at[n]
-                )
-                copy.start()
-                jobs.append((copy, target, base, low, high))
-        loads = []
-        for n, (low, high) in enumerate(chunks(width, 448)):
-            loads.append(
-                pltpu.make_async_copy(up_hbm.at[low:high], up_ref.at[low:high], weight_sems.at[n])
-            )
-            loads[-1].start()
         slots = lax.broadcasted_iota(jnp.int32, (slot_count, block_rows), 0)
         expert = lax.shift_right_logical(slots, CAP.bit_length() - 1)
         place = (slots & (CAP - 1)).astype(jnp.float32)
@@ -87,8 +70,8 @@
         earlier = jnp.where(before < after, 1.0, 0.0).astype(jnp.bfloat16)
         member = jnp.zeros((slot_count, block_rows), jnp.float32)
         gate = jnp.zeros((slot_count, block_rows), jnp.float32)
-        for copy in small:
-            copy.wait()
+        copies[0].wait()
+        copies[1].wait()
         for k in range(names):
             named = ids_ref[k : k + 1, :] == expert
             member = jnp.where(named, 1.0, member)
@@ -98,47 +81,33 @@
         gates = jnp.sum(held * gate, axis=1, keepdims=True)
         hold = held.astype(jnp.bfloat16)
         hold_ref[...] = hold
-        outs = []
-        for n, (copy, target, base, low, high) in enumerate(jobs):
-            copy.wait()
-            rows = contract(hold, target[:, low:high], 1, 0)
-            if base:
-                rows = rows * gates
-            out[:, base + low : base + high] = rows.astype(jnp.bfloat16)
-            end = base + (step if high == width else high)
-            push = pltpu.make_async_copy(
-                out.at[:, base + low : end], send_ref.at[:, base + low : end], out_sems.at[n]
-            )
-            push.start()
-            outs.append(push)
-        for push in outs + loads:
-            push.wait()
-
-    count = 2 * len(parts)
+        copies[2].wait()
+        for low, high in chunks(width, 256):
+            send_ref[:, low:high] = contract(hold, tok[:, low:high], 1, 0).astype(jnp.bfloat16)
+        copies[3].wait()
+        for low, high in chunks(width, 256):
+            rows = contract(hold, cot[:, low:high], 1, 0) * gates
+            send_ref[:, step + low : step + high] = rows.astype(jnp.bfloat16)
+
     return pl.pallas_call(
         kernel,
         out_shape=(
-            jax.ShapeDtypeStruct((slot_count, 2 * step), jnp.bfloat16),
-            jax.ShapeDtypeStruct((slot_count, block_rows), jnp.bfloat16),
-            pltpu.VMEM(up_weight.shape, jnp.bfloat16),
+            pltpu.VMEM((slot_count, 2 * step), jnp.bfloat16),
+            pltpu.VMEM((slot_count, block_rows), jnp.bfloat16),
         ),
-        in_specs=[HBM] * 5,
-        out_specs=(ANY, VMEM, VMEM),
+        in_specs=[HBM] * (4 + len(weights)),
+        out_specs=(VMEM, VMEM),
         scratch_shapes=[
             pltpu.VMEM(ids.shape, ids.dtype),
             pltpu.VMEM(probs.shape, probs.dtype),
             pltpu.VMEM(tokens.shape, jnp.bfloat16),
             pltpu.VMEM(tokens.shape, jnp.bfloat16),
-            pltpu.VMEM((slot_count, 2 * step), jnp.bfloat16),
-            pltpu.SemaphoreType.DMA((2,)),
-            pltpu.SemaphoreType.DMA((count,)),
-            pltpu.SemaphoreType.DMA((count,)),
-            pltpu.SemaphoreType.DMA((len(chunks(width, 448)),)),
+            pltpu.SemaphoreType.DMA((4,)),
         ],
-        compiler_params=params(16),
+        compiler_params=params(8),
         cost_estimate=cost(4 * slot_count * block_rows * width, 8 * block_rows * width),
         name="route",
-    )(*map(in_hbm, (ids, probs, tokens, cotangent, up_weight)))
+    )(*map(in_hbm, (ids, probs, tokens, cotangent, *weights)))
 
 
 def core_rows(half):
@@ -146,31 +115,15 @@
     return pl.multiple_of(core * half, half), pl.multiple_of((1 - core) * half, half)
 
 
-def products(rows, up_weight, down_weight):
-    slot_count = rows.shape[0]
-    half = slot_count // 2
-    width, units = up_weight.shape
-    step = padded(width)
-
-    parts = chunks(units, 256)
-
-    def kernel(rows_ref, up_ref, down_hbm, give_ref, keep_ref, whole, down_ref, sems):
-        loads = []
-        for n, (low, high) in enumerate(parts):
-            loads.append(
-                pltpu.make_async_copy(down_hbm.at[low:high], down_ref.at[low:high], sems.at[n])
-            )
-            loads[-1].start()
+def split(hidden, query):
+    rows, units = hidden.shape
+    half = rows // 2
+
+    def kernel(hidden_ref, query_ref, give_ref, keep_ref):
         mine, other = core_rows(half)
-        for low, high in parts:
-            whole[:, low:high] = contract(rows_ref[:, :width], up_ref[:, low:high], 1, 0)
-        for (low, high), load in zip(parts, loads):
-            load.wait()
-            whole[:, units + low : units + high] = contract(
-                rows_ref[:, step : step + width], down_ref[low:high, :], 1, 1
-            )
-        give_ref[...] = whole[pl.ds(other, half), :].astype(jnp.bfloat16)
-        keep_ref[...] = whole[pl.ds(mine, half), :]
+        for at, source in ((0, hidden_ref), (units, query_ref)):
+            give_ref[:, at : at + units] = source[pl.ds(other, half), :].astype(jnp.bfloat16)
+            keep_ref[:, at : at + units] = source[pl.ds(mine, half), :]
 
     return pl.pallas_call(
         kernel,
@@ -178,17 +131,12 @@
             jax.ShapeDtypeStruct((half, 2 * units), jnp.bfloat16),
             jax.ShapeDtypeStruct((half, 2 * units), jnp.float32),
         ),
-        in_specs=[VMEM, VMEM, HBM],
+        in_specs=[VMEM, VMEM],
         out_specs=(VMEM, VMEM),
-        scratch_shapes=[
-            pltpu.VMEM((slot_count, 2 * units), jnp.float32),
-            pltpu.VMEM(down_weight.shape, jnp.bfloat16),
-            pltpu.SemaphoreType.DMA((len(parts),)),
-        ],
-        compiler_params=params(24),
-        cost_estimate=cost(4 * slot_count * width * units, 4 * width * units),
-        name="products",
-    )(rows, in_vmem(up_weight), in_hbm(down_weight))
+        compiler_params=params(8),
+        cost_estimate=cost(0, 12 * half * units),
+        name="split",
+    )(hidden, query)
 
 
 def activate(own, other, units):
@@ -221,37 +169,27 @@
     half = own.shape[0]
     width, units = up_weight.shape
     step = padded(width)
-    parts = chunks(width, 256)
-
-    def kernel(own_ref, other_ref, up_ref, send_ref, act_ref, grad_ref, out, sems):
+
+    def kernel(own_ref, other_ref, up_ref, send_ref, act_ref, grad_ref):
         for at, source in zip(core_rows(half), (own_ref, other_ref)):
             act_ref[pl.ds(at, half), :] = source[:, :units]
             grad_ref[pl.ds(at, half), :] = source[:, units : 2 * units]
-            out[pl.ds(at, half), step:] = source[:, 2 * units :]
-        pushes = []
-        for n, (low, high) in enumerate(parts):
-            out[:, low:high] = contract(grad_ref[...], up_ref[low:high, :], 1, 1).astype(jnp.bfloat16)
-            end = step + LANES if high == width else high
-            push = pltpu.make_async_copy(out.at[:, low:end], send_ref.at[:, low:end], sems.at[n])
-            push.start()
-            pushes.append(push)
-        for push in pushes:
-            push.wait()
+            send_ref[pl.ds(at, half), step:] = source[:, 2 * units :]
+        for low, high in chunks(width, 256):
+            send_ref[:, low:high] = contract(grad_ref[...], up_ref[low:high, :], 1, 1).astype(
+                jnp.bfloat16
+            )
 
     return pl.pallas_call(
         kernel,
         out_shape=(
-            jax.ShapeDtypeStruct((2 * half, step + LANES), jnp.bfloat16),
-            jax.ShapeDtypeStruct((2 * half, units), jnp.bfloat16),
-            jax.ShapeDtypeStruct((2 * half, units), jnp.bfloat16),
+            pltpu.VMEM((2 * half, step + LANES), jnp.bfloat16),
+            pltpu.VMEM((2 * half, units), jnp.bfloat16),
+            pltpu.VMEM((2 * half, units), jnp.bfloat16),
         ),
         in_specs=[VMEM, VMEM, VMEM],
-        out_specs=(ANY, VMEM, VMEM),
-        scratch_shapes=[
-            pltpu.VMEM((2 * half, step + LANES), jnp.bfloat16),
-            pltpu.SemaphoreType.DMA((len(parts),)),
-        ],
-        compiler_params=params(16),
+        out_specs=(VMEM, VMEM, VMEM),
+        compiler_params=params(8),
         cost_estimate=cost(4 * half * width * units, 2 * width * units),
         name="returned",
     )(own, other, in_vmem(up_weight))
@@ -313,11 +251,14 @@
     slot_count = experts * CAP
     ids = expert_ids.T
     probs = route_probs.T
+    up_weight = w_up[0]
     down_weight = w_down[0]
-    send, hold, up_weight = route(ids, probs, tokens, cotangent, w_up[0], slot_count)
+    send, hold = route(ids, probs, tokens, cotangent, (up_weight, down_weight), slot_count)
     rows = exchange(send, experts)
     if dp_count > 1 and dp_count & (dp_count - 1) == 0:
-        gives, keeps = products(rows, up_weight, down_weight)
+        hidden = contract(rows[:, :width], up_weight, 1, 0)
+        hidden, ahead = lax.optimization_barrier((hidden, rows))
+        gives, keeps = split(hidden, contract(ahead[:, step : step + width], down_weight, 1, 1))
         own = (keeps + swap(gives, 1).astype(jnp.float32)).astype(jnp.bfloat16)
         other = jnp.zeros_like(own)
         bit = 2

time: 53.2 us -> 50.5 us (0.949)
  Pallas kernels: 10.9 us -> 5.93 us
  matrix products: 5.96 us -> 7.95 us
    pallas_call x3, Pallas kernels: 8.94 us -> 3.97 us  [the longest x1 1.99 us: route(): pl.pallas_call(kernel, out_shape=(pltpu.VMEM((slot_count, 2 * step), jnp....]
    dot_general x2 -> x4, matrix products: 5.96 us -> 7.95 us  [contract(): lax.dot_general(left, right, (((left_dim,), (right_dim,)), ((), ())), pre...]
  transfers between devices with their start and end apart: 4 -> 4, of which waited for: 4 -> 4; matrix products, arithmetic and copies ran while one was open for 11% -> 12% of each run, Pallas kernels for 0% -> 0%
where the time goes in v4:
time: 50.5 us; the launch traced here: 50.2 us
  blocking collectives  20.5 us (41%)
  waiting for transfers between devices  9.81 us (19%)
  matrix products  7.95 us (16%)
  Pallas kernels  5.93 us (12%)
  starting transfers between devices  5.24 us (10%)
  between operations  0.72 us (1%)
    all_to_all x1, blocking collectives, exchange(): lax.all_to_all(rows, 'expert', split_axis=0, concat_axis=0, tiled=True)  20.5 us
    dot_general x4, matrix products, contract(): lax.dot_general(left, right, (((left_dim,), (right_dim,)), ((), ())), pre...  7.95 us
    ppermute x3, waiting for transfers between devices, swap(): return lax.ppermute(value, 'dp', [(i, i ^ bit) for i in range(count)])  6.71 us
    all_to_all x1, starting transfers between devices, exchange(): lax.all_to_all(rows, 'expert', split_axis=0, concat_axis=0, tiled=True)  3.53 us
    all_to_all x1, waiting for transfers between devices, exchange(): lax.all_to_all(rows, 'expert', split_axis=0, concat_axis=0, tiled=True)  3.1 us
    pallas_call x1, Pallas kernels, route(): pl.pallas_call(kernel, out_shape=(pltpu.VMEM((slot_count, 2 * step), jnp....  1.99 us
    pallas_call x1, Pallas kernels, returned(): pl.pallas_call(kernel, out_shape=(pltpu.VMEM((2 * half, step + LANES), jn...  1.93 us
    pallas_call x1, Pallas kernels, collect(): pl.pallas_call(kernel, out_shape=(jax.ShapeDtypeStruct((block_rows, width...  1.84 us
  transfers between devices with their start and end apart: 4, of which 4 were waited for; matrix products, arithmetic and copies ran while one was open for 12% of the time, Pallas kernels for 0%

profile of v4, /device:TPU:0, one launch (start us, length us, event | category | flops | bytes accessed | tf_op | source)
XLA Modules:
  0.0 50.2 jit_solution(2906015788013742447)
XLA Ops:
  0.6 0.0 copy-start
  0.6 2.0 %route.1 = (bf16[64,3584]{1,0:T(8,128)(2,1)S(1)}, bf16[64,256]{1,0:T(8,128)(2,1)S(1)}) custom-call(s32[8,256]{1,0:T(8,128)} %bitcast.23, bf16[8,256]{1,0:T(8,128)(2,1)} %bitcast.25, bf16[256,1792]{1,0:T(8,128)(2,1)} %tok_hbm.1, bf16[256,1792]{1,0:T(8,128)(2,1)} %cot_hbm.1, bf16[1792,1024]{1,0:T(8,128)(2,1)} %bitcast.19, bf16[1024,1792]{1,0:T(8,128)(2,1)} %bitcast.27), custom_call_target="tpu_custom_call" | custom-call | flops 117440512 | bytes 3670016 | tf_op jit(solution)/shard_map/route/pallas_call | solution.py:92
  2.6 0.0 copy-start.3
  2.7 20.5 %all_to_all.10 = bf16[8,8,3584]{2,1,0:T(8,128)(2,1)S(1)} all-to-all(bf16[8,8,3584]{2,1,0:T(8,128)(2,1)S(1)} %bitcast.22), channel_id=1, replica_groups=mesh['dp'=4,'expert'=8] {'expert'}, dimensions={0} | all-to-all | bytes 917504 | tf_op jit(solution)/shard_map/all_to_all | solution.py:241
  23.2 0.0 copy-done
  23.2 0.8 %fusion.6.hidden_ref = f32[64,1024]{1,0:T(8,128)S(1)} fusion(bf16[64,3584]{1,0:T(8,128)(2,1)S(1)} %bitcast.28, bf16[1,1792,1024]{2,1,0:T(8,128)(2,1)S(1)} %copy-done), kind=kOutput, calls=%fused_computation.9 | convolution fusion | flops 234881024 | bytes 4161536 | tf_op jit(solution)/shard_map/dot_general | solution.py:16
  24.0 0.0 copy-done.3
  24.0 1.2 %fusion.3.query_ref = f32[64,1024]{1,0:T(8,128)S(1)} fusion(bf16[64,3584]{1,0:T(8,128)(2,1)S(1)} %bitcast.29, bf16[1,1024,1792]{2,1,0:T(8,128)(2,1)S(1)} %copy-done.3), kind=kOutput, calls=%fused_computation.6 | convolution fusion | flops 234881024 | bytes 4161536 | tf_op jit(solution)/shard_map/dot_general | solution.py:16
  25.2 0.1 collective-permute-start
  25.3 1.3 %collective-permute-done = bf16[32,2048]{1,0:T(8,128)(2,1)S(1)} collective-permute-done((bf16[32,2048]{1,0:T(8,128)(2,1)S(1)}, bf16[32,2048]{1,0:T(8,128)(2,1)S(1)}, u32[]{:S(2)}, u32[]{:S(2)}) %collective-permute-start) | collective-permute-done | bytes 131104 | tf_op jit(solution)/shard_map/ppermute | solution.py:23
  26.7 1.6 %collective-permute-start.1 = (bf16[32,2048]{1,0:T(8,128)(2,1)S(1)}, bf16[32,2048]{1,0:T(8,128)(2,1)S(1)}, u32[]{:S(2)}, u32[]{:S(2)}) collective-permute-start(bf16[32,2048]{1,0:T(8,128)(2,1)S(1)} %add_convert_fusion.own_ref), channel_id=1, source_target_pairs={{0,16},{8,24},{16,0},{24,8},{1,17},{9,25},{17,1},{25,9},{2,18},{10... | collective-permute-start | bytes 393224 | tf_op jit(solution)/shard_map/ppermute | solution.py:23
  28.3 4.0 %collective-permute-done.1.other_ref = bf16[32,2048]{1,0:T(8,128)(2,1)S(1)} collective-permute-done((bf16[32,2048]{1,0:T(8,128)(2,1)S(1)}, bf16[32,2048]{1,0:T(8,128)(2,1)S(1)}, u32[]{:S(2)}, u32[]{:S(2)}) %collective-permute-start.1) | collective-permute-done | bytes 131104 | tf_op jit(solution)/shard_map/ppermute | solution.py:23
  32.3 0.1 activate.1.own_ref
  32.4 0.1 collective-permute-start.2
  32.5 1.3 %collective-permute-done.2.other_ref = bf16[32,2176]{1,0:T(8,128)(2,1)S(1)} collective-permute-done((bf16[32,2176]{1,0:T(8,128)(2,1)S(1)}, bf16[32,2176]{1,0:T(8,128)(2,1)S(1)}, u32[]{:S(2)}, u32[]{:S(2)}) %collective-permute-start.2) | collective-permute-done | bytes 139296 | tf_op jit(solution)/shard_map/ppermute | solution.py:23
  33.8 1.9 %returned.1 = (bf16[64,1920]{1,0:T(8,128)(2,1)}, bf16[64,1024]{1,0:T(8,128)(2,1)S(1)}, bf16[64,1024]{1,0:T(8,128)(2,1)S(1)}) custom-call(bf16[32,2176]{1,0:T(8,128)(2,1)S(1)} %activate.1.own_ref, bf16[32,2176]{1,0:T(8,128)(2,1)S(1)} %collective-permute-done.2.other_ref, bf16[1792,1024]{1,0:T(8,128)(2,1)S(1)} %bitcast.20), custom_call_target="tpu_custom_call" | custom-call | flops 234881024 | bytes 3670016 | tf_op jit(solution)/shard_map/returned/pallas_call | solution.py:183
  35.8 3.5 %all-to-all-start.1 = ((bf16[8,8,1920]{2,1,0:T(8,128)(2,1)}), bf16[8,8,1920]{2,1,0:T(8,128)(2,1)S(1)}, u32[]{:S(2)}, u32[]{:S(2)}) async-start(bf16[8,8,1920]{2,1,0:T(8,128)(2,1)} %bitcast.6), calls=%async_computation.1 | async-start | bytes 491520 | tf_op jit(solution)/shard_map/all_to_all | solution.py:241
  39.3 0.0 copy-start.1
  39.3 0.0 copy-start.2
  39.3 3.0 %fusion = bf16[1,1792,1024]{2,1,0:T(8,128)(2,1)} fusion(bf16[64,1024]{1,0:T(8,128)(2,1)S(1)} %get-tuple-element.24, bf16[64,3584]{1,0:T(8,128)(2,1)S(1)} %bitcast.30), kind=kOutput, calls=%fused_computation.2 | convolution fusion | flops 236716032 | bytes 4030464 | tf_op jit(solution)/shard_map/dot_general | solution.py:16
  42.3 3.0 %fusion.1 = bf16[1,1024,1792]{2,1,0:T(8,128)(2,1)} fusion(bf16[64,1024]{1,0:T(8,128)(2,1)S(1)} %get-tuple-element.25, bf16[64,3584]{1,0:T(8,128)(2,1)S(1)} %bitcast.31), kind=kOutput, calls=%fused_computation.3 | convolution fusion | flops 236716032 | bytes 4030464 | tf_op jit(solution)/shard_map/dot_general | solution.py:16
  45.3 3.1 %all-to-all-done.1 = bf16[8,8,1920]{2,1,0:T(8,128)(2,1)S(1)} async-done(((bf16[8,8,1920]{2,1,0:T(8,128)(2,1)}), bf16[8,8,1920]{2,1,0:T(8,128)(2,1)S(1)}, u32[]{:S(2)}, u32[]{:S(2)}) %all-to-all-start.1) | async-done | bytes 245792 | tf_op jit(solution)/shard_map/all_to_all | solution.py:241
  48.4 0.0 copy-done.1
  48.4 0.0 copy-done.2
  48.4 1.8 %collect.1 = (bf16[256,1792]{1,0:T(8,128)(2,1)}, bf16[8,256]{1,0:T(8,128)(2,1)}) custom-call(s32[8,256]{1,0:T(8,128)S(1)} %bitcast.24, bf16[8,256]{1,0:T(8,128)(2,1)S(1)} %bitcast.26, bf16[64,256]{1,0:T(8,128)(2,1)S(1)} %get-tuple-element.15.hold_ref, bf16[64,1920]{1,0:T(8,128)(2,1)S(1)} %bitcast.21), custom_call_target="tpu_custom_call" | custom-call | flops 58720256 | bytes 1835008 | tf_op jit(solution)/shard_map/collect/pallas_call | solution.py:221
  (2 shorter events, 0.1 us)
Async XLA Ops:
  0.6 22.6 %copy-start = (bf16[1,1792,1024]{2,1,0:T(8,128)(2,1)S(1)}, bf16[1,1792,1024]{2,1,0:T(8,128)(2,1)}, u32[]{:S(2)}) copy-start(bf16[1,1792,1024]{2,1,0:T(8,128)(2,1)} %param.10) | copy-start | bytes 11010052
  2.6 21.3 %copy-start.3 = (bf16[1,1024,1792]{2,1,0:T(8,128)(2,1)S(1)}, bf16[1,1024,1792]{2,1,0:T(8,128)(2,1)}, u32[]{:S(2)}) copy-start(bf16[1,1024,1792]{2,1,0:T(8,128)(2,1)} %param.11) | copy-start | bytes 11010052
  25.2 1.4 %collective-permute-start = (bf16[32,2048]{1,0:T(8,128)(2,1)S(1)}, bf16[32,2048]{1,0:T(8,128)(2,1)S(1)}, u32[]{:S(2)}, u32[]{:S(2)}) collective-permute-start(bf16[32,2048]{1,0:T(8,128)(2,1)S(1)} %get-tuple-element.20), channel_id=1, source_target_pairs={{0,8},{8,0},{16,24},{24,16},{1,9},{9,1},{17,25},{25,17},{2,10},{10... | collective-permute-start | bytes 393224 | tf_op jit(solution)/shard_map/ppermute | solution.py:23
  26.7 5.6 %collective-permute-start.1 = (bf16[32,2048]{1,0:T(8,128)(2,1)S(1)}, bf16[32,2048]{1,0:T(8,128)(2,1)S(1)}, u32[]{:S(2)}, u32[]{:S(2)}) collective-permute-start(bf16[32,2048]{1,0:T(8,128)(2,1)S(1)} %add_convert_fusion.own_ref), channel_id=1, source_target_pairs={{0,16},{8,24},{16,0},{24,8},{1,17},{9,25},{17,1},{25,9},{2,18},{10... | collective-permute-start | bytes 393224 | tf_op jit(solution)/shard_map/ppermute | solution.py:23
  32.4 1.4 %collective-permute-start.2 = (bf16[32,2176]{1,0:T(8,128)(2,1)S(1)}, bf16[32,2176]{1,0:T(8,128)(2,1)S(1)}, u32[]{:S(2)}, u32[]{:S(2)}) collective-permute-start(bf16[32,2176]{1,0:T(8,128)(2,1)S(1)} %activate.1.own_ref), channel_id=1, source_target_pairs={{0,8},{8,0},{16,24},{24,16},{1,9},{9,1},{17,25},{25,17},{2,10},{10... | collective-permute-start | bytes 417800 | tf_op jit(solution)/shard_map/ppermute | solution.py:23
  35.8 12.6 %all-to-all-start.1 = ((bf16[8,8,1920]{2,1,0:T(8,128)(2,1)}), bf16[8,8,1920]{2,1,0:T(8,128)(2,1)S(1)}, u32[]{:S(2)}, u32[]{:S(2)}) async-start(bf16[8,8,1920]{2,1,0:T(8,128)(2,1)} %bitcast.6), calls=%async_computation.1 | async-start | bytes 491520 | tf_op jit(solution)/shard_map/all_to_all | solution.py:241
  39.3 9.1 %copy-start.1 = (s32[256,8]{0,1:T(8,128)S(1)}, s32[256,8]{0,1:T(8,128)}, u32[]{:S(2)}) copy-start(s32[256,8]{0,1:T(8,128)} %param.8) | copy-start | bytes 24580
  39.3 9.1 %copy-start.2 = (bf16[256,8]{0,1:T(8,128)(2,1)S(1)}, bf16[256,8]{0,1:T(8,128)(2,1)}, u32[]{:S(2)}) copy-start(bf16[256,8]{0,1:T(8,128)(2,1)} %param.9) | copy-start | bytes 12292

commit v5 on v4

--- a/solution.py
+++ b/solution.py
@@ -115,37 +115,47 @@
     return pl.multiple_of(core * half, half), pl.multiple_of((1 - core) * half, half)
 
 
-def split(hidden, query):
-    rows, units = hidden.shape
+def split(value):
+    rows, units = value.shape
     half = rows // 2
 
-    def kernel(hidden_ref, query_ref, give_ref, keep_ref):
+    def kernel(value_ref, give_ref, keep_ref):
         mine, other = core_rows(half)
-        for at, source in ((0, hidden_ref), (units, query_ref)):
-            give_ref[:, at : at + units] = source[pl.ds(other, half), :].astype(jnp.bfloat16)
-            keep_ref[:, at : at + units] = source[pl.ds(mine, half), :]
+        give_ref[...] = value_ref[pl.ds(other, half), :].astype(jnp.bfloat16)
+        keep_ref[...] = value_ref[pl.ds(mine, half), :]
 
     return pl.pallas_call(
         kernel,
         out_shape=(
-            jax.ShapeDtypeStruct((half, 2 * units), jnp.bfloat16),
-            jax.ShapeDtypeStruct((half, 2 * units), jnp.float32),
+            jax.ShapeDtypeStruct((half, units), jnp.bfloat16),
+            jax.ShapeDtypeStruct((half, units), jnp.float32),
         ),
-        in_specs=[VMEM, VMEM],
+        in_specs=[VMEM],
         out_specs=(VMEM, VMEM),
         compiler_params=params(8),
-        cost_estimate=cost(0, 12 * half * units),
+        cost_estimate=cost(0, 10 * half * units),
         name="split",
-    )(hidden, query)
-
-
-def activate(own, other, units):
-    half = own.shape[0]
-
-    def kernel(own_ref, other_ref, out_ref):
-        total = own_ref[...].astype(jnp.float32) + other_ref[...].astype(jnp.float32)
-        hidden = total[:, :units]
-        query = total[:, units:]
+    )(value)
+
+
+def summed(give, keep):
+    own = (keep + swap(give, 1).astype(jnp.float32)).astype(jnp.bfloat16)
+    other = jnp.zeros_like(own)
+    bit = 2
+    while bit < lax.axis_size("dp"):
+        if bit > 2:
+            own = (own.astype(jnp.float32) + other.astype(jnp.float32)).astype(jnp.bfloat16)
+        other = swap(own, bit)
+        bit *= 2
+    return own, other
+
+
+def activate(*terms):
+    half, units = terms[0].shape
+
+    def kernel(hidden_own, hidden_other, query_own, query_other, out_ref):
+        hidden = hidden_own[...].astype(jnp.float32) + hidden_other[...].astype(jnp.float32)
+        query = query_own[...].astype(jnp.float32) + query_other[...].astype(jnp.float32)
         sigma_h = jax.nn.sigmoid(hidden)
         act = (hidden * sigma_h).astype(jnp.bfloat16)
         score = jnp.sum(act.astype(jnp.float32) * query, axis=1, keepdims=True)
@@ -157,12 +167,12 @@
     return pl.pallas_call(
         kernel,
         out_shape=jax.ShapeDtypeStruct((half, 2 * units + LANES), jnp.bfloat16),
-        in_specs=[VMEM, VMEM],
+        in_specs=[VMEM] * 4,
         out_specs=VMEM,
         compiler_params=params(16),
         cost_estimate=cost(20 * half * units, 12 * half * units),
         name="activate",
-    )(own, other)
+    )(*terms)
 
 
 def returned(own, other, up_weight):
@@ -247,7 +257,6 @@
     dp_count = lax.axis_size("dp")
     width = tokens.shape[1]
     step = padded(width)
-    units = w_up.shape[2]
     slot_count = experts * CAP
     ids = expert_ids.T
     probs = route_probs.T
@@ -257,17 +266,12 @@
     rows = exchange(send, experts)
     if dp_count > 1 and dp_count & (dp_count - 1) == 0:
         hidden = contract(rows[:, :width], up_weight, 1, 0)
-        hidden, ahead = lax.optimization_barrier((hidden, rows))
-        gives, keeps = split(hidden, contract(ahead[:, step : step + width], down_weight, 1, 1))
-        own = (keeps + swap(gives, 1).astype(jnp.float32)).astype(jnp.bfloat16)
-        other = jnp.zeros_like(own)
-        bit = 2
-        while bit < dp_count:
-            if bit > 2:
-                own = (own.astype(jnp.float32) + other.astype(jnp.float32)).astype(jnp.bfloat16)
-            other = swap(own, bit)
-            bit *= 2
-        packed = activate(own, other, units)
+        give, keep = split(hidden)
+        give, ahead = lax.optimization_barrier((give, rows))
+        query = contract(ahead[:, step : step + width], down_weight, 1, 1)
+        hidden_terms = summed(give, keep)
+        query_terms = summed(*split(query))
+        packed = activate(*hidden_terms, *query_terms)
         back, act, hidden_grad = returned(packed, swap(packed, 1), up_weight)
     else:
         hidden = contract(rows[:, :width], up_weight, 1, 0)
@@ -302,6 +306,5 @@
         P("expert", "dp", None),
         P("expert", None, "dp"),
     )
-    return jax.shard_map(
-        on_device, mesh=mesh, in_specs=in_specs, out_specs=out_specs, check_vma=False
-    )
+
+    return jax.shard_map(on_device, mesh=mesh, in_specs=in_specs, out_specs=out_specs, check_vma=False)

time: 50.5 us -> 50.7 us (level)
  starting transfers between devices: 5.24 us -> 6.3 us
  waiting for transfers between devices: 9.81 us -> 8.96 us
    ppermute x3 -> x5, starting transfers between devices: 1.71 us -> 2.78 us  [swap(): return lax.ppermute(value, 'dp', [(i, i ^ bit) for i in range(count)])]
    ppermute x3 -> x5, waiting for transfers between devices: 6.71 us -> 5.85 us  [swap(): return lax.ppermute(value, 'dp', [(i, i ^ bit) for i in range(count)])]
  transfers between devices with their start and end apart: 4 -> 6, of which waited for: 4 -> 5; matrix products, arithmetic and copies ran while one was open for 12% -> 12% of each run, Pallas kernels for 0% -> 0%
where the time goes in v5:
time: 50.7 us; the launch traced here: 50.5 us
  blocking collectives  20.5 us (40%)
  waiting for transfers between devices  8.96 us (18%)
  matrix products  7.94 us (16%)
  starting transfers between devices  6.3 us (12%)
  Pallas kernels  5.95 us (12%)
  between operations  0.74 us (1%)
    all_to_all x1, blocking collectives, exchange(): lax.all_to_all(rows, 'expert', split_axis=0, concat_axis=0, tiled=True)  20.5 us
    dot_general x4, matrix products, contract(): lax.dot_general(left, right, (((left_dim,), (right_dim,)), ((), ())), pre...  7.94 us
    ppermute x5, waiting for transfers between devices, swap(): return lax.ppermute(value, 'dp', [(i, i ^ bit) for i in range(count)])  5.85 us
    all_to_all x1, starting transfers between devices, exchange(): lax.all_to_all(rows, 'expert', split_axis=0, concat_axis=0, tiled=True)  3.52 us
    all_to_all x1, waiting for transfers between devices, exchange(): lax.all_to_all(rows, 'expert', split_axis=0, concat_axis=0, tiled=True)  3.11 us
    ppermute x5, starting transfers between devices, swap(): return lax.ppermute(value, 'dp', [(i, i ^ bit) for i in range(count)])  2.78 us
    pallas_call x1, Pallas kernels, route(): pl.pallas_call(kernel, out_shape=(pltpu.VMEM((slot_count, 2 * step), jnp....  1.99 us
    pallas_call x1, Pallas kernels, returned(): pl.pallas_call(kernel, out_shape=(pltpu.VMEM((2 * half, step + LANES), jn...  1.93 us
  transfers between devices with their start and end apart: 6, of which 5 were waited for; matrix products, arithmetic and copies ran while one was open for 12% of the time, Pallas kernels for 0%

profile of v5, /device:TPU:0, one launch (start us, length us, event | category | flops | bytes accessed | tf_op | source)
XLA Modules:
  0.0 50.5 jit_solution(692338753110651085)
XLA Ops:
  0.6 0.0 copy-start
  0.6 2.0 %route.1 = (bf16[64,3584]{1,0:T(8,128)(2,1)S(1)}, bf16[64,256]{1,0:T(8,128)(2,1)S(1)}) custom-call(s32[8,256]{1,0:T(8,128)} %bitcast.23, bf16[8,256]{1,0:T(8,128)(2,1)} %bitcast.25, bf16[256,1792]{1,0:T(8,128)(2,1)} %tok_hbm.1, bf16[256,1792]{1,0:T(8,128)(2,1)} %cot_hbm.1, bf16[1792,1024]{1,0:T(8,128)(2,1)} %bitcast.19, bf16[1024,1792]{1,0:T(8,128)(2,1)} %bitcast.27), custom_call_target="tpu_custom_call" | custom-call | flops 117440512 | bytes 3670016 | tf_op jit(solution)/shard_map/route/pallas_call | solution.py:92
  2.6 0.0 copy-start.3
  2.7 20.5 %all_to_all.10 = bf16[8,8,3584]{2,1,0:T(8,128)(2,1)S(1)} all-to-all(bf16[8,8,3584]{2,1,0:T(8,128)(2,1)S(1)} %bitcast.22), channel_id=1, replica_groups=mesh['dp'=4,'expert'=8] {'expert'}, dimensions={0} | all-to-all | bytes 917504 | tf_op jit(solution)/shard_map/all_to_all | solution.py:251
  23.2 0.0 copy-done
  23.2 0.8 %fusion.6.value_ref = f32[64,1024]{1,0:T(8,128)S(1)} fusion(bf16[64,3584]{1,0:T(8,128)(2,1)S(1)} %bitcast.28, bf16[1,1792,1024]{2,1,0:T(8,128)(2,1)S(1)} %copy-done), kind=kOutput, calls=%fused_computation.8 | convolution fusion | flops 234881024 | bytes 4161536 | tf_op jit(solution)/shard_map/dot_general | solution.py:16
  24.0 0.0 copy-done.3
  24.0 1.2 %fusion.3.value_ref = f32[64,1024]{1,0:T(8,128)S(1)} fusion(bf16[64,3584]{1,0:T(8,128)(2,1)S(1)} %bitcast.29, bf16[1,1024,1792]{2,1,0:T(8,128)(2,1)S(1)} %copy-done.3), kind=kOutput, calls=%fused_computation.5 | convolution fusion | flops 234881024 | bytes 4161536 | tf_op jit(solution)/shard_map/dot_general | solution.py:16
  25.3 0.1 collective-permute-start.2
  25.3 0.5 collective-permute-start
  25.8 0.7 %collective-permute-done.2 = bf16[32,1024]{1,0:T(8,128)(2,1)S(1)} collective-permute-done((bf16[32,1024]{1,0:T(8,128)(2,1)S(1)}, bf16[32,1024]{1,0:T(8,128)(2,1)S(1)}, u32[]{:S(2)}, u32[]{:S(2)}) %collective-permute-start.2) | collective-permute-done | bytes 65568 | tf_op jit(solution)/shard_map/ppermute | solution.py:23
  26.6 1.6 %collective-permute-start.3 = (bf16[32,1024]{1,0:T(8,128)(2,1)S(1)}, bf16[32,1024]{1,0:T(8,128)(2,1)S(1)}, u32[]{:S(2)}, u32[]{:S(2)}) collective-permute-start(bf16[32,1024]{1,0:T(8,128)(2,1)S(1)} %add_convert_fusion.query_own), channel_id=1, source_target_pairs={{0,16},{8,24},{16,0},{24,8},{1,17},{9,25},{17,1},{25,9},{2,18},{10... | collective-permute-start | bytes 196616 | tf_op jit(solution)/shard_map/ppermute | solution.py:23
  28.2 0.0 collective-permute-done
  28.2 0.6 %collective-permute-start.1 = (bf16[32,1024]{1,0:T(8,128)(2,1)S(1)}, bf16[32,1024]{1,0:T(8,128)(2,1)S(1)}, u32[]{:S(2)}, u32[]{:S(2)}) collective-permute-start(bf16[32,1024]{1,0:T(8,128)(2,1)S(1)} %add_convert_fusion.1.hidden_own), channel_id=1, source_target_pairs={{0,16},{8,24},{16,0},{24,8},{1,17},{9,25},{17,1},{25,9},{2,18},{10... | collective-permute-start | bytes 196616 | tf_op jit(solution)/shard_map/ppermute | solution.py:23
  28.8 2.3 %collective-permute-done.3.query_other = bf16[32,1024]{1,0:T(8,128)(2,1)S(1)} collective-permute-done((bf16[32,1024]{1,0:T(8,128)(2,1)S(1)}, bf16[32,1024]{1,0:T(8,128)(2,1)S(1)}, u32[]{:S(2)}, u32[]{:S(2)}) %collective-permute-start.3) | collective-permute-done | bytes 65568 | tf_op jit(solution)/shard_map/ppermute | solution.py:23
  31.1 1.4 %collective-permute-done.1.hidden_other = bf16[32,1024]{1,0:T(8,128)(2,1)S(1)} collective-permute-done((bf16[32,1024]{1,0:T(8,128)(2,1)S(1)}, bf16[32,1024]{1,0:T(8,128)(2,1)S(1)}, u32[]{:S(2)}, u32[]{:S(2)}) %collective-permute-start.1) | collective-permute-done | bytes 65568 | tf_op jit(solution)/shard_map/ppermute | solution.py:23
  32.5 0.1 activate.1.own_ref
  32.7 0.1 collective-permute-start.4
  32.7 1.3 %collective-permute-done.4.other_ref = bf16[32,2176]{1,0:T(8,128)(2,1)S(1)} collective-permute-done((bf16[32,2176]{1,0:T(8,128)(2,1)S(1)}, bf16[32,2176]{1,0:T(8,128)(2,1)S(1)}, u32[]{:S(2)}, u32[]{:S(2)}) %collective-permute-start.4) | collective-permute-done | bytes 139296 | tf_op jit(solution)/shard_map/ppermute | solution.py:23
  34.1 1.9 %returned.1 = (bf16[64,1920]{1,0:T(8,128)(2,1)}, bf16[64,1024]{1,0:T(8,128)(2,1)S(1)}, bf16[64,1024]{1,0:T(8,128)(2,1)S(1)}) custom-call(bf16[32,2176]{1,0:T(8,128)(2,1)S(1)} %activate.1.own_ref, bf16[32,2176]{1,0:T(8,128)(2,1)S(1)} %collective-permute-done.4.other_ref, bf16[1792,1024]{1,0:T(8,128)(2,1)S(1)} %bitcast.20), custom_call_target="tpu_custom_call" | custom-call | flops 234881024 | bytes 3670016 | tf_op jit(solution)/shard_map/returned/pallas_call | solution.py:193
  36.0 3.5 %all-to-all-start.1 = ((bf16[8,8,1920]{2,1,0:T(8,128)(2,1)}), bf16[8,8,1920]{2,1,0:T(8,128)(2,1)S(1)}, u32[]{:S(2)}, u32[]{:S(2)}) async-start(bf16[8,8,1920]{2,1,0:T(8,128)(2,1)} %bitcast.6), calls=%async_computation.1 | async-start | bytes 491520 | tf_op jit(solution)/shard_map/all_to_all | solution.py:251
  39.5 0.0 copy-start.1
  39.5 0.0 copy-start.2
  39.6 3.0 %fusion = bf16[1,1792,1024]{2,1,0:T(8,128)(2,1)} fusion(bf16[64,1024]{1,0:T(8,128)(2,1)S(1)} %get-tuple-element.28, bf16[64,3584]{1,0:T(8,128)(2,1)S(1)} %bitcast.30), kind=kOutput, calls=%fused_computation.2 | convolution fusion | flops 236716032 | bytes 4030464 | tf_op jit(solution)/shard_map/dot_general | solution.py:16
  42.5 3.0 %fusion.1 = bf16[1,1024,1792]{2,1,0:T(8,128)(2,1)} fusion(bf16[64,1024]{1,0:T(8,128)(2,1)S(1)} %get-tuple-element.29, bf16[64,3584]{1,0:T(8,128)(2,1)S(1)} %bitcast.31), kind=kOutput, calls=%fused_computation.3 | convolution fusion | flops 236716032 | bytes 4030464 | tf_op jit(solution)/shard_map/dot_general | solution.py:16
  45.5 3.1 %all-to-all-done.1 = bf16[8,8,1920]{2,1,0:T(8,128)(2,1)S(1)} async-done(((bf16[8,8,1920]{2,1,0:T(8,128)(2,1)}), bf16[8,8,1920]{2,1,0:T(8,128)(2,1)S(1)}, u32[]{:S(2)}, u32[]{:S(2)}) %all-to-all-start.1) | async-done | bytes 245792 | tf_op jit(solution)/shard_map/all_to_all | solution.py:251
  48.6 0.0 copy-done.1
  48.6 0.0 copy-done.2
  48.6 1.8 %collect.1 = (bf16[256,1792]{1,0:T(8,128)(2,1)}, bf16[8,256]{1,0:T(8,128)(2,1)}) custom-call(s32[8,256]{1,0:T(8,128)S(1)} %bitcast.24, bf16[8,256]{1,0:T(8,128)(2,1)S(1)} %bitcast.26, bf16[64,256]{1,0:T(8,128)(2,1)S(1)} %get-tuple-element.17.hold_ref, bf16[64,1920]{1,0:T(8,128)(2,1)S(1)} %bitcast.21), custom_call_target="tpu_custom_call" | custom-call | flops 58720256 | bytes 1835008 | tf_op jit(solution)/shard_map/collect/pallas_call | solution.py:231
  (4 shorter events, 0.1 us)
Async XLA Ops:
  0.6 22.6 %copy-start = (bf16[1,1792,1024]{2,1,0:T(8,128)(2,1)S(1)}, bf16[1,1792,1024]{2,1,0:T(8,128)(2,1)}, u32[]{:S(2)}) copy-start(bf16[1,1792,1024]{2,1,0:T(8,128)(2,1)} %param.10) | copy-start | bytes 11010052
  2.6 21.4 %copy-start.3 = (bf16[1,1024,1792]{2,1,0:T(8,128)(2,1)S(1)}, bf16[1,1024,1792]{2,1,0:T(8,128)(2,1)}, u32[]{:S(2)}) copy-start(bf16[1,1024,1792]{2,1,0:T(8,128)(2,1)} %param.11) | copy-start | bytes 11010052
  25.3 1.3 %collective-permute-start.2 = (bf16[32,1024]{1,0:T(8,128)(2,1)S(1)}, bf16[32,1024]{1,0:T(8,128)(2,1)S(1)}, u32[]{:S(2)}, u32[]{:S(2)}) collective-permute-start(bf16[32,1024]{1,0:T(8,128)(2,1)S(1)} %get-tuple-element.24), channel_id=1, source_target_pairs={{0,8},{8,0},{16,24},{24,16},{1,9},{9,1},{17,25},{25,17},{2,10},{10... | collective-permute-start | bytes 196616 | tf_op jit(solution)/shard_map/ppermute | solution.py:23
  25.3 2.9 %collective-permute-start = (bf16[32,1024]{1,0:T(8,128)(2,1)S(1)}, bf16[32,1024]{1,0:T(8,128)(2,1)S(1)}, u32[]{:S(2)}, u32[]{:S(2)}) collective-permute-start(bf16[32,1024]{1,0:T(8,128)(2,1)S(1)} %get-tuple-element.21), channel_id=1, source_target_pairs={{0,8},{8,0},{16,24},{24,16},{1,9},{9,1},{17,25},{25,17},{2,10},{10... | collective-permute-start | bytes 196616 | tf_op jit(solution)/shard_map/ppermute | solution.py:23
  26.6 4.5 %collective-permute-start.3 = (bf16[32,1024]{1,0:T(8,128)(2,1)S(1)}, bf16[32,1024]{1,0:T(8,128)(2,1)S(1)}, u32[]{:S(2)}, u32[]{:S(2)}) collective-permute-start(bf16[32,1024]{1,0:T(8,128)(2,1)S(1)} %add_convert_fusion.query_own), channel_id=1, source_target_pairs={{0,16},{8,24},{16,0},{24,8},{1,17},{9,25},{17,1},{25,9},{2,18},{10... | collective-permute-start | bytes 196616 | tf_op jit(solution)/shard_map/ppermute | solution.py:23
  28.2 4.3 %collective-permute-start.1 = (bf16[32,1024]{1,0:T(8,128)(2,1)S(1)}, bf16[32,1024]{1,0:T(8,128)(2,1)S(1)}, u32[]{:S(2)}, u32[]{:S(2)}) collective-permute-start(bf16[32,1024]{1,0:T(8,128)(2,1)S(1)} %add_convert_fusion.1.hidden_own), channel_id=1, source_target_pairs={{0,16},{8,24},{16,0},{24,8},{1,17},{9,25},{17,1},{25,9},{2,18},{10... | collective-permute-start | bytes 196616 | tf_op jit(solution)/shard_map/ppermute | solution.py:23
  32.7 1.4 %collective-permute-start.4 = (bf16[32,2176]{1,0:T(8,128)(2,1)S(1)}, bf16[32,2176]{1,0:T(8,128)(2,1)S(1)}, u32[]{:S(2)}, u32[]{:S(2)}) collective-permute-start(bf16[32,2176]{1,0:T(8,128)(2,1)S(1)} %activate.1.own_ref), channel_id=1, source_target_pairs={{0,8},{8,0},{16,24},{24,16},{1,9},{9,1},{17,25},{25,17},{2,10},{10... | collective-permute-start | bytes 417800 | tf_op jit(solution)/shard_map/ppermute | solution.py:23
  36.0 12.6 %all-to-all-start.1 = ((bf16[8,8,1920]{2,1,0:T(8,128)(2,1)}), bf16[8,8,1920]{2,1,0:T(8,128)(2,1)S(1)}, u32[]{:S(2)}, u32[]{:S(2)}) async-start(bf16[8,8,1920]{2,1,0:T(8,128)(2,1)} %bitcast.6), calls=%async_computation.1 | async-start | bytes 491520 | tf_op jit(solution)/shard_map/all_to_all | solution.py:251
  39.5 9.1 %copy-start.1 = (s32[256,8]{0,1:T(8,128)S(1)}, s32[256,8]{0,1:T(8,128)}, u32[]{:S(2)}) copy-start(s32[256,8]{0,1:T(8,128)} %param.8) | copy-start | bytes 24580
  39.5 9.1 %copy-start.2 = (bf16[256,8]{0,1:T(8,128)(2,1)S(1)}, bf16[256,8]{0,1:T(8,128)(2,1)}, u32[]{:S(2)}) copy-start(bf16[256,8]{0,1:T(8,128)(2,1)} %param.9) | copy-start | bytes 12292

commit v6 on v5

--- a/solution.py
+++ b/solution.py
@@ -47,13 +47,28 @@
     return pl.CostEstimate(flops=flops, bytes_accessed=nbytes, transcendentals=0)
 
 
-def route(ids, probs, tokens, cotangent, weights, slot_count):
+def reorder(rows, me):
+    count = rows.shape[0]
+    here = lax.broadcasted_iota(jnp.int32, (count, count), 0)
+    there = lax.broadcasted_iota(jnp.int32, (count, count), 1)
+    moves = jnp.where(here == (there ^ (me * CAP)), 1.0, 0.0).astype(jnp.bfloat16)
+    return contract(moves, rows, 1, 0).astype(jnp.bfloat16)
+
+
+def route(ids, probs, tokens, cotangent, weights, slot_count, direct):
     names, block_rows = ids.shape
     width = tokens.shape[1]
     step = padded(width)
 
     def kernel(ids_hbm, probs_hbm, tok_hbm, cot_hbm, *refs):
-        send_ref, hold_ref, ids_ref, probs_ref, tok, cot, sems = refs[len(weights) :]
+        *send_refs, hold_ref, ids_ref, probs_ref, tok, cot, sems = refs[len(weights) :]
+        me = lax.axis_index("expert") if direct else 0
+
+        def store(rows, low, high):
+            each = slot_count // len(send_refs)
+            for j, send_ref in enumerate(send_refs):
+                send_ref[:, low:high] = rows[j * each : (j + 1) * each].astype(jnp.bfloat16)
+
         copies = [
             pltpu.make_async_copy(source, target, sems.at[n])
             for n, (source, target) in enumerate(
@@ -63,7 +78,7 @@
         for copy in copies:
             copy.start()
         slots = lax.broadcasted_iota(jnp.int32, (slot_count, block_rows), 0)
-        expert = lax.shift_right_logical(slots, CAP.bit_length() - 1)
+        expert = lax.shift_right_logical(slots, CAP.bit_length() - 1) ^ me
         place = (slots & (CAP - 1)).astype(jnp.float32)
         before = lax.broadcasted_iota(jnp.int32, (block_rows, block_rows), 0)
         after = lax.broadcasted_iota(jnp.int32, (block_rows, block_rows), 1)
@@ -80,23 +95,21 @@
         held = jnp.where(rank == place, member, 0.0)
         gates = jnp.sum(held * gate, axis=1, keepdims=True)
         hold = held.astype(jnp.bfloat16)
-        hold_ref[...] = hold
+        hold_ref[...] = reorder(hold, me) if direct else hold
         copies[2].wait()
         for low, high in chunks(width, 256):
-            send_ref[:, low:high] = contract(hold, tok[:, low:high], 1, 0).astype(jnp.bfloat16)
+            store(contract(hold, tok[:, low:high], 1, 0), low, high)
         copies[3].wait()
         for low, high in chunks(width, 256):
-            rows = contract(hold, cot[:, low:high], 1, 0) * gates
-            send_ref[:, step + low : step + high] = rows.astype(jnp.bfloat16)
-
-    return pl.pallas_call(
-        kernel,
-        out_shape=(
-            pltpu.VMEM((slot_count, 2 * step), jnp.bfloat16),
-            pltpu.VMEM((slot_count, block_rows), jnp.bfloat16),
-        ),
+            store(contract(hold, cot[:, low:high], 1, 0) * gates, step + low, step + high)
+
+    pieces = slot_count // CAP if direct else 1
+    *send, hold = pl.pallas_call(
+        kernel,
+        out_shape=(pltpu.VMEM((slot_count // pieces, 2 * step), jnp.bfloat16),) * pieces
+        + (pltpu.VMEM((slot_count, block_rows), jnp.bfloat16),),
         in_specs=[HBM] * (4 + len(weights)),
-        out_specs=(VMEM, VMEM),
+        out_specs=(VMEM,) * (pieces + 1),
         scratch_shapes=[
             pltpu.VMEM(ids.shape, ids.dtype),
             pltpu.VMEM(probs.shape, probs.dtype),
@@ -108,6 +121,7 @@
         cost_estimate=cost(4 * slot_count * block_rows * width, 8 * block_rows * width),
         name="route",
     )(*map(in_hbm, (ids, probs, tokens, cotangent, *weights)))
+    return send, hold
 
 
 def core_rows(half):
@@ -175,7 +189,7 @@
     )(*terms)
 
 
-def returned(own, other, up_weight):
+def returned(own, other, up_weight, direct):
     half = own.shape[0]
     width, units = up_weight.shape
     step = padded(width)
@@ -185,8 +199,13 @@
             act_ref[pl.ds(at, half), :] = source[:, :units]
             grad_ref[pl.ds(at, half), :] = source[:, units : 2 * units]
             send_ref[pl.ds(at, half), step:] = source[:, 2 * units :]
+        grad = grad_ref[...]
+        if direct:
+            me = lax.axis_index("expert")
+            grad = reorder(grad, me)
+            send_ref[:, step:] = reorder(send_ref[:, step:], me)
         for low, high in chunks(width, 256):
-            send_ref[:, low:high] = contract(grad_ref[...], up_ref[low:high, :], 1, 1).astype(
+            send_ref[:, low:high] = contract(grad, up_ref[low:high, :], 1, 1).astype(
                 jnp.bfloat16
             )
 
@@ -246,6 +265,14 @@
     )(ids, probs, hold, back)
 
 
+def dispatch(pieces):
+    count = len(pieces)
+    got = [pieces[0]]
+    for j in range(1, count):
+        got.append(lax.ppermute(pieces[j], "expert", [(i, i ^ j) for i in range(count)]))
+    return jnp.concatenate(got, axis=0)
+
+
 def exchange(rows, experts):
     rows = rows.reshape(experts, CAP, -1)
     rows = lax.all_to_all(rows, "expert", split_axis=0, concat_axis=0, tiled=True)
@@ -262,8 +289,11 @@
     probs = route_probs.T
     up_weight = w_up[0]
     down_weight = w_down[0]
-    send, hold = route(ids, probs, tokens, cotangent, (up_weight, down_weight), slot_count)
-    rows = exchange(send, experts)
+    direct = experts > 1 and experts & (experts - 1) == 0
+    send, hold = route(
+        ids, probs, tokens, cotangent, (up_weight, down_weight), slot_count, direct
+    )
+    rows = dispatch(send) if direct else exchange(send[0], experts)
     if dp_count > 1 and dp_count & (dp_count - 1) == 0:
         hidden = contract(rows[:, :width], up_weight, 1, 0)
         give, keep = split(hidden)
@@ -272,7 +302,7 @@
         hidden_terms = summed(give, keep)
         query_terms = summed(*split(query))
         packed = activate(*hidden_terms, *query_terms)
-        back, act, hidden_grad = returned(packed, swap(packed, 1), up_weight)
+        back, act, hidden_grad = returned(packed, swap(packed, 1), up_weight, direct)
     else:
         hidden = contract(rows[:, :width], up_weight, 1, 0)
         query = contract(rows[:, step : step + width], down_weight, 1, 1)
@@ -284,6 +314,9 @@
         pad = jnp.zeros((slot_count, step - width), jnp.bfloat16)
         row_grad = contract(hidden_grad, up_weight, 1, 1).astype(jnp.bfloat16)
         back = jnp.concatenate([row_grad, pad, jnp.broadcast_to(score, (slot_count, LANES))], axis=1)
+        if direct:
+            order = jnp.arange(slot_count, dtype=jnp.int32) ^ (lax.axis_index("expert") * CAP)
+            back = back[order]
     back = exchange(back, experts)
     grad_up = contract(rows[:, :width], hidden_grad, 0, 0).astype(jnp.bfloat16)[None]
     grad_down = contract(act, rows[:, step : step + width], 0, 0).astype(jnp.bfloat16)[None]

time: 50.7 us -> 49.8 us (0.982)
  blocking collectives: 20.5 us -> 0 us
  starting transfers between devices: 6.3 us -> 18.8 us
  waiting for transfers between devices: 8.96 us -> 15.9 us
    all_to_all x1 -> x0, blocking collectives: 20.5 us -> none  [exchange(): lax.all_to_all(rows, 'expert', split_axis=0, concat_axis=0, tiled=True)]
    ppermute x0 -> x7, starting transfers between devices: none -> 12.6 us  [dispatch(): lax.ppermute(pieces[j], 'expert', [(i, i ^ j) for i in range(count)])]
    ppermute x0 -> x7, waiting for transfers between devices: none -> 6.78 us  [dispatch(): lax.ppermute(pieces[j], 'expert', [(i, i ^ j) for i in range(count)])]
  transfers between devices with their start and end apart: 6 -> 13, of which waited for: 5 -> 7; matrix products, arithmetic and copies ran while one was open for 12% -> 12% of each run, Pallas kernels for 0% -> 0%
where the time goes in v6:
time: 49.8 us; the launch traced here: 49.6 us
  starting transfers between devices  18.8 us (38%)
  waiting for transfers between devices  15.9 us (32%)
  matrix products  7.94 us (16%)
  Pallas kernels  6.03 us (12%)
  between operations  0.82 us (2%)
    ppermute x7, starting transfers between devices, dispatch(): lax.ppermute(pieces[j], 'expert', [(i, i ^ j) for i in range(count)])  12.6 us
    dot_general x4, matrix products, contract(): lax.dot_general(left, right, (((left_dim,), (right_dim,)), ((), ())), pre...  7.94 us
    ppermute x7, waiting for transfers between devices, dispatch(): lax.ppermute(pieces[j], 'expert', [(i, i ^ j) for i in range(count)])  6.78 us
    ppermute x5, waiting for transfers between devices, swap(): return lax.ppermute(value, 'dp', [(i, i ^ bit) for i in range(count)])  5.85 us
    all_to_all x1, starting transfers between devices, exchange(): lax.all_to_all(rows, 'expert', split_axis=0, concat_axis=0, tiled=True)  3.41 us
    all_to_all x1, waiting for transfers between devices, exchange(): lax.all_to_all(rows, 'expert', split_axis=0, concat_axis=0, tiled=True)  3.22 us
    ppermute x5, starting transfers between devices, swap(): return lax.ppermute(value, 'dp', [(i, i ^ bit) for i in range(count)])  2.78 us
    pallas_call x1, Pallas kernels, returned(): pl.pallas_call(kernel, out_shape=(pltpu.VMEM((2 * half, step + LANES), jn...  2.02 us
  transfers between devices with their start and end apart: 13, of which 7 were waited for; matrix products, arithmetic and copies ran while one was open for 12% of the time, Pallas kernels for 0%

profile of v6, /device:TPU:0, one launch (start us, length us, event | category | flops | bytes accessed | tf_op | source)
XLA Modules:
  0.0 49.6 jit_solution(14319277396852905895)
XLA Ops:
  0.6 0.0 copy-start
  0.6 2.0 %route.1 = (bf16[8,3584]{1,0:T(8,128)(2,1)S(1)}, bf16[8,3584]{1,0:T(8,128)(2,1)S(1)}, bf16[8,3584]{1,0:T(8,128)(2,1)S(1)}, bf16[8,3584]{1,0:T(8,128)(2,1)S(1)}, ...) custom-call(s32[8,256]{1,0:T(8,128)} %bitcast.20, ...), custom_call_target="tpu_custom_call" | custom-call | flops 117440512 | bytes 3670016 | tf_op jit(solution)/shard_map/route/pallas_call | solution.py:107
  2.6 0.0 copy-start.3
  2.7 3.0 %collective-permute-start = (bf16[8,3584]{1,0:T(8,128)(2,1)S(1)}, bf16[8,3584]{1,0:T(8,128)(2,1)S(1)}, u32[]{:S(2)}, u32[]{:S(2)}) collective-permute-start(bf16[8,3584]{1,0:T(8,128)(2,1)S(1)} %get-tuple-element.26), channel_id=1, source_target_pairs={{0,1},{1,0},{2,3},{3,2},{4,5},{5,4},{6,7},{7,6},{8,9},{9,8},{10,11... | collective-permute-start | bytes 172040 | tf_op jit(solution)/shard_map/ppermute | solution.py:272
  5.7 1.6 %collective-permute-start.1 = (bf16[8,3584]{1,0:T(8,128)(2,1)S(1)}, bf16[8,3584]{1,0:T(8,128)(2,1)S(1)}, u32[]{:S(2)}, u32[]{:S(2)}) collective-permute-start(bf16[8,3584]{1,0:T(8,128)(2,1)S(1)} %get-tuple-element.27), channel_id=1, source_target_pairs={{0,2},{1,3},{2,0},{3,1},{4,6},{5,7},{6,4},{7,5},{8,10},{9,11},{10,... | collective-permute-start | bytes 172040 | tf_op jit(solution)/shard_map/ppermute | solution.py:272
  7.3 0.0 collective-permute-start.2
  7.3 3.0 %collective-permute-start.3 = (bf16[8,3584]{1,0:T(8,128)(2,1)S(1)}, bf16[8,3584]{1,0:T(8,128)(2,1)S(1)}, u32[]{:S(2)}, u32[]{:S(2)}) collective-permute-start(bf16[8,3584]{1,0:T(8,128)(2,1)S(1)} %get-tuple-element.29), channel_id=1, source_target_pairs={{0,4},{1,5},{2,6},{3,7},{4,0},{5,1},{6,2},{7,3},{8,12},{9,13},{10,... | collective-permute-start | bytes 172040 | tf_op jit(solution)/shard_map/ppermute | solution.py:272
  10.3 1.3 %collective-permute-start.4 = (bf16[8,3584]{1,0:T(8,128)(2,1)S(1)}, bf16[8,3584]{1,0:T(8,128)(2,1)S(1)}, u32[]{:S(2)}, u32[]{:S(2)}) collective-permute-start(bf16[8,3584]{1,0:T(8,128)(2,1)S(1)} %get-tuple-element.30), channel_id=1, source_target_pairs={{0,5},{1,4},{2,7},{3,6},{4,1},{5,0},{6,3},{7,2},{8,13},{9,12},{10,... | collective-permute-start | bytes 172040 | tf_op jit(solution)/shard_map/ppermute | solution.py:272
  11.5 0.0 collective-permute-done
  11.6 3.7 %collective-permute-start.5 = (bf16[8,3584]{1,0:T(8,128)(2,1)S(1)}, bf16[8,3584]{1,0:T(8,128)(2,1)S(1)}, u32[]{:S(2)}, u32[]{:S(2)}) collective-permute-start(bf16[8,3584]{1,0:T(8,128)(2,1)S(1)} %get-tuple-element.31), channel_id=1, source_target_pairs={{0,6},{1,7},{2,4},{3,5},{4,2},{5,3},{6,0},{7,1},{8,14},{9,15},{10,... | collective-permute-start | bytes 172040 | tf_op jit(solution)/shard_map/ppermute | solution.py:272
  15.2 0.0 collective-permute-done.1
  15.2 0.1 collective-permute-start.6
  15.3 0.0 collective-permute-done.2
  15.3 0.0 collective-permute-done.3
  15.4 3.4 %collective-permute-done.4 = bf16[8,3584]{1,0:T(8,128)(2,1)S(1)} collective-permute-done((bf16[8,3584]{1,0:T(8,128)(2,1)S(1)}, bf16[8,3584]{1,0:T(8,128)(2,1)S(1)}, u32[]{:S(2)}, u32[]{:S(2)}) %collective-permute-start.4) | collective-permute-done | bytes 57376 | tf_op jit(solution)/shard_map/ppermute | solution.py:272
  18.8 0.0 collective-permute-done.5
  18.8 3.4 %collective-permute-done.6 = bf16[8,3584]{1,0:T(8,128)(2,1)S(1)} collective-permute-done((bf16[8,3584]{1,0:T(8,128)(2,1)S(1)}, bf16[8,3584]{1,0:T(8,128)(2,1)S(1)}, u32[]{:S(2)}, u32[]{:S(2)}) %collective-permute-start.6) | collective-permute-done | bytes 57376 | tf_op jit(solution)/shard_map/ppermute | solution.py:272
  22.2 0.0 copy-done
  22.2 0.8 %fusion.6.value_ref = f32[64,1024]{1,0:T(8,128)S(1)} fusion(bf16[64,3584]{1,0:T(8,128)(2,1)S(1)} %constant_dynamic-update-slice_fusion, bf16[1,1792,1024]{2,1,0:T(8,128)(2,1)S(1)} %copy-done), kind=kOutput, calls=%fused_computation.8 | convolution fusion | flops 234881024 | bytes 4161536 | tf_op jit(solution)/shard_map/dot_general | solution.py:16
  23.0 0.0 copy-done.3
  23.0 1.2 %fusion.3.value_ref = f32[64,1024]{1,0:T(8,128)S(1)} fusion(bf16[64,3584]{1,0:T(8,128)(2,1)S(1)} %constant_dynamic-update-slice_fusion, bf16[1,1024,1792]{2,1,0:T(8,128)(2,1)S(1)} %copy-done.3), kind=kOutput, calls=%fused_computation.5 | convolution fusion | flops 234881024 | bytes 4161536 | tf_op jit(solution)/shard_map/dot_general | solution.py:16
  24.3 0.1 collective-permute-start.9
  24.3 0.5 %collective-permute-start.7 = (bf16[32,1024]{1,0:T(8,128)(2,1)S(1)}, bf16[32,1024]{1,0:T(8,128)(2,1)S(1)}, u32[]{:S(2)}, u32[]{:S(2)}) collective-permute-start(bf16[32,1024]{1,0:T(8,128)(2,1)S(1)} %get-tuple-element.35), channel_id=1, source_target_pairs={{0,8},{8,0},{16,24},{24,16},{1,9},{9,1},{17,25},{25,17},{2,10},{10... | collective-permute-start | bytes 196616 | tf_op jit(solution)/shard_map/ppermute | solution.py:23
  24.8 0.7 %collective-permute-done.9 = bf16[32,1024]{1,0:T(8,128)(2,1)S(1)} collective-permute-done((bf16[32,1024]{1,0:T(8,128)(2,1)S(1)}, bf16[32,1024]{1,0:T(8,128)(2,1)S(1)}, u32[]{:S(2)}, u32[]{:S(2)}) %collective-permute-start.9) | collective-permute-done | bytes 65568 | tf_op jit(solution)/shard_map/ppermute | solution.py:23
  25.6 1.6 %collective-permute-start.10 = (bf16[32,1024]{1,0:T(8,128)(2,1)S(1)}, bf16[32,1024]{1,0:T(8,128)(2,1)S(1)}, u32[]{:S(2)}, u32[]{:S(2)}) collective-permute-start(bf16[32,1024]{1,0:T(8,128)(2,1)S(1)} %add_convert_fusion.query_own), channel_id=1, source_target_pairs={{0,16},{8,24},{16,0},{24,8},{1,17},{9,25},{17,1},{25,9},{2,18},{10... | collective-permute-start | bytes 196616 | tf_op jit(solution)/shard_map/ppermute | solution.py:23
  27.2 0.0 collective-permute-done.7
  27.2 0.6 %collective-permute-start.8 = (bf16[32,1024]{1,0:T(8,128)(2,1)S(1)}, bf16[32,1024]{1,0:T(8,128)(2,1)S(1)}, u32[]{:S(2)}, u32[]{:S(2)}) collective-permute-start(bf16[32,1024]{1,0:T(8,128)(2,1)S(1)} %add_convert_fusion.1.hidden_own), channel_id=1, source_target_pairs={{0,16},{8,24},{16,0},{24,8},{1,17},{9,25},{17,1},{25,9},{2,18},{10... | collective-permute-start | bytes 196616 | tf_op jit(solution)/shard_map/ppermute | solution.py:23
  27.8 2.3 %collective-permute-done.10.query_other = bf16[32,1024]{1,0:T(8,128)(2,1)S(1)} collective-permute-done((bf16[32,1024]{1,0:T(8,128)(2,1)S(1)}, bf16[32,1024]{1,0:T(8,128)(2,1)S(1)}, u32[]{:S(2)}, u32[]{:S(2)}) %collective-permute-start.10) | collective-permute-done | bytes 65568 | tf_op jit(solution)/shard_map/ppermute | solution.py:23
  30.1 1.4 %collective-permute-done.8.hidden_other = bf16[32,1024]{1,0:T(8,128)(2,1)S(1)} collective-permute-done((bf16[32,1024]{1,0:T(8,128)(2,1)S(1)}, bf16[32,1024]{1,0:T(8,128)(2,1)S(1)}, u32[]{:S(2)}, u32[]{:S(2)}) %collective-permute-start.8) | collective-permute-done | bytes 65568 | tf_op jit(solution)/shard_map/ppermute | solution.py:23
  31.5 0.1 activate.1.own_ref
  31.7 0.1 collective-permute-start.11
  31.7 1.3 %collective-permute-done.11.other_ref = bf16[32,2176]{1,0:T(8,128)(2,1)S(1)} collective-permute-done((bf16[32,2176]{1,0:T(8,128)(2,1)S(1)}, bf16[32,2176]{1,0:T(8,128)(2,1)S(1)}, u32[]{:S(2)}, u32[]{:S(2)}) %collective-permute-start.11) | collective-permute-done | bytes 139296 | tf_op jit(solution)/shard_map/ppermute | solution.py:23
  33.1 2.0 %returned.1 = (bf16[64,1920]{1,0:T(8,128)(2,1)}, bf16[64,1024]{1,0:T(8,128)(2,1)S(1)}, bf16[64,1024]{1,0:T(8,128)(2,1)S(1)}) custom-call(bf16[32,2176]{1,0:T(8,128)(2,1)S(1)} %activate.1.own_ref, bf16[32,2176]{1,0:T(8,128)(2,1)S(1)} %collective-permute-done.11.other_ref, bf16[1792,1024]{1,0:T(8,128)(2,1)S(1)} %bitcast.18), custom_call_target="tpu_custom_call" | custom-call | flops 234881024 | bytes 3670016 | tf_op jit(solution)/shard_map/returned/pallas_call | solution.py:212
  35.1 3.4 %all-to-all-start = ((bf16[8,8,1920]{2,1,0:T(8,128)(2,1)}), bf16[8,8,1920]{2,1,0:T(8,128)(2,1)S(1)}, u32[]{:S(2)}, u32[]{:S(2)}) async-start(bf16[8,8,1920]{2,1,0:T(8,128)(2,1)} %bitcast.4), calls=%async_computation | async-start | bytes 491520 | tf_op jit(solution)/shard_map/all_to_all | solution.py:278
  38.5 0.0 copy-start.1
  38.5 0.0 copy-start.2
  38.5 3.0 %fusion.1 = bf16[1,1024,1792]{2,1,0:T(8,128)(2,1)} fusion(bf16[64,1024]{1,0:T(8,128)(2,1)S(1)} %get-tuple-element.43, bf16[64,3584]{1,0:T(8,128)(2,1)S(1)} %constant_dynamic-update-slice_fusion), kind=kOutput, calls=%fused_computation.3 | convolution fusion | flops 236716032 | bytes 4030464 | tf_op jit(solution)/shard_map/dot_general | solution.py:16
  41.5 3.0 %fusion = bf16[1,1792,1024]{2,1,0:T(8,128)(2,1)} fusion(bf16[64,1024]{1,0:T(8,128)(2,1)S(1)} %get-tuple-element.42, bf16[64,3584]{1,0:T(8,128)(2,1)S(1)} %constant_dynamic-update-slice_fusion), kind=kOutput, calls=%fused_computation.2 | convolution fusion | flops 236716032 | bytes 4030464 | tf_op jit(solution)/shard_map/dot_general | solution.py:16
  44.5 3.2 %all-to-all-done = bf16[8,8,1920]{2,1,0:T(8,128)(2,1)S(1)} async-done(((bf16[8,8,1920]{2,1,0:T(8,128)(2,1)}), bf16[8,8,1920]{2,1,0:T(8,128)(2,1)S(1)}, u32[]{:S(2)}, u32[]{:S(2)}) %all-to-all-start) | async-done | bytes 245792 | tf_op jit(solution)/shard_map/all_to_all | solution.py:278
  47.7 0.0 copy-done.1
  47.7 0.0 copy-done.2
  47.7 1.8 %collect.1 = (bf16[256,1792]{1,0:T(8,128)(2,1)}, bf16[8,256]{1,0:T(8,128)(2,1)}) custom-call(s32[8,256]{1,0:T(8,128)S(1)} %bitcast.21, bf16[8,256]{1,0:T(8,128)(2,1)S(1)} %bitcast.23, bf16[64,256]{1,0:T(8,128)(2,1)S(1)} %get-tuple-element.24.hold_ref, bf16[64,1920]{1,0:T(8,128)(2,1)S(1)} %bitcast.19), custom_call_target="tpu_custom_call" | custom-call | flops 58720256 | bytes 1835008 | tf_op jit(solution)/shard_map/collect/pallas_call | solution.py:250
  (12 shorter events, 0.1 us)
Async XLA Ops:
  0.6 21.5 %copy-start = (bf16[1,1792,1024]{2,1,0:T(8,128)(2,1)S(1)}, bf16[1,1792,1024]{2,1,0:T(8,128)(2,1)}, u32[]{:S(2)}) copy-start(bf16[1,1792,1024]{2,1,0:T(8,128)(2,1)} %param.10) | copy-start | bytes 11010052
  2.6 20.4 %copy-start.3 = (bf16[1,1024,1792]{2,1,0:T(8,128)(2,1)S(1)}, bf16[1,1024,1792]{2,1,0:T(8,128)(2,1)}, u32[]{:S(2)}) copy-start(bf16[1,1024,1792]{2,1,0:T(8,128)(2,1)} %param.11) | copy-start | bytes 11010052
  2.7 8.9 %collective-permute-start = (bf16[8,3584]{1,0:T(8,128)(2,1)S(1)}, bf16[8,3584]{1,0:T(8,128)(2,1)S(1)}, u32[]{:S(2)}, u32[]{:S(2)}) collective-permute-start(bf16[8,3584]{1,0:T(8,128)(2,1)S(1)} %get-tuple-element.26), channel_id=1, source_target_pairs={{0,1},{1,0},{2,3},{3,2},{4,5},{5,4},{6,7},{7,6},{8,9},{9,8},{10,11... | collective-permute-start | bytes 172040 | tf_op jit(solution)/shard_map/ppermute | solution.py:272
  5.7 9.5 %collective-permute-start.1 = (bf16[8,3584]{1,0:T(8,128)(2,1)S(1)}, bf16[8,3584]{1,0:T(8,128)(2,1)S(1)}, u32[]{:S(2)}, u32[]{:S(2)}) collective-permute-start(bf16[8,3584]{1,0:T(8,128)(2,1)S(1)} %get-tuple-element.27), channel_id=1, source_target_pairs={{0,2},{1,3},{2,0},{3,1},{4,6},{5,7},{6,4},{7,5},{8,10},{9,11},{10,... | collective-permute-start | bytes 172040 | tf_op jit(solution)/shard_map/ppermute | solution.py:272
  7.3 8.1 %collective-permute-start.2 = (bf16[8,3584]{1,0:T(8,128)(2,1)S(1)}, bf16[8,3584]{1,0:T(8,128)(2,1)S(1)}, u32[]{:S(2)}, u32[]{:S(2)}) collective-permute-start(bf16[8,3584]{1,0:T(8,128)(2,1)S(1)} %get-tuple-element.28), channel_id=1, source_target_pairs={{0,3},{1,2},{2,1},{3,0},{4,7},{5,6},{6,5},{7,4},{8,11},{9,10},{10,... | collective-permute-start | bytes 172040 | tf_op jit(solution)/shard_map/ppermute | solution.py:272
  7.3 8.1 %collective-permute-start.3 = (bf16[8,3584]{1,0:T(8,128)(2,1)S(1)}, bf16[8,3584]{1,0:T(8,128)(2,1)S(1)}, u32[]{:S(2)}, u32[]{:S(2)}) collective-permute-start(bf16[8,3584]{1,0:T(8,128)(2,1)S(1)} %get-tuple-element.29), channel_id=1, source_target_pairs={{0,4},{1,5},{2,6},{3,7},{4,0},{5,1},{6,2},{7,3},{8,12},{9,13},{10,... | collective-permute-start | bytes 172040 | tf_op jit(solution)/shard_map/ppermute | solution.py:272
  10.3 8.5 %collective-permute-start.4 = (bf16[8,3584]{1,0:T(8,128)(2,1)S(1)}, bf16[8,3584]{1,0:T(8,128)(2,1)S(1)}, u32[]{:S(2)}, u32[]{:S(2)}) collective-permute-start(bf16[8,3584]{1,0:T(8,128)(2,1)S(1)} %get-tuple-element.30), channel_id=1, source_target_pairs={{0,5},{1,4},{2,7},{3,6},{4,1},{5,0},{6,3},{7,2},{8,13},{9,12},{10,... | collective-permute-start | bytes 172040 | tf_op jit(solution)/shard_map/ppermute | solution.py:272
  11.6 7.2 %collective-permute-start.5 = (bf16[8,3584]{1,0:T(8,128)(2,1)S(1)}, bf16[8,3584]{1,0:T(8,128)(2,1)S(1)}, u32[]{:S(2)}, u32[]{:S(2)}) collective-permute-start(bf16[8,3584]{1,0:T(8,128)(2,1)S(1)} %get-tuple-element.31), channel_id=1, source_target_pairs={{0,6},{1,7},{2,4},{3,5},{4,2},{5,3},{6,0},{7,1},{8,14},{9,15},{10,... | collective-permute-start | bytes 172040 | tf_op jit(solution)/shard_map/ppermute | solution.py:272
  15.2 6.9 %collective-permute-start.6 = (bf16[8,3584]{1,0:T(8,128)(2,1)S(1)}, bf16[8,3584]{1,0:T(8,128)(2,1)S(1)}, u32[]{:S(2)}, u32[]{:S(2)}) collective-permute-start(bf16[8,3584]{1,0:T(8,128)(2,1)S(1)} %get-tuple-element.32), channel_id=1, source_target_pairs={{0,7},{1,6},{2,5},{3,4},{4,3},{5,2},{6,1},{7,0},{8,15},{9,14},{10,... | collective-permute-start | bytes 172040 | tf_op jit(solution)/shard_map/ppermute | solution.py:272
  24.3 1.3 %collective-permute-start.9 = (bf16[32,1024]{1,0:T(8,128)(2,1)S(1)}, bf16[32,1024]{1,0:T(8,128)(2,1)S(1)}, u32[]{:S(2)}, u32[]{:S(2)}) collective-permute-start(bf16[32,1024]{1,0:T(8,128)(2,1)S(1)} %get-tuple-element.38), channel_id=1, source_target_pairs={{0,8},{8,0},{16,24},{24,16},{1,9},{9,1},{17,25},{25,17},{2,10},{10... | collective-permute-start | bytes 196616 | tf_op jit(solution)/shard_map/ppermute | solution.py:23
  24.3 2.8 %collective-permute-start.7 = (bf16[32,1024]{1,0:T(8,128)(2,1)S(1)}, bf16[32,1024]{1,0:T(8,128)(2,1)S(1)}, u32[]{:S(2)}, u32[]{:S(2)}) collective-permute-start(bf16[32,1024]{1,0:T(8,128)(2,1)S(1)} %get-tuple-element.35), channel_id=1, source_target_pairs={{0,8},{8,0},{16,24},{24,16},{1,9},{9,1},{17,25},{25,17},{2,10},{10... | collective-permute-start | bytes 196616 | tf_op jit(solution)/shard_map/ppermute | solution.py:23
  25.6 4.5 %collective-permute-start.10 = (bf16[32,1024]{1,0:T(8,128)(2,1)S(1)}, bf16[32,1024]{1,0:T(8,128)(2,1)S(1)}, u32[]{:S(2)}, u32[]{:S(2)}) collective-permute-start(bf16[32,1024]{1,0:T(8,128)(2,1)S(1)} %add_convert_fusion.query_own), channel_id=1, source_target_pairs={{0,16},{8,24},{16,0},{24,8},{1,17},{9,25},{17,1},{25,9},{2,18},{10... | collective-permute-start | bytes 196616 | tf_op jit(solution)/shard_map/ppermute | solution.py:23
  27.2 4.3 %collective-permute-start.8 = (bf16[32,1024]{1,0:T(8,128)(2,1)S(1)}, bf16[32,1024]{1,0:T(8,128)(2,1)S(1)}, u32[]{:S(2)}, u32[]{:S(2)}) collective-permute-start(bf16[32,1024]{1,0:T(8,128)(2,1)S(1)} %add_convert_fusion.1.hidden_own), channel_id=1, source_target_pairs={{0,16},{8,24},{16,0},{24,8},{1,17},{9,25},{17,1},{25,9},{2,18},{10... | collective-permute-start | bytes 196616 | tf_op jit(solution)/shard_map/ppermute | solution.py:23
  31.7 1.4 %collective-permute-start.11 = (bf16[32,2176]{1,0:T(8,128)(2,1)S(1)}, bf16[32,2176]{1,0:T(8,128)(2,1)S(1)}, u32[]{:S(2)}, u32[]{:S(2)}) collective-permute-start(bf16[32,2176]{1,0:T(8,128)(2,1)S(1)} %activate.1.own_ref), channel_id=1, source_target_pairs={{0,8},{8,0},{16,24},{24,16},{1,9},{9,1},{17,25},{25,17},{2,10},{10... | collective-permute-start | bytes 417800 | tf_op jit(solution)/shard_map/ppermute | solution.py:23
  35.1 12.6 %all-to-all-start = ((bf16[8,8,1920]{2,1,0:T(8,128)(2,1)}), bf16[8,8,1920]{2,1,0:T(8,128)(2,1)S(1)}, u32[]{:S(2)}, u32[]{:S(2)}) async-start(bf16[8,8,1920]{2,1,0:T(8,128)(2,1)} %bitcast.4), calls=%async_computation | async-start | bytes 491520 | tf_op jit(solution)/shard_map/all_to_all | solution.py:278
  38.5 9.2 %copy-start.1 = (s32[256,8]{0,1:T(8,128)S(1)}, s32[256,8]{0,1:T(8,128)}, u32[]{:S(2)}) copy-start(s32[256,8]{0,1:T(8,128)} %param.8) | copy-start | bytes 24580
  38.5 9.2 %copy-start.2 = (bf16[256,8]{0,1:T(8,128)(2,1)S(1)}, bf16[256,8]{0,1:T(8,128)(2,1)}, u32[]{:S(2)}) copy-start(bf16[256,8]{0,1:T(8,128)(2,1)} %param.9) | copy-start | bytes 12292

commit v7 on v6

--- a/solution.py
+++ b/solution.py
@@ -124,6 +124,24 @@
     return send, hold
 
 
+def turned(weight):
+    rows, columns = weight.shape
+
+    def kernel(weight_ref, out_ref):
+        for low, high in chunks(rows, 256):
+            out_ref[:, low:high] = weight_ref[low:high, :].T
+
+    return pl.pallas_call(
+        kernel,
+        out_shape=pltpu.VMEM((columns, rows), weight.dtype),
+        in_specs=[VMEM],
+        out_specs=VMEM,
+        compiler_params=params(8),
+        cost_estimate=cost(0, 4 * weight.size),
+        name="turned",
+    )(in_vmem(weight))
+
+
 def core_rows(half):
     core = lax.axis_index("dp") & 1
     return pl.multiple_of(core * half, half), pl.multiple_of((1 - core) * half, half)
@@ -189,9 +207,9 @@
     )(*terms)
 
 
-def returned(own, other, up_weight, direct):
+def returned(own, other, up_turned, direct):
     half = own.shape[0]
-    width, units = up_weight.shape
+    units, width = up_turned.shape
     step = padded(width)
 
     def kernel(own_ref, other_ref, up_ref, send_ref, act_ref, grad_ref):
@@ -205,7 +223,7 @@
             grad = reorder(grad, me)
             send_ref[:, step:] = reorder(send_ref[:, step:], me)
         for low, high in chunks(width, 256):
-            send_ref[:, low:high] = contract(grad, up_ref[low:high, :], 1, 1).astype(
+            send_ref[:, low:high] = contract(grad, up_ref[:, low:high], 1, 0).astype(
                 jnp.bfloat16
             )
 
@@ -221,7 +239,7 @@
         compiler_params=params(8),
         cost_estimate=cost(4 * half * width * units, 2 * width * units),
         name="returned",
-    )(own, other, in_vmem(up_weight))
+    )(own, other, in_vmem(up_turned))
 
 
 def collect(ids, probs, hold, back, width):
@@ -265,6 +283,10 @@
     )(ids, probs, hold, back)
 
 
+def direct_size(experts):
+    return experts > 1 and experts & (experts - 1) == 0
+
+
 def dispatch(pieces):
     count = len(pieces)
     got = [pieces[0]]
@@ -289,20 +311,21 @@
     probs = route_probs.T
     up_weight = w_up[0]
     down_weight = w_down[0]
-    direct = experts > 1 and experts & (experts - 1) == 0
+    direct = direct_size(experts)
     send, hold = route(
         ids, probs, tokens, cotangent, (up_weight, down_weight), slot_count, direct
     )
     rows = dispatch(send) if direct else exchange(send[0], experts)
     if dp_count > 1 and dp_count & (dp_count - 1) == 0:
+        up_turned, down_turned = turned(up_weight), turned(down_weight)
         hidden = contract(rows[:, :width], up_weight, 1, 0)
         give, keep = split(hidden)
         give, ahead = lax.optimization_barrier((give, rows))
-        query = contract(ahead[:, step : step + width], down_weight, 1, 1)
+        query = contract(ahead[:, step : step + width], down_turned, 1, 0)
         hidden_terms = summed(give, keep)
         query_terms = summed(*split(query))
         packed = activate(*hidden_terms, *query_terms)
-        back, act, hidden_grad = returned(packed, swap(packed, 1), up_weight, direct)
+        back, act, hidden_grad = returned(packed, swap(packed, 1), up_turned, direct)
     else:
         hidden = contract(rows[:, :width], up_weight, 1, 0)
         query = contract(rows[:, step : step + width], down_weight, 1, 1)

time: 49.8 us -> 49.9 us (level)
  Pallas kernels: 6.03 us -> 7.61 us
  waiting for transfers between devices: 15.9 us -> 14.9 us
    pallas_call x0 -> x2, Pallas kernels: none -> 2.1 us  [turned(): pl.pallas_call(kernel, out_shape=pltpu.VMEM((columns, rows), weight.dtype...]
    ppermute x5, waiting for transfers between devices: 5.85 us -> 4.85 us  [swap(): return lax.ppermute(value, 'dp', [(i, i ^ bit) for i in range(count)])]
    pallas_call x1, Pallas kernels: 2.02 us -> 1.49 us  [returned(): pl.pallas_call(kernel, out_shape=(pltpu.VMEM((2 * half, step + LANES), jn...]
  transfers between devices with their start and end apart: 13 -> 13, of which waited for: 7 -> 7; matrix products, arithmetic and copies ran while one was open for 12% -> 12% of each run, Pallas kernels for 0% -> 4%
where the time goes in v7:
time: 49.9 us; the launch traced here: 49.7 us
  starting transfers between devices  18.8 us (38%)
  waiting for transfers between devices  14.9 us (30%)
  Pallas kernels  7.61 us (15%)
  matrix products  7.52 us (15%)
  between operations  0.82 us (2%)
    ppermute x7, starting transfers between devices, dispatch(): lax.ppermute(pieces[j], 'expert', [(i, i ^ j) for i in range(count)])  12.6 us
    dot_general x4, matrix products, contract(): lax.dot_general(left, right, (((left_dim,), (right_dim,)), ((), ())), pre...  7.52 us
    ppermute x7, waiting for transfers between devices, dispatch(): lax.ppermute(pieces[j], 'expert', [(i, i ^ j) for i in range(count)])  6.8 us
    ppermute x5, waiting for transfers between devices, swap(): return lax.ppermute(value, 'dp', [(i, i ^ bit) for i in range(count)])  4.85 us
    all_to_all x1, starting transfers between devices, exchange(): lax.all_to_all(rows, 'expert', split_axis=0, concat_axis=0, tiled=True)  3.41 us
    all_to_all x1, waiting for transfers between devices, exchange(): lax.all_to_all(rows, 'expert', split_axis=0, concat_axis=0, tiled=True)  3.23 us
    ppermute x5, starting transfers between devices, swap(): return lax.ppermute(value, 'dp', [(i, i ^ bit) for i in range(count)])  2.78 us
    pallas_call x2, Pallas kernels, turned(): pl.pallas_call(kernel, out_shape=pltpu.VMEM((columns, rows), weight.dtype...  2.1 us
  transfers between devices with their start and end apart: 13, of which 7 were waited for; matrix products, arithmetic and copies ran while one was open for 12% of the time, Pallas kernels for 4%

profile of v7, /device:TPU:0, one launch (start us, length us, event | category | flops | bytes accessed | tf_op | source)
XLA Modules:
  0.0 49.7 jit_solution(15250592266263672138)
XLA Ops:
  0.6 0.0 copy-start.1
  0.6 2.0 %route.1 = (bf16[8,3584]{1,0:T(8,128)(2,1)S(1)}, bf16[8,3584]{1,0:T(8,128)(2,1)S(1)}, bf16[8,3584]{1,0:T(8,128)(2,1)S(1)}, bf16[8,3584]{1,0:T(8,128)(2,1)S(1)}, ...) custom-call(s32[8,256]{1,0:T(8,128)} %bitcast.21, ...), custom_call_target="tpu_custom_call" | custom-call | flops 117440512 | bytes 3670016 | tf_op jit(solution)/shard_map/route/pallas_call | solution.py:107
  2.6 3.0 %collective-permute-start = (bf16[8,3584]{1,0:T(8,128)(2,1)S(1)}, bf16[8,3584]{1,0:T(8,128)(2,1)S(1)}, u32[]{:S(2)}, u32[]{:S(2)}) collective-permute-start(bf16[8,3584]{1,0:T(8,128)(2,1)S(1)} %get-tuple-element.26), channel_id=1, source_target_pairs={{0,1},{1,0},{2,3},{3,2},{4,5},{5,4},{6,7},{7,6},{8,9},{9,8},{10,11... | collective-permute-start | bytes 172040 | tf_op jit(solution)/shard_map/ppermute | solution.py:294
  5.7 1.6 %collective-permute-start.1 = (bf16[8,3584]{1,0:T(8,128)(2,1)S(1)}, bf16[8,3584]{1,0:T(8,128)(2,1)S(1)}, u32[]{:S(2)}, u32[]{:S(2)}) collective-permute-start(bf16[8,3584]{1,0:T(8,128)(2,1)S(1)} %get-tuple-element.27), channel_id=1, source_target_pairs={{0,2},{1,3},{2,0},{3,1},{4,6},{5,7},{6,4},{7,5},{8,10},{9,11},{10,... | collective-permute-start | bytes 172040 | tf_op jit(solution)/shard_map/ppermute | solution.py:294
  7.3 0.0 collective-permute-start.2
  7.3 3.0 %collective-permute-start.3 = (bf16[8,3584]{1,0:T(8,128)(2,1)S(1)}, bf16[8,3584]{1,0:T(8,128)(2,1)S(1)}, u32[]{:S(2)}, u32[]{:S(2)}) collective-permute-start(bf16[8,3584]{1,0:T(8,128)(2,1)S(1)} %get-tuple-element.29), channel_id=1, source_target_pairs={{0,4},{1,5},{2,6},{3,7},{4,0},{5,1},{6,2},{7,3},{8,12},{9,13},{10,... | collective-permute-start | bytes 172040 | tf_op jit(solution)/shard_map/ppermute | solution.py:294
  10.3 1.3 %collective-permute-start.4 = (bf16[8,3584]{1,0:T(8,128)(2,1)S(1)}, bf16[8,3584]{1,0:T(8,128)(2,1)S(1)}, u32[]{:S(2)}, u32[]{:S(2)}) collective-permute-start(bf16[8,3584]{1,0:T(8,128)(2,1)S(1)} %get-tuple-element.30), channel_id=1, source_target_pairs={{0,5},{1,4},{2,7},{3,6},{4,1},{5,0},{6,3},{7,2},{8,13},{9,12},{10,... | collective-permute-start | bytes 172040 | tf_op jit(solution)/shard_map/ppermute | solution.py:294
  11.5 0.0 copy-done.1
  11.5 0.0 copy-start
  11.5 1.1 %turned.2 = bf16[1792,1024]{1,0:T(8,128)(2,1)S(1)} custom-call(bf16[1024,1792]{1,0:T(8,128)(2,1)S(1)} %bitcast.19), custom_call_target="tpu_custom_call" | custom-call | bytes 7340032 | tf_op jit(solution)/shard_map/turned/pallas_call | solution.py:134
  12.6 0.0 collective-permute-done
  12.7 3.7 %collective-permute-start.5 = (bf16[8,3584]{1,0:T(8,128)(2,1)S(1)}, bf16[8,3584]{1,0:T(8,128)(2,1)S(1)}, u32[]{:S(2)}, u32[]{:S(2)}) collective-permute-start(bf16[8,3584]{1,0:T(8,128)(2,1)S(1)} %get-tuple-element.31), channel_id=1, source_target_pairs={{0,6},{1,7},{2,4},{3,5},{4,2},{5,3},{6,0},{7,1},{8,14},{9,15},{10,... | collective-permute-start | bytes 172040 | tf_op jit(solution)/shard_map/ppermute | solution.py:294
  16.3 0.0 collective-permute-done.1
  16.3 0.1 collective-permute-start.6
  16.4 0.0 collective-permute-done.2
  16.5 0.0 collective-permute-done.3
  16.5 2.3 %collective-permute-done.4 = bf16[8,3584]{1,0:T(8,128)(2,1)S(1)} collective-permute-done((bf16[8,3584]{1,0:T(8,128)(2,1)S(1)}, bf16[8,3584]{1,0:T(8,128)(2,1)S(1)}, u32[]{:S(2)}, u32[]{:S(2)}) %collective-permute-start.4) | collective-permute-done | bytes 57376 | tf_op jit(solution)/shard_map/ppermute | solution.py:294
  18.8 0.0 collective-permute-done.5
  18.8 4.5 %collective-permute-done.6 = bf16[8,3584]{1,0:T(8,128)(2,1)S(1)} collective-permute-done((bf16[8,3584]{1,0:T(8,128)(2,1)S(1)}, bf16[8,3584]{1,0:T(8,128)(2,1)S(1)}, u32[]{:S(2)}, u32[]{:S(2)}) %collective-permute-start.6) | collective-permute-done | bytes 57376 | tf_op jit(solution)/shard_map/ppermute | solution.py:294
  23.3 0.0 copy-done
  23.3 0.8 %fusion.6.value_ref = f32[64,1024]{1,0:T(8,128)S(1)} fusion(bf16[64,3584]{1,0:T(8,128)(2,1)S(1)} %constant_dynamic-update-slice_fusion, bf16[1,1792,1024]{2,1,0:T(8,128)(2,1)S(1)} %copy-done), kind=kOutput, calls=%fused_computation.8 | convolution fusion | flops 234881024 | bytes 4161536 | tf_op jit(solution)/shard_map/dot_general | solution.py:16
  24.1 0.8 %fusion.3.value_ref = f32[64,1024]{1,0:T(8,128)S(1)} fusion(bf16[1792,1024]{1,0:T(8,128)(2,1)S(1)} %turned.2, bf16[64,3584]{1,0:T(8,128)(2,1)S(1)} %constant_dynamic-update-slice_fusion), kind=kOutput, calls=%fused_computation.5 | convolution fusion | flops 234881024 | bytes 4161536 | tf_op jit(solution)/shard_map/dot_general | solution.py:16
  24.9 0.1 collective-permute-start.9
  25.0 0.5 collective-permute-start.7
  25.5 0.7 %collective-permute-done.9 = bf16[32,1024]{1,0:T(8,128)(2,1)S(1)} collective-permute-done((bf16[32,1024]{1,0:T(8,128)(2,1)S(1)}, bf16[32,1024]{1,0:T(8,128)(2,1)S(1)}, u32[]{:S(2)}, u32[]{:S(2)}) %collective-permute-start.9) | collective-permute-done | bytes 65568 | tf_op jit(solution)/shard_map/ppermute | solution.py:23
  26.3 1.6 %collective-permute-start.10 = (bf16[32,1024]{1,0:T(8,128)(2,1)S(1)}, bf16[32,1024]{1,0:T(8,128)(2,1)S(1)}, u32[]{:S(2)}, u32[]{:S(2)}) collective-permute-start(bf16[32,1024]{1,0:T(8,128)(2,1)S(1)} %add_convert_fusion.query_own), channel_id=1, source_target_pairs={{0,16},{8,24},{16,0},{24,8},{1,17},{9,25},{17,1},{25,9},{2,18},{10... | collective-permute-start | bytes 196616 | tf_op jit(solution)/shard_map/ppermute | solution.py:23
  27.9 0.0 collective-permute-done.7
  27.9 0.6 %collective-permute-start.8 = (bf16[32,1024]{1,0:T(8,128)(2,1)S(1)}, bf16[32,1024]{1,0:T(8,128)(2,1)S(1)}, u32[]{:S(2)}, u32[]{:S(2)}) collective-permute-start(bf16[32,1024]{1,0:T(8,128)(2,1)S(1)} %add_convert_fusion.1.hidden_own), channel_id=1, source_target_pairs={{0,16},{8,24},{16,0},{24,8},{1,17},{9,25},{17,1},{25,9},{2,18},{10... | collective-permute-start | bytes 196616 | tf_op jit(solution)/shard_map/ppermute | solution.py:23
  28.4 2.3 %collective-permute-done.10.query_other = bf16[32,1024]{1,0:T(8,128)(2,1)S(1)} collective-permute-done((bf16[32,1024]{1,0:T(8,128)(2,1)S(1)}, bf16[32,1024]{1,0:T(8,128)(2,1)S(1)}, u32[]{:S(2)}, u32[]{:S(2)}) %collective-permute-start.10) | collective-permute-done | bytes 65568 | tf_op jit(solution)/shard_map/ppermute | solution.py:23
  30.8 1.4 %collective-permute-done.8.hidden_other = bf16[32,1024]{1,0:T(8,128)(2,1)S(1)} collective-permute-done((bf16[32,1024]{1,0:T(8,128)(2,1)S(1)}, bf16[32,1024]{1,0:T(8,128)(2,1)S(1)}, u32[]{:S(2)}, u32[]{:S(2)}) %collective-permute-start.8) | collective-permute-done | bytes 65568 | tf_op jit(solution)/shard_map/ppermute | solution.py:23
  32.2 0.1 activate.1.own_ref
  32.3 0.1 collective-permute-start.11
  32.4 1.0 %turned.3.up_ref = bf16[1024,1792]{1,0:T(8,128)(2,1)S(1)} custom-call(bf16[1792,1024]{1,0:T(8,128)(2,1)S(1)} %bitcast.17), custom_call_target="tpu_custom_call" | custom-call | bytes 7340032 | tf_op jit(solution)/shard_map/turned/pallas_call | solution.py:134
  33.4 0.3 collective-permute-done.11.other_ref
  33.7 1.5 %returned.1 = (bf16[64,1920]{1,0:T(8,128)(2,1)}, bf16[64,1024]{1,0:T(8,128)(2,1)S(1)}, bf16[64,1024]{1,0:T(8,128)(2,1)S(1)}) custom-call(bf16[32,2176]{1,0:T(8,128)(2,1)S(1)} %activate.1.own_ref, bf16[32,2176]{1,0:T(8,128)(2,1)S(1)} %collective-permute-done.11.other_ref, bf16[1024,1792]{1,0:T(8,128)(2,1)S(1)} %turned.3.up_ref), custom_call_target="tpu_custom_call" | custom-call | flops 234881024 | bytes 3670016 | tf_op jit(solution)/shard_map/returned/pallas_call | solution.py:230
  35.2 3.4 %all-to-all-start = ((bf16[8,8,1920]{2,1,0:T(8,128)(2,1)}), bf16[8,8,1920]{2,1,0:T(8,128)(2,1)S(1)}, u32[]{:S(2)}, u32[]{:S(2)}) async-start(bf16[8,8,1920]{2,1,0:T(8,128)(2,1)} %bitcast.4), calls=%async_computation | async-start | bytes 491520 | tf_op jit(solution)/shard_map/all_to_all | solution.py:300
  38.6 0.0 copy-start.2
  38.7 0.0 copy-start.3
  38.7 3.0 %fusion.1 = bf16[1,1024,1792]{2,1,0:T(8,128)(2,1)} fusion(bf16[64,1024]{1,0:T(8,128)(2,1)S(1)} %get-tuple-element.43, bf16[64,3584]{1,0:T(8,128)(2,1)S(1)} %constant_dynamic-update-slice_fusion), kind=kOutput, calls=%fused_computation.3 | convolution fusion | flops 236716032 | bytes 4030464 | tf_op jit(solution)/shard_map/dot_general | solution.py:16
  41.7 3.0 %fusion = bf16[1,1792,1024]{2,1,0:T(8,128)(2,1)} fusion(bf16[64,1024]{1,0:T(8,128)(2,1)S(1)} %get-tuple-element.42, bf16[64,3584]{1,0:T(8,128)(2,1)S(1)} %constant_dynamic-update-slice_fusion), kind=kOutput, calls=%fused_computation.2 | convolution fusion | flops 236716032 | bytes 4030464 | tf_op jit(solution)/shard_map/dot_general | solution.py:16
  44.6 3.2 %all-to-all-done = bf16[8,8,1920]{2,1,0:T(8,128)(2,1)S(1)} async-done(((bf16[8,8,1920]{2,1,0:T(8,128)(2,1)}), bf16[8,8,1920]{2,1,0:T(8,128)(2,1)S(1)}, u32[]{:S(2)}, u32[]{:S(2)}) %all-to-all-start) | async-done | bytes 245792 | tf_op jit(solution)/shard_map/all_to_all | solution.py:300
  47.9 0.0 copy-done.2
  47.9 0.0 copy-done.3
  47.9 1.8 %collect.1 = (bf16[256,1792]{1,0:T(8,128)(2,1)}, bf16[8,256]{1,0:T(8,128)(2,1)}) custom-call(s32[8,256]{1,0:T(8,128)S(1)} %bitcast.22, bf16[8,256]{1,0:T(8,128)(2,1)S(1)} %bitcast.24, bf16[64,256]{1,0:T(8,128)(2,1)S(1)} %get-tuple-element.24.hold_ref, bf16[64,1920]{1,0:T(8,128)(2,1)S(1)} %bitcast.20), custom_call_target="tpu_custom_call" | custom-call | flops 58720256 | bytes 1835008 | tf_op jit(solution)/shard_map/collect/pallas_call | solution.py:268
  (12 shorter events, 0.1 us)
Async XLA Ops:
  0.6 10.9 %copy-start.1 = (bf16[1,1024,1792]{2,1,0:T(8,128)(2,1)S(1)}, bf16[1,1024,1792]{2,1,0:T(8,128)(2,1)}, u32[]{:S(2)}) copy-start(bf16[1,1024,1792]{2,1,0:T(8,128)(2,1)} %param.11) | copy-start | bytes 11010052
  2.6 10.0 %collective-permute-start = (bf16[8,3584]{1,0:T(8,128)(2,1)S(1)}, bf16[8,3584]{1,0:T(8,128)(2,1)S(1)}, u32[]{:S(2)}, u32[]{:S(2)}) collective-permute-start(bf16[8,3584]{1,0:T(8,128)(2,1)S(1)} %get-tuple-element.26), channel_id=1, source_target_pairs={{0,1},{1,0},{2,3},{3,2},{4,5},{5,4},{6,7},{7,6},{8,9},{9,8},{10,11... | collective-permute-start | bytes 172040 | tf_op jit(solution)/shard_map/ppermute | solution.py:294
  5.7 10.7 %collective-permute-start.1 = (bf16[8,3584]{1,0:T(8,128)(2,1)S(1)}, bf16[8,3584]{1,0:T(8,128)(2,1)S(1)}, u32[]{:S(2)}, u32[]{:S(2)}) collective-permute-start(bf16[8,3584]{1,0:T(8,128)(2,1)S(1)} %get-tuple-element.27), channel_id=1, source_target_pairs={{0,2},{1,3},{2,0},{3,1},{4,6},{5,7},{6,4},{7,5},{8,10},{9,11},{10,... | collective-permute-start | bytes 172040 | tf_op jit(solution)/shard_map/ppermute | solution.py:294
  7.3 9.2 %collective-permute-start.2 = (bf16[8,3584]{1,0:T(8,128)(2,1)S(1)}, bf16[8,3584]{1,0:T(8,128)(2,1)S(1)}, u32[]{:S(2)}, u32[]{:S(2)}) collective-permute-start(bf16[8,3584]{1,0:T(8,128)(2,1)S(1)} %get-tuple-element.28), channel_id=1, source_target_pairs={{0,3},{1,2},{2,1},{3,0},{4,7},{5,6},{6,5},{7,4},{8,11},{9,10},{10,... | collective-permute-start | bytes 172040 | tf_op jit(solution)/shard_map/ppermute | solution.py:294
  7.3 9.2 %collective-permute-start.3 = (bf16[8,3584]{1,0:T(8,128)(2,1)S(1)}, bf16[8,3584]{1,0:T(8,128)(2,1)S(1)}, u32[]{:S(2)}, u32[]{:S(2)}) collective-permute-start(bf16[8,3584]{1,0:T(8,128)(2,1)S(1)} %get-tuple-element.29), channel_id=1, source_target_pairs={{0,4},{1,5},{2,6},{3,7},{4,0},{5,1},{6,2},{7,3},{8,12},{9,13},{10,... | collective-permute-start | bytes 172040 | tf_op jit(solution)/shard_map/ppermute | solution.py:294
  10.3 8.5 %collective-permute-start.4 = (bf16[8,3584]{1,0:T(8,128)(2,1)S(1)}, bf16[8,3584]{1,0:T(8,128)(2,1)S(1)}, u32[]{:S(2)}, u32[]{:S(2)}) collective-permute-start(bf16[8,3584]{1,0:T(8,128)(2,1)S(1)} %get-tuple-element.30), channel_id=1, source_target_pairs={{0,5},{1,4},{2,7},{3,6},{4,1},{5,0},{6,3},{7,2},{8,13},{9,12},{10,... | collective-permute-start | bytes 172040 | tf_op jit(solution)/shard_map/ppermute | solution.py:294
  11.5 11.8 %copy-start = (bf16[1,1792,1024]{2,1,0:T(8,128)(2,1)S(1)}, bf16[1,1792,1024]{2,1,0:T(8,128)(2,1)}, u32[]{:S(2)}) copy-start(bf16[1,1792,1024]{2,1,0:T(8,128)(2,1)} %param.10) | copy-start | bytes 11010052
  12.7 6.1 %collective-permute-start.5 = (bf16[8,3584]{1,0:T(8,128)(2,1)S(1)}, bf16[8,3584]{1,0:T(8,128)(2,1)S(1)}, u32[]{:S(2)}, u32[]{:S(2)}) collective-permute-start(bf16[8,3584]{1,0:T(8,128)(2,1)S(1)} %get-tuple-element.31), channel_id=1, source_target_pairs={{0,6},{1,7},{2,4},{3,5},{4,2},{5,3},{6,0},{7,1},{8,14},{9,15},{10,... | collective-permute-start | bytes 172040 | tf_op jit(solution)/shard_map/ppermute | solution.py:294
  16.3 6.9 %collective-permute-start.6 = (bf16[8,3584]{1,0:T(8,128)(2,1)S(1)}, bf16[8,3584]{1,0:T(8,128)(2,1)S(1)}, u32[]{:S(2)}, u32[]{:S(2)}) collective-permute-start(bf16[8,3584]{1,0:T(8,128)(2,1)S(1)} %get-tuple-element.32), channel_id=1, source_target_pairs={{0,7},{1,6},{2,5},{3,4},{4,3},{5,2},{6,1},{7,0},{8,15},{9,14},{10,... | collective-permute-start | bytes 172040 | tf_op jit(solution)/shard_map/ppermute | solution.py:294
  24.9 1.3 %collective-permute-start.9 = (bf16[32,1024]{1,0:T(8,128)(2,1)S(1)}, bf16[32,1024]{1,0:T(8,128)(2,1)S(1)}, u32[]{:S(2)}, u32[]{:S(2)}) collective-permute-start(bf16[32,1024]{1,0:T(8,128)(2,1)S(1)} %get-tuple-element.38), channel_id=1, source_target_pairs={{0,8},{8,0},{16,24},{24,16},{1,9},{9,1},{17,25},{25,17},{2,10},{10... | collective-permute-start | bytes 196616 | tf_op jit(solution)/shard_map/ppermute | solution.py:23
  25.0 2.8 %collective-permute-start.7 = (bf16[32,1024]{1,0:T(8,128)(2,1)S(1)}, bf16[32,1024]{1,0:T(8,128)(2,1)S(1)}, u32[]{:S(2)}, u32[]{:S(2)}) collective-permute-start(bf16[32,1024]{1,0:T(8,128)(2,1)S(1)} %get-tuple-element.35), channel_id=1, source_target_pairs={{0,8},{8,0},{16,24},{24,16},{1,9},{9,1},{17,25},{25,17},{2,10},{10... | collective-permute-start | bytes 196616 | tf_op jit(solution)/shard_map/ppermute | solution.py:23
  26.3 4.5 %collective-permute-start.10 = (bf16[32,1024]{1,0:T(8,128)(2,1)S(1)}, bf16[32,1024]{1,0:T(8,128)(2,1)S(1)}, u32[]{:S(2)}, u32[]{:S(2)}) collective-permute-start(bf16[32,1024]{1,0:T(8,128)(2,1)S(1)} %add_convert_fusion.query_own), channel_id=1, source_target_pairs={{0,16},{8,24},{16,0},{24,8},{1,17},{9,25},{17,1},{25,9},{2,18},{10... | collective-permute-start | bytes 196616 | tf_op jit(solution)/shard_map/ppermute | solution.py:23
  27.9 4.3 %collective-permute-start.8 = (bf16[32,1024]{1,0:T(8,128)(2,1)S(1)}, bf16[32,1024]{1,0:T(8,128)(2,1)S(1)}, u32[]{:S(2)}, u32[]{:S(2)}) collective-permute-start(bf16[32,1024]{1,0:T(8,128)(2,1)S(1)} %add_convert_fusion.1.hidden_own), channel_id=1, source_target_pairs={{0,16},{8,24},{16,0},{24,8},{1,17},{9,25},{17,1},{25,9},{2,18},{10... | collective-permute-start | bytes 196616 | tf_op jit(solution)/shard_map/ppermute | solution.py:23
  32.3 1.4 %collective-permute-start.11 = (bf16[32,2176]{1,0:T(8,128)(2,1)S(1)}, bf16[32,2176]{1,0:T(8,128)(2,1)S(1)}, u32[]{:S(2)}, u32[]{:S(2)}) collective-permute-start(bf16[32,2176]{1,0:T(8,128)(2,1)S(1)} %activate.1.own_ref), channel_id=1, source_target_pairs={{0,8},{8,0},{16,24},{24,16},{1,9},{9,1},{17,25},{25,17},{2,10},{10... | collective-permute-start | bytes 417800 | tf_op jit(solution)/shard_map/ppermute | solution.py:23
  35.2 12.6 %all-to-all-start = ((bf16[8,8,1920]{2,1,0:T(8,128)(2,1)}), bf16[8,8,1920]{2,1,0:T(8,128)(2,1)S(1)}, u32[]{:S(2)}, u32[]{:S(2)}) async-start(bf16[8,8,1920]{2,1,0:T(8,128)(2,1)} %bitcast.4), calls=%async_computation | async-start | bytes 491520 | tf_op jit(solution)/shard_map/all_to_all | solution.py:300
  38.6 9.2 %copy-start.2 = (s32[256,8]{0,1:T(8,128)S(1)}, s32[256,8]{0,1:T(8,128)}, u32[]{:S(2)}) copy-start(s32[256,8]{0,1:T(8,128)} %param.8) | copy-start | bytes 24580
  38.7 9.2 %copy-start.3 = (bf16[256,8]{0,1:T(8,128)(2,1)S(1)}, bf16[256,8]{0,1:T(8,128)(2,1)}, u32[]{:S(2)}) copy-start(bf16[256,8]{0,1:T(8,128)(2,1)} %param.9) | copy-start | bytes 12292
